TPU v7x, 256 devices: a whole 4x4x8 slice. The times are simulated.
256 devices in a mesh: lon: 8 (over z), lat: 8 (over x, y_hi), dp: 4 (over y_lo, core).
Axes of the slice: x: 4, y: 4 (y_hi: 2, y_lo: 2; y = y_hi * 2 + y_lo), z: 8, core: 2. Of those that a mesh axis runs over, the one named last changes fastest.
Arguments:
- fields: bfloat16 [4, 256, 64, 1024], P('dp', None, 'lat', 'lon'), may hold values from -6 to 6
- weight_one: bfloat16 [9, 256, 256], replicated, may hold values from -0.125 to 0.125
- weight_two: bfloat16 [9, 256, 256], replicated, may hold values from -0.125 to 0.125
- edge_flips: int32 [7, 8], replicated, may hold values from 0 to 1, as said below
- cotangent: bfloat16 [4, 256, 64, 1024], P('dp', None, 'lat', 'lon'), may hold values from -6 to 6
Outputs:
- output: bfloat16 [4, 256, 64, 1024], P('dp', None, 'lat', 'lon')
- grad_fields: bfloat16 [4, 256, 64, 1024], P('dp', None, 'lat', 'lon')
- grad_one: float32 [9, 256, 256], replicated
- grad_two: float32 [9, 256, 256], replicated
Inputs may be any that keep to these rules, and one draw needn't show every extreme that they name: `edge_flips`: 0 on every edge inside a face; only row 8 // 2 - 1, the boundary between the band's two face rows, may hold 1, where the two faces meeting at that longitude tile store longitude in opposite orders.
All inputs are finite; a program needn't handle non-finite values.
Results may differ from a plain program's by a relative error of at most 0.0034.
Values may be sent and summed in bfloat16 or wider, within the bound.
No kernel may reach another device: no remote copies, remote signals or barrier semaphores. Data moves between devices by JAX's collectives and lax.ppermute only.
A program may use at most 128 MiB of HBM per device.

v0:
```python
import jax
import jax.numpy as jnp
from jax import lax
from jax.sharding import PartitionSpec as P


def with_halo(cells, sides, width, closed):
    for axis, dim in sides:
        count = lax.axis_size(axis)
        ends = count if closed else count - 1
        head = lax.slice_in_dim(cells, 0, width, axis=dim)
        tail = lax.slice_in_dim(cells, cells.shape[dim] - width, cells.shape[dim], axis=dim)
        cells = jnp.concatenate(
            [
                lax.ppermute(tail, axis, [(i, (i + 1) % count) for i in range(ends)]),
                cells,
                lax.ppermute(head, axis, [((i + 1) % count, i) for i in range(ends)]),
            ],
            axis=dim,
        )
    return cells


def oriented(line_cells, reverse_flag):
    return jnp.where(reverse_flag == 1, jnp.flip(line_cells, -1), line_cells)


def edge_flags(edge_flips):
    lat_index = lax.axis_index("lat")
    lon_index = lax.axis_index("lon")
    lat_count = lax.axis_size("lat")
    upper_flip = lax.dynamic_slice(edge_flips, (jnp.maximum(lat_index - 1, 0), lon_index), (1, 1))[
        0, 0
    ]
    lower_flip = lax.dynamic_slice(
        edge_flips, (jnp.minimum(lat_index, lat_count - 2), lon_index), (1, 1)
    )[0, 0]
    return (upper_flip, lower_flip, lat_index > 0, lat_index < lat_count - 1)


def padded(source, edge_info):
    upper_flip, lower_flip, has_upper, has_lower = edge_info
    extended = with_halo(source, (("lon", 3), ("lat", 2)), 1, True)
    top_rim = jnp.where(has_upper, extended[:, :, 0, :], jnp.zeros_like(extended[:, :, 0, :]))
    bottom = jnp.where(has_lower, extended[:, :, -1, :], jnp.zeros_like(extended[:, :, -1, :]))
    top_rim = oriented(top_rim, upper_flip)
    bottom = oriented(bottom, lower_flip)
    return jnp.concatenate(
        [top_rim[:, :, None, :], extended[:, :, 1:-1, :], bottom[:, :, None, :]], 2
    )


def patches_of(padded_in, tile_rows, tile_cols):
    return jnp.stack(
        [
            padded_in[:, :, tap_row : tap_row + tile_rows, tap_col : tap_col + tile_cols]
            for tap_row in range(3)
            for tap_col in range(3)
        ],
        1,
    )


def convolve(patches, weight):
    return jnp.einsum("toc,btchw->bohw", weight, patches, preferred_element_type=jnp.float32)


def transposed(grad_tile, weight, tile_rows, tile_cols):
    batch, chans = (grad_tile.shape[0], weight.shape[2])
    padded_grad = jnp.zeros((batch, chans, tile_rows + 2, tile_cols + 2), jnp.float32)
    for tap_row in range(3):
        for tap_col in range(3):
            tap_term = jnp.einsum(
                "oc,bohw->bchw",
                weight[3 * tap_row + tap_col],
                grad_tile,
                preferred_element_type=jnp.float32,
            )
            padded_grad = padded_grad.at[
                :, :, tap_row : tap_row + tile_rows, tap_col : tap_col + tile_cols
            ].add(tap_term)
    return padded_grad


def returned(padded_grad, edge_info):
    upper_flip, lower_flip, has_upper, has_lower = edge_info
    top_rim = oriented(padded_grad[:, :, 0, :], upper_flip)
    bottom = oriented(padded_grad[:, :, -1, :], lower_flip)
    rim_rows = jnp.stack([top_rim, bottom], 2)
    received = with_halo(rim_rows, (("lat", 2),), 1, False)
    interior = padded_grad[:, :, 1:-1, :]
    interior = interior.at[:, :, 0, :].add(received[:, :, 0, :])
    interior = interior.at[:, :, -1, :].add(received[:, :, -1, :])
    side_cols = jnp.stack([interior[..., 0], interior[..., -1]], -1)
    beside = with_halo(side_cols, (("lon", 3),), 1, True)
    result = interior[..., 1:-1]
    result = result.at[..., 0].add(beside[..., 0])
    result = result.at[..., -1].add(beside[..., -1])
    return result


def per_device(fields, weight_one, weight_two, edge_flips, cotangent):
    tile_rows, tile_cols = (fields.shape[2], fields.shape[3])
    edge_info = edge_flags(edge_flips)
    patch_in = patches_of(padded(fields, edge_info), tile_rows, tile_cols)
    hidden = convolve(patch_in, weight_one)
    activation = jax.nn.silu(hidden).astype(jnp.bfloat16)
    patch_act = patches_of(padded(activation, edge_info), tile_rows, tile_cols)
    output = (fields.astype(jnp.float32) + convolve(patch_act, weight_two)).astype(jnp.bfloat16)
    local_two = jnp.einsum(
        "bohw,btchw->toc", cotangent, patch_act, preferred_element_type=jnp.float32
    )
    back_act = returned(transposed(cotangent, weight_two, tile_rows, tile_cols), edge_info)
    sigmoid_h = jax.nn.sigmoid(hidden)
    back_hidden = (back_act * sigmoid_h * (1.0 + hidden * (1.0 - sigmoid_h))).astype(jnp.bfloat16)
    local_one = jnp.einsum(
        "bohw,btchw->toc", back_hidden, patch_in, preferred_element_type=jnp.float32
    )
    grad_one, grad_two = lax.psum((local_one, local_two), ("lon", "lat", "dp"))
    back_fields = returned(transposed(back_hidden, weight_one, tile_rows, tile_cols), edge_info)
    grad_fields = (cotangent.astype(jnp.float32) + back_fields).astype(jnp.bfloat16)
    return (output, grad_fields, grad_one, grad_two)


def solution(mesh):
    in_specs = (P("dp", None, "lat", "lon"), P(), P(), P(), P("dp", None, "lat", "lon"))
    out_specs = (P("dp", None, "lat", "lon"), P("dp", None, "lat", "lon"), P(), P())
    return jax.shard_map(
        per_device, mesh=mesh, in_specs=in_specs, out_specs=out_specs, check_vma=False
    )
```

profile of v0, /device:TPU:1, one launch (start us, length us, event | category | flops | bytes accessed | tf_op | source)
XLA Modules:
  0.0 452.7 jit_solution(17974031605681476931)
XLA Ops:
  11.2 4.0 collective-permute-start.1
  21.7 4.0 scatter-add.89
  25.8 3.2 add_select_fusion.1
  29.0 4.0 scatter-add.90
  35.5 2.7 scatter-add.94
  39.5 2.7 scatter-add.95
  44.8 2.7 scatter-add.99
  48.7 2.7 scatter-add.100
  54.8 5.2 %collective-permute-start.3 = (bf16[1,256,1,130]{1,3,2,0:T(8,128)(2,1)S(1)}, bf16[1,256,1,130]{1,3,2,0:T(8,128)(2,1)S(1)}, u32[]{:S(2)}, u32[]{:S(2)}) collective-permute-start(bf16[1,256,1,130]{1,3,2,0:T(8,128)(2,1)S(1)} %get-tuple-element.342), channel_id=1, source_target_pairs={{4,0},{8,4},{12,8},{16,12},{20,16},{24,20},{28,24},{0,28},{5,1},{9... | collective-permute-start | bytes 199688 | tf_op jit(solution)/shard_map/ppermute | solution.py:17
  61.4 5.5 %collective-permute-start.8 = (f32[1,256,1,130]{1,3,2,0:T(8,128)S(1)}, f32[1,256,1,130]{1,3,2,0:T(8,128)S(1)}, u32[]{:S(2)}, u32[]{:S(2)}) collective-permute-start(f32[1,256,1,130]{1,3,2,0:T(8,128)S(1)} %get-tuple-element.327), channel_id=1, source_target_pairs={{0,4},{4,8},{8,12},{12,16},{16,20},{20,24},{24,28},{1,5},{5,9},{9,... | collective-permute-start | bytes 399368 | tf_op jit(solution)/shard_map/ppermute | solution.py:15
  68.4 6.4 %collective-permute-done.2 = bf16[1,256,1,130]{1,3,2,0:T(8,128)(2,1)S(1)} collective-permute-done((bf16[1,256,1,130]{1,3,2,0:T(8,128)(2,1)S(1)}, bf16[1,256,1,130]{1,3,2,0:T(8,128)(2,1)S(1)}, u32[]{:S(2)}, u32[]{:S(2)}) %collective-permute-start.2) | collective-permute-done | bytes 66592 | tf_op jit(solution)/shard_map/ppermute | solution.py:15
  80.7 2.7 collective-permute-start.11
  87.2 4.4 multiply_convert_fusion
  91.6 2.9 fusion.8
  94.8 2.6 fusion.29
  97.6 2.7 collective-permute-start.5
  100.3 7.2 %scatter-add.110 = f32[1,256,10,130]{1,3,2,0:T(8,128)S(1)} dynamic-update-slice(f32[1,256,10,130]{1,3,2,0:T(8,128)S(1)} %scatter-add.109, f32[1,256,8,128]{1,3,2,0:T(8,128)} %fusion.29, s32[]{:T(128)} %constant.657.clone.1, s32[]{:T(128)} %constant.657.clone.1, s32[]{:T(128)} %bitcast.51, s32[]{:T(128)} %bitcast.52) | dynamic-update-slice | bytes 2097156 | tf_op jit(solution)/shard_map/scatter-add | solution.py:81
  107.5 4.1 add_select_fusion
  111.6 7.2 %scatter-add.111 = f32[1,256,10,130]{1,3,2,0:T(8,128)S(1)} dynamic-update-slice(f32[1,256,10,130]{1,3,2,0:T(8,128)S(1)} %scatter-add.110, f32[1,256,8,128]{1,3,2,0:T(8,128)} %add_select_fusion, s32[]{:T(128)} %constant.657.clone.1, s32[]{:T(128)} %constant.657.clone.1, s32[]{:T(128)} %bitcast.57, s32[]{:T(128)} %bitcast.58) | dynamic-update-slice | bytes 2097156 | tf_op jit(solution)/shard_map/scatter-add | solution.py:81
  122.2 5.9 %scatter-add.115 = f32[1,256,10,130]{1,3,2,0:T(8,128)S(1)} dynamic-update-slice(f32[1,256,10,130]{1,3,2,0:T(8,128)S(1)} %fusion.31, f32[1,256,8,128]{1,3,2,0:T(8,128)} %fusion.32, s32[]{:T(128)} %constant.657.clone.1, s32[]{:T(128)} %constant.657.clone.1, s32[]{:T(128)} %constant.670.clone.1, s32[]{:T(128)} %constant.670.clone.1) | dynamic-update-slice | bytes 2097156 | tf_op jit(solution)/shard_map/scatter-add | solution.py:81
  130.2 5.9 %scatter-add.116 = f32[1,256,10,130]{1,3,2,0:T(8,128)S(1)} dynamic-update-slice(f32[1,256,10,130]{1,3,2,0:T(8,128)S(1)} %scatter-add.115, f32[1,256,8,128]{1,3,2,0:T(8,128)} %fusion.33, s32[]{:T(128)} %constant.657.clone.1, s32[]{:T(128)} %constant.657.clone.1, s32[]{:T(128)} %constant.670.clone.1, s32[]{:T(128)} %constant.667.clone.1) | dynamic-update-slice | bytes 2097156 | tf_op jit(solution)/shard_map/scatter-add | solution.py:81
  139.5 5.9 %scatter-add.120 = f32[1,256,10,130]{1,3,2,0:T(8,128)S(1)} dynamic-update-slice(f32[1,256,10,130]{1,3,2,0:T(8,128)S(1)} %fusion.35, f32[1,256,8,128]{1,3,2,0:T(8,128)} %fusion.36, s32[]{:T(128)} %constant.657.clone.1, s32[]{:T(128)} %constant.657.clone.1, s32[]{:T(128)} %constant.667.clone.1, s32[]{:T(128)} %constant.670.clone.1) | dynamic-update-slice | bytes 2097156 | tf_op jit(solution)/shard_map/scatter-add | solution.py:81
  148.3 5.9 %scatter-add.121 = f32[1,256,10,130]{1,3,2,0:T(8,128)S(1)} dynamic-update-slice(f32[1,256,10,130]{1,3,2,0:T(8,128)S(1)} %scatter-add.120, f32[1,256,8,128]{1,3,2,0:T(8,128)} %fusion.37, s32[]{:T(128)} %constant.657.clone.1, s32[]{:T(128)} %constant.657.clone.1, s32[]{:T(128)} %constant.667.clone.1, s32[]{:T(128)} %constant.667.clone.1) | dynamic-update-slice | bytes 2097156 | tf_op jit(solution)/shard_map/scatter-add | solution.py:81
  154.1 3.0 collective-permute-start.6
  158.4 2.6 collective-permute-done.6
  165.6 2.9 fusion.11
  169.2 3.0 collective-permute-start.12
  174.1 6.0 %collective-permute-done.13 = f32[1,256,1,130]{1,3,2,0:T(8,128)S(1)} collective-permute-done((f32[1,256,1,130]{1,3,2,0:T(8,128)S(1)}, f32[1,256,1,130]{1,3,2,0:T(8,128)S(1)}, u32[]{:S(2)}, u32[]{:S(2)}) %collective-permute-start.13) | collective-permute-done | bytes 133152 | tf_op jit(solution)/shard_map/ppermute | solution.py:17
  181.2 3.8 fusion.41
  186.2 2.7 collective-permute-start.15
  191.0 249.7 %all-reduce.5.cloned.1.call-done = (f32[9,256,256]{1,2,0:T(8,128)}, f32[9,256,256]{1,2,0:T(8,128)}) async-done(((f32[9,256,256]{1,2,0:T(8,128)}, f32[9,256,256]{1,2,0:T(8,128)}), (f32[9,256,256]{1,2,0:T(8,128)}, f32[9,256,256]{1,2,0:T(8,128)})) %all-reduce.5.cloned.1.call-update) | async-done | bytes 4718608 | tf_op jit(solution)/shard_map/psum | solution.py:119
  440.7 3.2 copy.38
  (136 shorter events, 59.3 us)
Async XLA Ops:
  7.2 10.7 %copy-start = (bf16[1,256,8,128]{3,2,1,0:T(8,128)(2,1)S(1)}, bf16[1,256,8,128]{3,2,1,0:T(8,128)(2,1)}, u32[]{:S(2)}) copy-start(bf16[1,256,8,128]{3,2,1,0:T(8,128)(2,1)} %param.61) | copy-start | bytes 1572868
  7.2 433.6 %all-reduce.5.cloned.1.call-start = ((), (), s32[]{:S(2)}) async-start(), calls=%async_computation | async-start | bytes 9437184 | tf_op jit(solution)/shard_map/psum | solution.py:119
  8.6 46.2 %collective-permute-start = (bf16[1,256,8,1]{1,3,2,0:T(2,128)(2,1)S(1)}, bf16[1,256,8,1]{1,3,2,0:T(2,128)(2,1)S(1)}, u32[]{:S(2)}, u32[]{:S(2)}) collective-permute-start(bf16[1,256,8,1]{1,3,2,0:T(2,128)(2,1)S(1)} %get-tuple-element.346), channel_id=1, source_target_pairs={{0,32},{32,64},{64,96},{96,128},{128,160},{160,192},{192,224},{224... | collective-permute-start | bytes 12296 | tf_op jit(solution)/shard_map/ppermute | solution.py:15
  11.2 43.6 %collective-permute-start.1 = (bf16[1,256,8,1]{1,3,2,0:T(2,128)(2,1)S(1)}, bf16[1,256,8,1]{1,3,2,0:T(2,128)(2,1)S(1)}, u32[]{:S(2)}, u32[]{:S(2)}) collective-permute-start(bf16[1,256,8,1]{1,3,2,0:T(2,128)(2,1)S(1)} %get-tuple-element.347), channel_id=1, source_target_pairs={{32,0},{64,32},{96,64},{128,96},{160,128},{192,160},{224,192},{0,2... | collective-permute-start | bytes 12296 | tf_op jit(solution)/shard_map/ppermute | solution.py:17
  54.8 13.1 %collective-permute-start.3 = (bf16[1,256,1,130]{1,3,2,0:T(8,128)(2,1)S(1)}, bf16[1,256,1,130]{1,3,2,0:T(8,128)(2,1)S(1)}, u32[]{:S(2)}, u32[]{:S(2)}) collective-permute-start(bf16[1,256,1,130]{1,3,2,0:T(8,128)(2,1)S(1)} %get-tuple-element.342), channel_id=1, source_target_pairs={{4,0},{8,4},{12,8},{16,12},{20,16},{24,20},{28,24},{0,28},{5,1},{9... | collective-permute-start | bytes 199688 | tf_op jit(solution)/shard_map/ppermute | solution.py:17
  60.1 17.0 %collective-permute-start.9 = (f32[1,256,1,130]{1,3,2,0:T(8,128)S(1)}, f32[1,256,1,130]{1,3,2,0:T(8,128)S(1)}, u32[]{:S(2)}, u32[]{:S(2)}) collective-permute-start(f32[1,256,1,130]{1,3,2,0:T(8,128)S(1)} %get-tuple-element.326), channel_id=1, source_target_pairs={{4,0},{8,4},{12,8},{16,12},{20,16},{24,20},{28,24},{5,1},{9,5},{13... | collective-permute-start | bytes 399368 | tf_op jit(solution)/shard_map/ppermute | solution.py:17
  61.4 14.8 %collective-permute-start.8 = (f32[1,256,1,130]{1,3,2,0:T(8,128)S(1)}, f32[1,256,1,130]{1,3,2,0:T(8,128)S(1)}, u32[]{:S(2)}, u32[]{:S(2)}) collective-permute-start(f32[1,256,1,130]{1,3,2,0:T(8,128)S(1)} %get-tuple-element.327), channel_id=1, source_target_pairs={{0,4},{4,8},{8,12},{12,16},{16,20},{20,24},{24,28},{1,5},{5,9},{9,... | collective-permute-start | bytes 399368 | tf_op jit(solution)/shard_map/ppermute | solution.py:15
  68.0 6.8 %collective-permute-start.2 = (bf16[1,256,1,130]{1,3,2,0:T(8,128)(2,1)S(1)}, bf16[1,256,1,130]{1,3,2,0:T(8,128)(2,1)S(1)}, u32[]{:S(2)}, u32[]{:S(2)}) collective-permute-start(bf16[1,256,1,130]{1,3,2,0:T(8,128)(2,1)S(1)} %get-tuple-element.343), channel_id=1, source_target_pairs={{0,4},{4,8},{8,12},{12,16},{16,20},{20,24},{24,28},{28,0},{1,5},{5... | collective-permute-start | bytes 199688 | tf_op jit(solution)/shard_map/ppermute | solution.py:15
  75.9 1.3 copy-start.1
  77.2 10.0 %copy-start.5 = (bf16[9,256,256]{2,1,0:T(8,128)(2,1)S(1)}, bf16[9,256,256]{2,1,0:T(8,128)(2,1)}, u32[]{:S(2)}) copy-start(bf16[9,256,256]{2,1,0:T(8,128)(2,1)} %param.58) | copy-start | bytes 3538948
  77.2 6.1 %collective-permute-start.10 = (f32[1,256,8,1]{1,3,2,0:T(1,128)S(1)}, f32[1,256,8,1]{1,3,2,0:T(1,128)S(1)}, u32[]{:S(2)}, u32[]{:S(2)}) collective-permute-start(f32[1,256,8,1]{1,3,2,0:T(1,128)S(1)} %get-tuple-element.333), channel_id=1, source_target_pairs={{0,32},{32,64},{64,96},{96,128},{128,160},{160,192},{192,224},{224... | collective-permute-start | bytes 24584 | tf_op jit(solution)/shard_map/ppermute | solution.py:15
  77.4 2.1 copy-start.8
  80.7 4.2 collective-permute-start.11
  87.2 4.4 copy-start.9
  97.5 47.9 %collective-permute-start.4 = (bf16[1,256,8,1]{1,3,2,0:T(2,128)(2,1)S(1)}, bf16[1,256,8,1]{1,3,2,0:T(2,128)(2,1)S(1)}, u32[]{:S(2)}, u32[]{:S(2)}) collective-permute-start(bf16[1,256,8,1]{1,3,2,0:T(2,128)(2,1)S(1)} %get-tuple-element.344), channel_id=1, source_target_pairs={{0,32},{32,64},{64,96},{96,128},{128,160},{160,192},{192,224},{224... | collective-permute-start | bytes 12296 | tf_op jit(solution)/shard_map/ppermute | solution.py:15
  97.6 47.8 %collective-permute-start.5 = (bf16[1,256,8,1]{1,3,2,0:T(2,128)(2,1)S(1)}, bf16[1,256,8,1]{1,3,2,0:T(2,128)(2,1)S(1)}, u32[]{:S(2)}, u32[]{:S(2)}) collective-permute-start(bf16[1,256,8,1]{1,3,2,0:T(2,128)(2,1)S(1)} %get-tuple-element.345), channel_id=1, source_target_pairs={{32,0},{64,32},{96,64},{128,96},{160,128},{192,160},{224,192},{0,2... | collective-permute-start | bytes 12296 | tf_op jit(solution)/shard_map/ppermute | solution.py:17
  146.1 11.1 %collective-permute-start.7 = (bf16[1,256,1,130]{1,3,2,0:T(8,128)(2,1)}, bf16[1,256,1,130]{1,3,2,0:T(8,128)(2,1)}, u32[]{:S(2)}, u32[]{:S(2)}) collective-permute-start(bf16[1,256,1,130]{1,3,2,0:T(8,128)(2,1)} %get-tuple-element.338), channel_id=1, source_target_pairs={{4,0},{8,4},{12,8},{16,12},{20,16},{24,20},{28,24},{0,28},{5,1},{9... | collective-permute-start | bytes 199688 | tf_op jit(solution)/shard_map/ppermute | solution.py:17
  148.3 5.9 %copy-start.7 = (bf16[1,256,1,130]{1,3,2,0:T(8,128)(2,1)S(1)}, bf16[1,256,1,130]{1,3,2,0:T(8,128)(2,1)}, u32[]{:S(2)}) copy-start(bf16[1,256,1,130]{1,3,2,0:T(8,128)(2,1)} %get-tuple-element.339) | copy-start | bytes 199684
  154.1 6.9 %collective-permute-start.6 = (bf16[1,256,1,130]{1,3,2,0:T(8,128)(2,1)S(1)}, bf16[1,256,1,130]{1,3,2,0:T(8,128)(2,1)S(1)}, u32[]{:S(2)}, u32[]{:S(2)}) collective-permute-start(bf16[1,256,1,130]{1,3,2,0:T(8,128)(2,1)S(1)} %copy-done.7), channel_id=1, source_target_pairs={{0,4},{4,8},{8,12},{12,16},{16,20},{20,24},{24,28},{28,0},{1,5},{5... | collective-permute-start | bytes 199688 | tf_op jit(solution)/shard_map/ppermute | solution.py:15
  163.4 2.1 copy-start.10
  169.2 4.9 %collective-permute-start.12 = (f32[1,256,1,130]{1,3,2,0:T(8,128)S(1)}, f32[1,256,1,130]{1,3,2,0:T(8,128)S(1)}, u32[]{:S(2)}, u32[]{:S(2)}) collective-permute-start(f32[1,256,1,130]{1,3,2,0:T(8,128)S(1)} %get-tuple-element.323), channel_id=1, source_target_pairs={{0,4},{4,8},{8,12},{12,16},{16,20},{20,24},{24,28},{1,5},{5,9},{9,... | collective-permute-start | bytes 399368 | tf_op jit(solution)/shard_map/ppermute | solution.py:15
  172.5 8.7 %copy-start.6 = (bf16[9,256,256]{2,1,0:T(8,128)(2,1)S(1)}, bf16[9,256,256]{2,1,0:T(8,128)(2,1)}, u32[]{:S(2)}) copy-start(bf16[9,256,256]{2,1,0:T(8,128)(2,1)} %param.59) | copy-start | bytes 3538948
  172.6 7.4 %collective-permute-start.13 = (f32[1,256,1,130]{1,3,2,0:T(8,128)S(1)}, f32[1,256,1,130]{1,3,2,0:T(8,128)S(1)}, u32[]{:S(2)}, u32[]{:S(2)}) collective-permute-start(f32[1,256,1,130]{1,3,2,0:T(8,128)S(1)} %get-tuple-element.322), channel_id=1, source_target_pairs={{4,0},{8,4},{12,8},{16,12},{20,16},{24,20},{28,24},{5,1},{9,5},{13... | collective-permute-start | bytes 399368 | tf_op jit(solution)/shard_map/ppermute | solution.py:17
  180.1 1.0 copy-start.2
  181.1 7.9 %collective-permute-start.14 = (f32[1,256,8,1]{1,3,2,0:T(1,128)S(1)}, f32[1,256,8,1]{1,3,2,0:T(1,128)S(1)}, u32[]{:S(2)}, u32[]{:S(2)}) collective-permute-start(f32[1,256,8,1]{1,3,2,0:T(1,128)S(1)} %get-tuple-element.331), channel_id=1, source_target_pairs={{0,32},{32,64},{64,96},{96,128},{128,160},{160,192},{192,224},{224... | collective-permute-start | bytes 24584 | tf_op jit(solution)/shard_map/ppermute | solution.py:15
  181.2 4.9 %copy-start.3 = (f32[1,256,8,130]{1,3,2,0:T(8,128)S(1)}, f32[1,256,8,130]{1,3,2,0:T(8,128)}, u32[]{:S(2)}) copy-start(f32[1,256,8,130]{1,3,2,0:T(8,128)} %copy-done.2) | copy-start | bytes 3194884
  186.2 3.5 collective-permute-start.15
  440.7 3.2 copy-start.4
Sparse Core Ops, SparseCore 0:
  168.6 272.1 all-reduce.4
where the time goes:
time: 455 us; the launch traced here: 453 us
  waiting for transfers between devices  265 us (58%)
  local copies, waits for them, and re-layouts  84.1 us (18%)
  matrix products  46.6 us (10%)
  starting transfers between devices  34.4 us (8%)
  between operations  16.1 us (4%)
  other arithmetic  6.15 us (1%)
    psum x1, waiting for transfers between devices, per_device(): grad_one, grad_two = lax.psum((local_one, local_two), ('lon', 'lat', 'dp'))  250 us
    scatter-add x14, local copies, waits for them, and re-layouts, transposed(): padded_grad = padded_grad.at[:, :, tap_row:tap_row + tile_rows, tap_col:t...  57 us
    dot_general x18, matrix products, transposed(): jnp.einsum('oc,bohw->bchw', weight[3 * tap_row + tap_col], grad_tile, pre...  32.6 us
    ppermute x8, starting transfers between devices, with_halo(): lax.ppermute(head, axis, [((i + 1) % count, i) for i in range(ends)])  20 us
    unnamed x40, local copies, waits for them, and re-layouts  16.1 us
    ppermute x8, starting transfers between devices, with_halo(): lax.ppermute(tail, axis, [(i, (i + 1) % count) for i in range(ends)])  14.3 us
  transfers between devices with their start and end apart: 17, of which 5 were waited for; matrix products, arithmetic and copies ran while one was open for 23% of the time, Pallas kernels for 0%

commit v1 on v0

v1 whole, which is shorter than its diff:
```python
import jax
import jax.numpy as jnp
from jax import lax
from jax.experimental import pallas as pl
from jax.experimental.pallas import tpu as pltpu
from jax.sharding import PartitionSpec as P

F32 = jnp.float32
BF16 = jnp.bfloat16
LANES = 128
ROWS = 8
CELLS = ROWS * LANES
PADDED = CELLS + 2 * LANES
NT = (((1,), (1,)), ((), ()))
TN = (((0,), (0,)), ((), ()))


def iota(shape, dim):
    return lax.broadcasted_iota(jnp.int32, shape, dim)


def one_hot(cond):
    return jnp.where(cond, 1.0, 0.0).astype(BF16)


def dot(a, b):
    return jnp.dot(a, b, preferred_element_type=F32)


def rims(first, second, flags, outs):
    east, west, south, north, se, sw, ne, nw = outs
    shape = (2 * ROWS, CELLS)
    row, cell = (iota(shape, 0), iota(shape, 1))
    pick = one_hot(cell == jnp.where(row < ROWS, row * LANES + LANES - 1, (row - ROWS) * LANES))
    one = lax.dot_general(pick, first, NT, preferred_element_type=F32)
    two = lax.dot_general(pick, second, NT, preferred_element_type=F32)
    east[...] = jnp.concatenate([one[:ROWS], two[:ROWS]], 0).astype(BF16)
    west[...] = jnp.concatenate([one[ROWS:], two[ROWS:]], 0).astype(BF16)
    chans = first.shape[0]
    south[:chans] = first[:, CELLS - LANES :]
    south[chans:] = second[:, CELLS - LANES :]
    north[:chans] = first[:, :LANES]
    north[chans:] = second[:, :LANES]
    upper, lower = (flags[0] == 1, flags[1] == 1)
    top, last = (0, ROWS - 1)

    def corner(out, mine, other, flip):
        pair = jnp.where(flip, two[other : other + 1], two[mine : mine + 1])
        head = jnp.broadcast_to(one[mine : mine + 1], (ROWS, chans))
        tail = jnp.broadcast_to(pair, (ROWS, chans))
        out[...] = jnp.where(iota((ROWS, chans), 0) == 0, head, tail).astype(BF16)

    corner(se, last, last + ROWS, lower)
    corner(sw, last + ROWS, last, lower)
    corner(ne, top, top + ROWS, upper)
    corner(nw, top + ROWS, top, upper)


def turned(line, flip):
    shape = (LANES, LANES)
    a, b = (iota(shape, 0), iota(shape, 1))
    turn = one_hot(b == a + flip * (LANES - 1 - 2 * a))
    return dot(line, turn)


def shifted(out, centre, top, bottom, west, east, swap_top=None, swap_bottom=None):
    chans = centre.shape[0]
    k, lane = (iota((16, PADDED), 0), iota((16, PADDED), 1))
    placed_west = lax.dot_general(
        west, one_hot(lane == k * LANES), TN, preferred_element_type=F32
    )
    placed_east = lax.dot_general(
        east, one_hot(lane == k * LANES + LANES - 1), TN, preferred_element_type=F32
    )
    lane_in = iota((chans, LANES), 1)
    for block in range(ROWS + 2):
        span = slice(block * LANES, (block + 1) * LANES)
        if block == 0:
            line = top
        elif block == ROWS + 1:
            line = bottom
        else:
            line = centre[:, (block - 1) * LANES : block * LANES].astype(F32)
        left = jnp.where(lane_in == 0, placed_west[:, span], pltpu.roll(line, 1, 1))
        right = jnp.where(lane_in == LANES - 1, placed_east[:, span], pltpu.roll(line, LANES - 1, 1))
        swap = swap_top if block == 0 else swap_bottom if block == ROWS + 1 else None
        if swap is not None:
            left, right = (jnp.where(swap, right, left), jnp.where(swap, left, right))
        out[0, :, span] = left.astype(BF16)
        out[1, :, span] = line.astype(BF16)
        out[2, :, span] = right.astype(BF16)


def lines(top, mid, bottom):
    return jnp.concatenate([top, mid, bottom, jnp.zeros((6, mid.shape[1]), F32)], 0).astype(BF16)


def pad_forward(out, centre, flags, halo):
    from_w, from_e, from_n, from_s, c_nw, c_ne, c_sw, c_se = halo
    chans = centre.shape[0]
    upper, lower = (flags[0] == 1, flags[1] == 1)
    get = lambda ref: ref[...].astype(F32)[:1]
    nw, ne, sw, se = (get(c_nw), get(c_ne), get(c_sw), get(c_se))
    west = lines(jnp.where(upper, ne, nw), from_w[...].astype(F32)[:ROWS], jnp.where(lower, se, sw))
    east = lines(jnp.where(upper, nw, ne), from_e[...].astype(F32)[:ROWS], jnp.where(lower, sw, se))
    top = turned(from_n[:chans], flags[0])
    bottom = turned(from_s[:chans], flags[1])
    shifted(out, centre, top, bottom, west, east)


def pad_backward(out, centre, flags, halo):
    from_w, from_e, from_n, from_s = halo[:4]
    chans = centre.shape[0]
    upper, lower = (flags[0] == 1, flags[1] == 1)
    none = jnp.zeros((1, chans), F32)
    west = lines(none, from_w[...].astype(F32)[ROWS:], none)
    east = lines(none, from_e[...].astype(F32)[ROWS:], none)
    top = turned(from_n[chans:], flags[0])
    bottom = turned(from_s[chans:], flags[1])
    shifted(out, centre, top, bottom, west, east, upper, lower)


def conv(weight, pads):
    total = None
    for tap in range(9):
        r, s = divmod(tap, 3)
        term = dot(weight[tap], pads[s, :, r * LANES : r * LANES + CELLS])
        total = term if total is None else total + term
    return total


def conv_adjoint(weight, pads, flags, halo):
    total = None
    for tap in range(9):
        r, s = divmod(tap, 3)
        start = (2 - r) * LANES
        term = lax.dot_general(
            weight[tap], pads[2 - s, :, start : start + CELLS], TN, preferred_element_type=F32
        )
        total = term if total is None else total + term
    c_nw, c_ne, c_sw, c_se = halo[4:]
    chans = total.shape[0]
    k, lane = (iota((ROWS, LANES), 0), iota((ROWS, LANES), 1))

    def corner(ref, at, tap):
        spread = lax.dot_general(
            ref[...], one_hot((k == 1) & (lane == at)), TN, preferred_element_type=F32
        ).astype(BF16)
        return lax.dot_general(weight[tap], spread, TN, preferred_element_type=F32)

    top = corner(c_nw, 0, 8 - 2 * flags[2]) + corner(c_ne, LANES - 1, 6 + 2 * flags[3])
    bottom = corner(c_sw, 0, 2 - 2 * flags[4]) + corner(c_se, LANES - 1, 2 * flags[5])
    return jnp.concatenate(
        [total[:, :LANES] + top, total[:, LANES : CELLS - LANES], total[:, CELLS - LANES :] + bottom],
        1,
    )


def prepare_kernel(flags, first, second, *outs):
    rims(first[...], second[...], flags, outs)


def hidden_kernel(flags, field, cotangent, one, two, *refs):
    halo, outs, back_pads = (refs[:8], refs[8:-1], refs[-1])
    act_out, back_out, pads = outs[:3]
    pad_forward(pads, field[...], flags, halo)
    pad_backward(back_pads, cotangent[...], flags, halo)
    hidden = conv(one, pads)
    back_act = conv_adjoint(two, back_pads, flags, halo)
    sigma = 1.0 / (1.0 + jnp.exp(-hidden))
    act_out[...] = (hidden * sigma).astype(BF16)
    back_out[...] = (back_act * sigma * (1.0 + hidden * (1.0 - sigma))).astype(BF16)
    rims(act_out[...], back_out[...], flags, outs[3:])


def grad_kernel(grad_tile, pads, out):
    for tap in range(9):
        r, s = divmod(tap, 3)
        out[tap] = lax.dot_general(
            grad_tile[...], pads[s, :, r * LANES : r * LANES + CELLS], NT, preferred_element_type=F32
        )


def grad_two_kernel(flags, act, cotangent, *refs):
    halo, pads, out = (refs[:8], refs[8], refs[9])
    pad_forward(pads, act[...], flags, halo)
    grad_kernel(cotangent, pads, out)


def result_kernel(flags, field, cotangent, back, one, two, pads, *refs):
    halo, (output, grad_fields, back_pads) = (refs[:8], refs[8:])
    output[...] = (field[...].astype(F32) + conv(two, pads)).astype(BF16)
    pad_backward(back_pads, back[...], flags, halo)
    grad_fields[...] = (
        cotangent[...].astype(F32) + conv_adjoint(one, back_pads, flags, halo)
    ).astype(BF16)


SMEM = pl.BlockSpec(memory_space=pltpu.SMEM)
VMEM = pl.BlockSpec(memory_space=pltpu.VMEM)


def call(kernel, name, out_shape, args, scratch=(), flags=True):
    return pl.pallas_call(
        kernel,
        name=name,
        out_shape=out_shape,
        in_specs=([SMEM] if flags else []) + [VMEM] * (len(args) - (1 if flags else 0)),
        out_specs=jax.tree.map(lambda _: VMEM, out_shape),
        scratch_shapes=list(scratch),
        compiler_params=pltpu.CompilerParams(vmem_limit_bytes=56 * 1024 * 1024),
    )(*args)


def struct(*shape, dtype=BF16):
    return jax.ShapeDtypeStruct(shape, dtype)


def rim_shapes(chans):
    side = struct(2 * ROWS, chans)
    line = struct(2 * chans, LANES)
    corner = struct(ROWS, chans)
    return (side, side, line, line, corner, corner, corner, corner)


def exchange(rim):
    east, west, south, north, se, sw, ne, nw = rim
    lons, lats = (lax.axis_size("lon"), lax.axis_size("lat"))

    def along(value, step):
        return lax.ppermute(value, "lon", [(i, (i + step) % lons) for i in range(lons)])

    def across(value, step):
        return lax.ppermute(
            value, "lat", [(i, i + step) for i in range(lats) if 0 <= i + step < lats]
        )

    def diagonal(value, down, right):
        pairs = [
            (o * lats + a, ((o + right) % lons) * lats + a + down)
            for o in range(lons)
            for a in range(lats)
            if 0 <= a + down < lats
        ]
        return lax.ppermute(value, ("lon", "lat"), pairs)

    from_n, from_s = (across(south, 1), across(north, -1))
    c_nw, c_ne = (diagonal(se, 1, 1), diagonal(sw, 1, -1))
    c_sw, c_se = (diagonal(ne, -1, 1), diagonal(nw, -1, -1))
    from_w, from_e = (along(east, 1), along(west, -1))
    return (from_w, from_e, from_n, from_s, c_nw, c_ne, c_sw, c_se)


def edge_flags(edge_flips):
    a, o = (lax.axis_index("lat"), lax.axis_index("lon"))
    lats, lons = (lax.axis_size("lat"), lax.axis_size("lon"))
    rows = lax.dynamic_slice(
        jnp.concatenate([jnp.zeros((1, lons), jnp.int32), edge_flips, jnp.zeros((1, lons), jnp.int32)]),
        (a, 0),
        (2, lons),
    )
    wide = jnp.concatenate([rows[:, -1:], rows, rows[:, :1]], 1)
    near = lax.dynamic_slice(wide, (0, o), (2, 3))
    return jnp.stack(
        [near[0, 1], near[1, 1], near[0, 0], near[0, 2], near[1, 0], near[1, 2]]
    )


def sum_over(value, axis, dtype):
    count = lax.axis_size(axis)
    parts = value.reshape(count, value.shape[0] // count, value.shape[1]).astype(dtype)
    return jnp.sum(lax.all_to_all(parts, axis, 0, 0).astype(F32), 0)


def spread_over(value, axis):
    count = lax.axis_size(axis)
    same = jnp.broadcast_to(value[None], (count,) + value.shape)
    got = lax.all_to_all(same, axis, 0, 0)
    return got.reshape(count * value.shape[0], value.shape[1])


def reduce_grads(one, two):
    chans = one.shape[-1]
    one, two = (one.reshape(-1, chans), two.reshape(-1, chans))
    place = lax.axis_index("dp")
    core, side = (place % 2, place // 2)
    got_one = lax.ppermute(one.astype(BF16), "dp", [(1, 0), (3, 2)])
    got_two = lax.ppermute(two.astype(BF16), "dp", [(0, 1), (2, 3)])
    mine = jnp.where(core == 0, one + got_one.astype(F32), two + got_two.astype(F32))
    half = mine.shape[0] // 2
    away = lax.dynamic_slice_in_dim(mine, (1 - side) * half, half, 0).astype(BF16)
    kept = lax.dynamic_slice_in_dim(mine, side * half, half, 0)
    got = lax.ppermute(away, "dp", [(i, (i + 2) % 4) for i in range(4)])
    part = sum_over(kept + got.astype(F32), "lat", BF16)
    part = sum_over(part, "lon", F32).astype(BF16)
    part = spread_over(spread_over(part, "lon"), "lat")
    other = lax.ppermute(part, "dp", [(i, (i + 2) % 4) for i in range(4)])
    full = jnp.where(
        side == 0, jnp.concatenate([part, other], 0), jnp.concatenate([other, part], 0)
    )
    pair = lax.ppermute(full, "dp", [(0, 1), (1, 0), (2, 3), (3, 2)])
    out_one = jnp.where(core == 0, full, pair).astype(F32)
    out_two = jnp.where(core == 0, pair, full).astype(F32)
    return (out_one.reshape(9, chans, chans), out_two.reshape(9, chans, chans))


def per_device(fields, weight_one, weight_two, edge_flips, cotangent):
    chans = fields.shape[1]
    flat = (chans, CELLS)
    field, cot = (fields.reshape(flat), cotangent.reshape(flat))
    flags = edge_flags(edge_flips)
    pads = struct(3, chans, PADDED)
    scratch = [pltpu.VMEM((3, chans, PADDED), BF16)]
    rim = call(prepare_kernel, "prepare", rim_shapes(chans), (flags, field, cot))
    halo = exchange(rim)
    act, back, pads_in, *rim = call(
        hidden_kernel,
        "hidden",
        (struct(*flat), struct(*flat), pads) + rim_shapes(chans),
        (flags, field, cot, weight_one, weight_two) + halo,
        scratch,
    )
    halo = exchange(rim)
    local = struct(9, chans, chans, dtype=F32)
    local_one = call(grad_kernel, "grad_one", local, (back, pads_in), flags=False)
    pads_act, local_two = call(grad_two_kernel, "grad_two", (pads, local), (flags, act, cot) + halo)
    grad_one, grad_two = reduce_grads(local_one, local_two)
    output, grad_fields = call(
        result_kernel,
        "result",
        (struct(*flat), struct(*flat)),
        (flags, field, cot, back, weight_one, weight_two, pads_act) + halo,
        scratch,
    )
    return (output.reshape(fields.shape), grad_fields.reshape(fields.shape), grad_one, grad_two)


def solution(mesh):
    in_specs = (P("dp", None, "lat", "lon"), P(), P(), P(), P("dp", None, "lat", "lon"))
    out_specs = (P("dp", None, "lat", "lon"), P("dp", None, "lat", "lon"), P(), P())
    return jax.shard_map(
        per_device, mesh=mesh, in_specs=in_specs, out_specs=out_specs, check_vma=False
    )
```

time: 455 us -> 219 us (0.48)
  waiting for transfers between devices: 265 us -> 37.9 us
  local copies, waits for them, and re-layouts: 84.1 us -> 14 us
  blocking collectives: 0 us -> 57.8 us
  matrix products: 46.6 us -> 0 us
  starting transfers between devices: 34.4 us -> 66.5 us
  Pallas kernels: 0 us -> 26.2 us
  between operations: 16.1 us -> 1.11 us
  other arithmetic: 6.15 us -> 14.2 us
    psum x1 -> x0, waiting for transfers between devices: 250 us -> none  [per_device(): grad_one, grad_two = lax.psum((local_one, local_two), ('lon', 'lat', 'dp'))]
    scatter-add x18 -> x0, local copies, waits for them, and re-layouts: 60.1 us -> none  [the longest x14 57 us: transposed(): padded_grad = padded_grad.at[:, :, tap_row:tap_row + tile_rows, tap_col:t...]
    all_to_all x0 -> x4, blocking collectives: none -> 57.8 us  [the longest x2 35.8 us: sum_over(): return jnp.sum(lax.all_to_all(parts, axis, 0, 0).astype(F32), 0)]
    dot_general x22 -> x0, matrix products: 46.6 us -> none  [the longest x18 32.6 us: transposed(): jnp.einsum('oc,bohw->bchw', weight[3 * tap_row + tap_col], grad_tile, pre...]
    ppermute x16 -> x21, starting transfers between devices: 34.4 us -> 66.5 us  [the longest x8 28.3 us: diagonal(): return lax.ppermute(value, ('lon', 'lat'), pairs)]
    pallas_call x0 -> x5, Pallas kernels: none -> 26.2 us  [call(): pl.pallas_call(kernel, name=name, out_shape=out_shape, in_specs=([SMEM] i...]
    ppermute x16 -> x21, waiting for transfers between devices: 15.7 us -> 37.9 us  [the longest x1 13.5 us: reduce_grads(): got = lax.ppermute(away, 'dp', [(i, (i + 2) % 4) for i in range(4)])]
    unnamed x40 -> x46, local copies, waits for them, and re-layouts: 16.1 us -> 6.27 us
  transfers between devices with their start and end apart: 17 -> 21, of which waited for: 5 -> 6; matrix products, arithmetic and copies ran while one was open for 23% -> 4% of each run, Pallas kernels for 0% -> 7%
where the time goes in v1:
time: 219 us; the launch traced here: 218 us
  starting transfers between devices  66.5 us (30%)
  blocking collectives  57.8 us (26%)
  waiting for transfers between devices  37.9 us (17%)
  Pallas kernels  26.2 us (12%)
  other arithmetic  14.2 us (6%)
  local copies, waits for them, and re-layouts  14 us (6%)
    all_to_all x2, blocking collectives, sum_over(): return jnp.sum(lax.all_to_all(parts, axis, 0, 0).astype(F32), 0)  35.8 us
    ppermute x8, starting transfers between devices, diagonal(): return lax.ppermute(value, ('lon', 'lat'), pairs)  28.3 us
    pallas_call x5, Pallas kernels, call(): pl.pallas_call(kernel, name=name, out_shape=out_shape, in_specs=([SMEM] i...  26.2 us
    all_to_all x2, blocking collectives, spread_over(): got = lax.all_to_all(same, axis, 0, 0)  22 us
    ppermute x4, starting transfers between devices, across(): lax.ppermute(value, 'lat', [(i, i + step) for i in range(lats) if 0 <= i...  13.9 us
    ppermute x1, waiting for transfers between devices, reduce_grads(): got = lax.ppermute(away, 'dp', [(i, (i + 2) % 4) for i in range(4)])  13.5 us
    ppermute x8, waiting for transfers between devices, diagonal(): return lax.ppermute(value, ('lon', 'lat'), pairs)  11.9 us
    ppermute x1, waiting for transfers between devices, reduce_grads(): other = lax.ppermute(part, 'dp', [(i, (i + 2) % 4) for i in range(4)])  8.92 us
  transfers between devices with their start and end apart: 21, of which 6 were waited for; matrix products, arithmetic and copies ran while one was open for 4% of the time, Pallas kernels for 7%

profile of v1, /device:TPU:1, one launch (start us, length us, event | category | flops | bytes accessed | tf_op | source)
XLA Modules:
  0.0 217.7 jit_solution(8554018293357266636)
XLA Ops:
  2.2 2.4 %copy_bitcast_fusion = (bf16[256,1024]{1,0:T(8,128)(2,1)}, bf16[256,1024]{1,0:T(8,128)(2,1)}) fusion(bf16[32,8,8,128]{3,2,1,0:T(8,128)(2,1)} %bitcast.45, bf16[32,8,8,128]{3,2,1,0:T(8,128)(2,1)} %bitcast.46), kind=kLoop, calls=%fused_computation.11 | loop fusion | bytes 2097152 | tf_op jit(solution)/shard_map/reshape | solution.py:310
  4.6 4.4 %stack.3.flags = s32[6]{0:T(128)} concatenate(s32[1]{0:T(128)} %bitcast, s32[1]{0:T(128)} %bitcast.1, s32[1]{0:T(128)} %bitcast.2, s32[1]{0:T(128)} %bitcast.3, s32[1]{0:T(128)} %bitcast.4, s32[1]{0:T(128)} %bitcast.5), dimensions={0} | concatenate | bytes 48 | tf_op jit(solution)/shard_map/stack | solution.py:264
  9.0 2.3 %prepare.1 = (bf16[16,256]{1,0:T(8,128)(2,1)}, bf16[16,256]{1,0:T(8,128)(2,1)}, bf16[512,128]{1,0:T(8,128)(2,1)}, bf16[512,128]{1,0:T(8,128)(2,1)}, bf16[8,256]{...) custom-call(s32[6]{0:T(128)} %stack.3.flags, ...), custom_call_target="tpu_custom_call" | custom-call | tf_op jit(solution)/shard_map/prepare/pallas_call | solution.py:204
  11.3 5.6 %collective-permute-start.2 = (bf16[512,128]{1,0:T(8,128)(2,1)}, bf16[512,128]{1,0:T(8,128)(2,1)S(1)}, u32[]{:S(2)}, u32[]{:S(2)}) collective-permute-start(bf16[512,128]{1,0:T(8,128)(2,1)} %get-tuple-element.29), channel_id=1, source_target_pairs={{0,4},{4,8},{8,12},{12,16},{16,20},{20,24},{24,28},{1,5},{5,9},{9,... | collective-permute-start | bytes 393224 | tf_op jit(solution)/shard_map/ppermute | solution.py:234
  18.2 6.8 %collective-permute-start.4 = (bf16[8,256]{1,0:T(8,128)(2,1)}, bf16[8,256]{1,0:T(8,128)(2,1)S(1)}, u32[]{:S(2)}, u32[]{:S(2)}) collective-permute-start(bf16[8,256]{1,0:T(8,128)(2,1)} %get-tuple-element.31), channel_id=1, source_target_pairs={{0,36},{4,40},{8,44},{12,48},{16,52},{20,56},{24,60},{32,68},{36,7... | collective-permute-start | bytes 12296 | tf_op jit(solution)/shard_map/ppermute | solution.py:245
  25.1 5.9 %collective-permute-start.5 = (bf16[8,256]{1,0:T(8,128)(2,1)}, bf16[8,256]{1,0:T(8,128)(2,1)S(1)}, u32[]{:S(2)}, u32[]{:S(2)}) collective-permute-start(bf16[8,256]{1,0:T(8,128)(2,1)} %get-tuple-element.32), channel_id=1, source_target_pairs={{0,228},{4,232},{8,236},{12,240},{16,244},{20,248},{24,252},{32,4}... | collective-permute-start | bytes 12296 | tf_op jit(solution)/shard_map/ppermute | solution.py:245
  32.4 3.1 %collective-permute-start.1 = (bf16[16,256]{1,0:T(8,128)(2,1)}, bf16[16,256]{1,0:T(8,128)(2,1)S(1)}, u32[]{:S(2)}, u32[]{:S(2)}) collective-permute-start(bf16[16,256]{1,0:T(8,128)(2,1)} %get-tuple-element.28), channel_id=1, source_target_pairs={{0,224},{32,0},{64,32},{96,64},{128,96},{160,128},{192,160},{224,1... | collective-permute-start | bytes 24584 | tf_op jit(solution)/shard_map/ppermute | solution.py:231
  35.5 3.6 %collective-permute-done.6.refs_6_ = bf16[8,256]{1,0:T(8,128)(2,1)S(1)} collective-permute-done((bf16[8,256]{1,0:T(8,128)(2,1)}, bf16[8,256]{1,0:T(8,128)(2,1)S(1)}, u32[]{:S(2)}, u32[]{:S(2)}) %collective-permute-start.6) | collective-permute-done | bytes 4128 | tf_op jit(solution)/shard_map/ppermute | solution.py:245
  40.4 5.7 %collective-permute-done.7.refs_7_ = bf16[8,256]{1,0:T(8,128)(2,1)S(1)} collective-permute-done((bf16[8,256]{1,0:T(8,128)(2,1)}, bf16[8,256]{1,0:T(8,128)(2,1)S(1)}, u32[]{:S(2)}, u32[]{:S(2)}) %collective-permute-start.7) | collective-permute-done | bytes 4128 | tf_op jit(solution)/shard_map/ppermute | solution.py:245
  47.4 7.7 %hidden.1 = (bf16[256,1024]{1,0:T(8,128)(2,1)}, bf16[256,1024]{1,0:T(8,128)(2,1)}, bf16[3,256,1280]{2,1,0:T(8,128)(2,1)}, bf16[16,256]{1,0:T(8,128)(2,1)}, bf16[...) custom-call(s32[6]{0:T(128)} %stack.3.flags, ...), custom_call_target="tpu_custom_call" | custom-call | tf_op jit(solution)/shard_map/hidden/pallas_call | solution.py:204
  55.1 3.4 %collective-permute-start.12 = (bf16[8,256]{1,0:T(8,128)(2,1)}, bf16[8,256]{1,0:T(8,128)(2,1)S(1)}, u32[]{:S(2)}, u32[]{:S(2)}) collective-permute-start(bf16[8,256]{1,0:T(8,128)(2,1)} %get-tuple-element.41), channel_id=1, source_target_pairs={{0,36},{4,40},{8,44},{12,48},{16,52},{20,56},{24,60},{32,68},{36,7... | collective-permute-start | bytes 12296 | tf_op jit(solution)/shard_map/ppermute | solution.py:245
  58.5 7.0 %collective-permute-start.13 = (bf16[8,256]{1,0:T(8,128)(2,1)}, bf16[8,256]{1,0:T(8,128)(2,1)S(1)}, u32[]{:S(2)}, u32[]{:S(2)}) collective-permute-start(bf16[8,256]{1,0:T(8,128)(2,1)} %get-tuple-element.42), channel_id=1, source_target_pairs={{0,228},{4,232},{8,236},{12,240},{16,244},{20,248},{24,252},{32,4}... | collective-permute-start | bytes 12296 | tf_op jit(solution)/shard_map/ppermute | solution.py:245
  66.9 2.7 %collective-permute-start.9 = (bf16[16,256]{1,0:T(8,128)(2,1)}, bf16[16,256]{1,0:T(8,128)(2,1)S(1)}, u32[]{:S(2)}, u32[]{:S(2)}) collective-permute-start(bf16[16,256]{1,0:T(8,128)(2,1)} %get-tuple-element.38), channel_id=1, source_target_pairs={{0,224},{32,0},{64,32},{96,64},{128,96},{160,128},{192,160},{224,1... | collective-permute-start | bytes 24584 | tf_op jit(solution)/shard_map/ppermute | solution.py:231
  69.6 4.6 %grad_one.1 = f32[9,256,256]{2,1,0:T(8,128)} custom-call(bf16[256,1024]{1,0:T(8,128)(2,1)} %get-tuple-element.35.back.grad_tile, bf16[3,256,1280]{2,1,0:T(8,128)(2,1)} %get-tuple-element.48.pads), custom_call_target="tpu_custom_call" | custom-call | tf_op jit(solution)/shard_map/grad_one/pallas_call | solution.py:204
  74.2 5.6 %collective-permute-start.10 = (bf16[512,128]{1,0:T(8,128)(2,1)S(1)}, bf16[512,128]{1,0:T(8,128)(2,1)S(1)}, u32[]{:S(2)}, u32[]{:S(2)}) collective-permute-start(bf16[512,128]{1,0:T(8,128)(2,1)S(1)} %copy-done.20), channel_id=1, source_target_pairs={{0,4},{4,8},{8,12},{12,16},{16,20},{20,24},{24,28},{1,5},{5,9},{9,... | collective-permute-start | bytes 393224 | tf_op jit(solution)/shard_map/ppermute | solution.py:234
  82.5 2.8 %bitcast_convert_fusion.1 = bf16[2304,256]{1,0:T(8,128)(2,1)} fusion(f32[9,256,256]{2,1,0:T(8,128)} %grad_one.1), kind=kLoop, calls=%fused_computation.4 | loop fusion | flops 589824 | bytes 3538944 | tf_op jit(solution)/shard_map/convert_element_type | solution.py:287
  85.3 2.6 %collective-permute-done.15.refs_7_ = bf16[8,256]{1,0:T(8,128)(2,1)S(1)} collective-permute-done((bf16[8,256]{1,0:T(8,128)(2,1)S(1)}, bf16[8,256]{1,0:T(8,128)(2,1)S(1)}, u32[]{:S(2)}, u32[]{:S(2)}) %collective-permute-start.15) | collective-permute-done | bytes 4128 | tf_op jit(solution)/shard_map/ppermute | solution.py:245
  87.9 8.3 %collective-permute-start.16 = (bf16[2304,256]{1,0:T(8,128)(2,1)}, bf16[2304,256]{1,0:T(8,128)(2,1)S(1)}, u32[]{:S(2)}, u32[]{:S(2)}) collective-permute-start(bf16[2304,256]{1,0:T(8,128)(2,1)} %bitcast_convert_fusion.1), channel_id=1, source_target_pairs={{1,0},{3,2},{5,4},{7,6},{9,8},{11,10},{13,12},{15,14},{17,16},{19,... | collective-permute-start | bytes 3538952 | tf_op jit(solution)/shard_map/ppermute | solution.py:287
  97.0 4.5 %grad_two.1 = (bf16[3,256,1280]{2,1,0:T(8,128)(2,1)}, f32[9,256,256]{2,1,0:T(8,128)}) custom-call(s32[6]{0:T(128)} %stack.3.flags, bf16[256,1024]{1,0:T(8,128)(2,1)} %get-tuple-element.36.act, bf16[256,1024]{1,0:T(8,128)(2,1)} %get-tuple-element.60.second.cotangent, bf16[16,256]{1,0:T(8,128)(2,1)} %copy-done.7, bf16[16,256]{1,0:T(8,128)(2,1)} %copy-done.8, ...), custom_call_target="tpu_custom_call" | custom-call | tf_op jit(solution)/shard_map/grad_two/pallas_call | solution.py:204
  101.6 3.0 %bitcast_convert_fusion = bf16[2304,256]{1,0:T(8,128)(2,1)} fusion(f32[9,256,256]{2,1,0:T(8,128)} %get-tuple-element.49), kind=kLoop, calls=%fused_computation.1 | loop fusion | flops 589824 | bytes 3538944 | tf_op jit(solution)/shard_map/convert_element_type | solution.py:288
  106.1 3.6 %collective-permute-done.17 = bf16[2304,256]{1,0:T(8,128)(2,1)} collective-permute-done((bf16[2304,256]{1,0:T(8,128)(2,1)}, bf16[2304,256]{1,0:T(8,128)(2,1)}, u32[]{:S(2)}, u32[]{:S(2)}) %collective-permute-start.17) | collective-permute-done | bytes 1179680 | tf_op jit(solution)/shard_map/ppermute | solution.py:288
  109.6 2.4 %fusion = f32[2304,256]{1,0:T(8,128)S(1)} fusion(f32[9,256,256]{2,1,0:T(8,128)} %get-tuple-element.49, f32[9,256,256]{2,1,0:T(8,128)S(1)} %copy-done, bf16[2304,256]{1,0:T(8,128)(2,1)} %collective-permute-done.17, bf16[2304,256]{1,0:T(8,128)(2,1)S(1)} %collective-permute-done.16, pred[]{:T(512)S(6)} %eq.10), kind=kLoop, calls=%fused_computation.2 | loop fusion | flops 2949120 | bytes 9437185 | tf_op jit(solution)/shard_map/jit(_where)/select_n | solution.py:289
  114.9 13.5 %collective-permute-done.18 = bf16[1152,256]{1,0:T(8,128)(2,1)S(1)} collective-permute-done((bf16[1152,256]{1,0:T(8,128)(2,1)S(1)}, bf16[1152,256]{1,0:T(8,128)(2,1)S(1)}, u32[]{:S(2)}, u32[]{:S(2)}) %collective-permute-start.18) | collective-permute-done | bytes 589856 | tf_op jit(solution)/shard_map/ppermute | solution.py:293
  129.8 21.2 %all_to_all.20 = bf16[8,144,256]{2,1,0:T(8,128)(2,1)S(1)} all-to-all(bf16[8,144,256]{2,1,0:T(8,128)(2,1)S(1)} %bitcast.40), channel_id=1, replica_groups=mesh['lon'=8,'lat'=8,'dp'=4] {'lat'}, dimensions={0} | all-to-all | bytes 1179648 | tf_op jit(solution)/shard_map/all_to_all | solution.py:272
  151.0 14.6 %all_to_all.21 = f32[8,18,256]{2,1,0:T(8,128)S(1)} all-to-all(f32[8,18,256]{2,1,0:T(8,128)S(1)} %reshape.56), channel_id=1, replica_groups=mesh['lon'=8,'lat'=8,'dp'=4] {'lon'}, dimensions={0} | all-to-all | bytes 294912 | tf_op jit(solution)/shard_map/all_to_all | solution.py:272
  165.7 10.0 %all_to_all.22 = bf16[8,18,256]{2,1,0:T(8,128)(2,1)S(1)} all-to-all(bf16[8,18,256]{2,1,0:T(8,128)(2,1)S(1)} %broadcast_in_dim.6), channel_id=1, replica_groups=mesh['lon'=8,'lat'=8,'dp'=4] {'lon'}, dimensions={0} | all-to-all | bytes 147456 | tf_op jit(solution)/shard_map/all_to_all | solution.py:278
  175.7 12.1 %all_to_all.23 = bf16[8,144,256]{2,1,0:T(8,128)(2,1)S(1)} all-to-all(bf16[8,144,256]{2,1,0:T(8,128)(2,1)S(1)} %broadcast_in_dim.15), channel_id=1, replica_groups=mesh['lon'=8,'lat'=8,'dp'=4] {'lat'}, dimensions={0} | all-to-all | bytes 1179648 | tf_op jit(solution)/shard_map/all_to_all | solution.py:278
  188.2 8.9 %collective-permute-done.19 = bf16[1152,256]{1,0:T(8,128)(2,1)S(1)} collective-permute-done((bf16[1152,256]{1,0:T(8,128)(2,1)S(1)}, bf16[1152,256]{1,0:T(8,128)(2,1)S(1)}, u32[]{:S(2)}, u32[]{:S(2)}) %collective-permute-start.19) | collective-permute-done | bytes 589856 | tf_op jit(solution)/shard_map/ppermute | solution.py:297
  197.4 6.8 %collective-permute-start.20 = (bf16[2304,256]{1,0:T(8,128)(2,1)S(1)}, bf16[2304,256]{1,0:T(8,128)(2,1)S(1)}, u32[]{:S(2)}, u32[]{:S(2)}) collective-permute-start(bf16[2304,256]{1,0:T(8,128)(2,1)S(1)} %maximum_select_fusion), channel_id=1, source_target_pairs={{0,1},{1,0},{2,3},{3,2},{4,5},{5,4},{6,7},{7,6},{8,9},{9,8},{10,11... | collective-permute-start | bytes 3538952 | tf_op jit(solution)/shard_map/ppermute | solution.py:301
  204.2 7.1 %result.1 = (bf16[256,1024]{1,0:T(8,128)(2,1)}, bf16[256,1024]{1,0:T(8,128)(2,1)}) custom-call(s32[6]{0:T(128)} %stack.3.flags, bf16[256,1024]{1,0:T(8,128)(2,1)} %get-tuple-element.61.first.field, bf16[256,1024]{1,0:T(8,128)(2,1)} %get-tuple-element.60.second.cotangent, bf16[256,1024]{1,0:T(8,128)(2,1)} %get-tuple-element.35.back.grad_tile, ...), custom_call_target="tpu_custom_call" | custom-call | tf_op jit(solution)/shard_map/result/pallas_call | solution.py:204
  211.4 2.0 copy.11
  214.4 1.6 convert.2
  (88 shorter events, 20.8 us)
Async XLA Ops:
  11.3 34.8 %collective-permute-start.2 = (bf16[512,128]{1,0:T(8,128)(2,1)}, bf16[512,128]{1,0:T(8,128)(2,1)S(1)}, u32[]{:S(2)}, u32[]{:S(2)}) collective-permute-start(bf16[512,128]{1,0:T(8,128)(2,1)} %get-tuple-element.29), channel_id=1, source_target_pairs={{0,4},{4,8},{8,12},{12,16},{16,20},{20,24},{24,28},{1,5},{5,9},{9,... | collective-permute-start | bytes 393224 | tf_op jit(solution)/shard_map/ppermute | solution.py:234
  16.9 29.2 %collective-permute-start.3 = (bf16[512,128]{1,0:T(8,128)(2,1)}, bf16[512,128]{1,0:T(8,128)(2,1)S(1)}, u32[]{:S(2)}, u32[]{:S(2)}) collective-permute-start(bf16[512,128]{1,0:T(8,128)(2,1)} %get-tuple-element.30), channel_id=1, source_target_pairs={{4,0},{8,4},{12,8},{16,12},{20,16},{24,20},{28,24},{5,1},{9,5},{13... | collective-permute-start | bytes 393224 | tf_op jit(solution)/shard_map/ppermute | solution.py:234
  18.2 14.0 %collective-permute-start.4 = (bf16[8,256]{1,0:T(8,128)(2,1)}, bf16[8,256]{1,0:T(8,128)(2,1)S(1)}, u32[]{:S(2)}, u32[]{:S(2)}) collective-permute-start(bf16[8,256]{1,0:T(8,128)(2,1)} %get-tuple-element.31), channel_id=1, source_target_pairs={{0,36},{4,40},{8,44},{12,48},{16,52},{20,56},{24,60},{32,68},{36,7... | collective-permute-start | bytes 12296 | tf_op jit(solution)/shard_map/ppermute | solution.py:245
  25.1 7.3 %collective-permute-start.5 = (bf16[8,256]{1,0:T(8,128)(2,1)}, bf16[8,256]{1,0:T(8,128)(2,1)S(1)}, u32[]{:S(2)}, u32[]{:S(2)}) collective-permute-start(bf16[8,256]{1,0:T(8,128)(2,1)} %get-tuple-element.32), channel_id=1, source_target_pairs={{0,228},{4,232},{8,236},{12,240},{16,244},{20,248},{24,252},{32,4}... | collective-permute-start | bytes 12296 | tf_op jit(solution)/shard_map/ppermute | solution.py:245
  30.9 8.2 %collective-permute-start.6 = (bf16[8,256]{1,0:T(8,128)(2,1)}, bf16[8,256]{1,0:T(8,128)(2,1)S(1)}, u32[]{:S(2)}, u32[]{:S(2)}) collective-permute-start(bf16[8,256]{1,0:T(8,128)(2,1)} %get-tuple-element.33), channel_id=1, source_target_pairs={{4,32},{8,36},{12,40},{16,44},{20,48},{24,52},{28,56},{36,64},{40,... | collective-permute-start | bytes 12296 | tf_op jit(solution)/shard_map/ppermute | solution.py:245
  32.2 13.9 %copy-start.15 = (bf16[8,256]{1,0:T(8,128)(2,1)}, bf16[8,256]{1,0:T(8,128)(2,1)S(1)}, u32[]{:S(2)}) copy-start(bf16[8,256]{1,0:T(8,128)(2,1)S(1)} %collective-permute-done.4.refs_4_) | copy-start | bytes 12292
  32.2 13.8 %collective-permute-start = (bf16[16,256]{1,0:T(8,128)(2,1)}, bf16[16,256]{1,0:T(8,128)(2,1)S(1)}, u32[]{:S(2)}, u32[]{:S(2)}) collective-permute-start(bf16[16,256]{1,0:T(8,128)(2,1)} %get-tuple-element.27), channel_id=1, source_target_pairs={{0,32},{32,64},{64,96},{96,128},{128,160},{160,192},{192,224},{224... | collective-permute-start | bytes 24584 | tf_op jit(solution)/shard_map/ppermute | solution.py:231
  32.3 13.8 %copy-start.16 = (bf16[8,256]{1,0:T(8,128)(2,1)}, bf16[8,256]{1,0:T(8,128)(2,1)S(1)}, u32[]{:S(2)}) copy-start(bf16[8,256]{1,0:T(8,128)(2,1)S(1)} %collective-permute-done.5.refs_5_) | copy-start | bytes 12292
  32.4 13.7 %collective-permute-start.1 = (bf16[16,256]{1,0:T(8,128)(2,1)}, bf16[16,256]{1,0:T(8,128)(2,1)S(1)}, u32[]{:S(2)}, u32[]{:S(2)}) collective-permute-start(bf16[16,256]{1,0:T(8,128)(2,1)} %get-tuple-element.28), channel_id=1, source_target_pairs={{0,224},{32,0},{64,32},{96,64},{128,96},{160,128},{192,160},{224,1... | collective-permute-start | bytes 24584 | tf_op jit(solution)/shard_map/ppermute | solution.py:231
  39.1 7.0 %copy-start.17 = (bf16[8,256]{1,0:T(8,128)(2,1)}, bf16[8,256]{1,0:T(8,128)(2,1)S(1)}, u32[]{:S(2)}) copy-start(bf16[8,256]{1,0:T(8,128)(2,1)S(1)} %collective-permute-done.6.refs_6_) | copy-start | bytes 12292
  39.1 7.0 %collective-permute-start.7 = (bf16[8,256]{1,0:T(8,128)(2,1)}, bf16[8,256]{1,0:T(8,128)(2,1)S(1)}, u32[]{:S(2)}, u32[]{:S(2)}) collective-permute-start(bf16[8,256]{1,0:T(8,128)(2,1)} %get-tuple-element.34), channel_id=1, source_target_pairs={{4,224},{8,228},{12,232},{16,236},{20,240},{24,244},{28,248},{36,0... | collective-permute-start | bytes 12296 | tf_op jit(solution)/shard_map/ppermute | solution.py:245
  55.1 19.1 %collective-permute-start.12 = (bf16[8,256]{1,0:T(8,128)(2,1)}, bf16[8,256]{1,0:T(8,128)(2,1)S(1)}, u32[]{:S(2)}, u32[]{:S(2)}) collective-permute-start(bf16[8,256]{1,0:T(8,128)(2,1)} %get-tuple-element.41), channel_id=1, source_target_pairs={{0,36},{4,40},{8,44},{12,48},{16,52},{20,56},{24,60},{32,68},{36,7... | collective-permute-start | bytes 12296 | tf_op jit(solution)/shard_map/ppermute | solution.py:245
  58.5 21.3 %collective-permute-start.13 = (bf16[8,256]{1,0:T(8,128)(2,1)}, bf16[8,256]{1,0:T(8,128)(2,1)S(1)}, u32[]{:S(2)}, u32[]{:S(2)}) collective-permute-start(bf16[8,256]{1,0:T(8,128)(2,1)} %get-tuple-element.42), channel_id=1, source_target_pairs={{0,228},{4,232},{8,236},{12,240},{16,244},{20,248},{24,252},{32,4}... | collective-permute-start | bytes 12296 | tf_op jit(solution)/shard_map/ppermute | solution.py:245
  65.5 15.6 %collective-permute-start.14 = (bf16[8,256]{1,0:T(8,128)(2,1)}, bf16[8,256]{1,0:T(8,128)(2,1)S(1)}, u32[]{:S(2)}, u32[]{:S(2)}) collective-permute-start(bf16[8,256]{1,0:T(8,128)(2,1)} %get-tuple-element.43), channel_id=1, source_target_pairs={{4,32},{8,36},{12,40},{16,44},{20,48},{24,52},{28,56},{36,64},{40,... | collective-permute-start | bytes 12296 | tf_op jit(solution)/shard_map/ppermute | solution.py:245
  66.8 29.5 %collective-permute-start.8 = (bf16[16,256]{1,0:T(8,128)(2,1)}, bf16[16,256]{1,0:T(8,128)(2,1)S(1)}, u32[]{:S(2)}, u32[]{:S(2)}) collective-permute-start(bf16[16,256]{1,0:T(8,128)(2,1)} %get-tuple-element.37), channel_id=1, source_target_pairs={{0,32},{32,64},{64,96},{96,128},{128,160},{160,192},{192,224},{224... | collective-permute-start | bytes 24584 | tf_op jit(solution)/shard_map/ppermute | solution.py:231
  66.9 29.4 %collective-permute-start.9 = (bf16[16,256]{1,0:T(8,128)(2,1)}, bf16[16,256]{1,0:T(8,128)(2,1)S(1)}, u32[]{:S(2)}, u32[]{:S(2)}) collective-permute-start(bf16[16,256]{1,0:T(8,128)(2,1)} %get-tuple-element.38), channel_id=1, source_target_pairs={{0,224},{32,0},{64,32},{96,64},{128,96},{160,128},{192,160},{224,1... | collective-permute-start | bytes 24584 | tf_op jit(solution)/shard_map/ppermute | solution.py:231
  69.6 4.6 %copy-start.20 = (bf16[512,128]{1,0:T(8,128)(2,1)S(1)}, bf16[512,128]{1,0:T(8,128)(2,1)}, u32[]{:S(2)}) copy-start(bf16[512,128]{1,0:T(8,128)(2,1)} %get-tuple-element.39) | copy-start | bytes 393220
  69.6 10.3 %copy-start.19 = (bf16[512,128]{1,0:T(8,128)(2,1)S(1)}, bf16[512,128]{1,0:T(8,128)(2,1)}, u32[]{:S(2)}) copy-start(bf16[512,128]{1,0:T(8,128)(2,1)} %get-tuple-element.40) | copy-start | bytes 393220
  69.6 11.6 %copy-start.21 = (bf16[8,256]{1,0:T(8,128)(2,1)S(1)}, bf16[8,256]{1,0:T(8,128)(2,1)}, u32[]{:S(2)}) copy-start(bf16[8,256]{1,0:T(8,128)(2,1)} %get-tuple-element.44) | copy-start | bytes 12292
  74.2 11.1 %copy-start.9 = (bf16[8,256]{1,0:T(8,128)(2,1)}, bf16[8,256]{1,0:T(8,128)(2,1)S(1)}, u32[]{:S(2)}) copy-start(bf16[8,256]{1,0:T(8,128)(2,1)S(1)} %collective-permute-done.12.refs_4_) | copy-start | bytes 12292
  74.2 22.1 %collective-permute-start.10 = (bf16[512,128]{1,0:T(8,128)(2,1)S(1)}, bf16[512,128]{1,0:T(8,128)(2,1)S(1)}, u32[]{:S(2)}, u32[]{:S(2)}) collective-permute-start(bf16[512,128]{1,0:T(8,128)(2,1)S(1)} %copy-done.20), channel_id=1, source_target_pairs={{0,4},{4,8},{8,12},{12,16},{16,20},{20,24},{24,28},{1,5},{5,9},{9,... | collective-permute-start | bytes 393224 | tf_op jit(solution)/shard_map/ppermute | solution.py:234
  79.8 5.5 %copy-start.10 = (bf16[8,256]{1,0:T(8,128)(2,1)}, bf16[8,256]{1,0:T(8,128)(2,1)S(1)}, u32[]{:S(2)}) copy-start(bf16[8,256]{1,0:T(8,128)(2,1)S(1)} %collective-permute-done.13.refs_5_) | copy-start | bytes 12292
  79.9 16.5 %collective-permute-start.11 = (bf16[512,128]{1,0:T(8,128)(2,1)S(1)}, bf16[512,128]{1,0:T(8,128)(2,1)S(1)}, u32[]{:S(2)}, u32[]{:S(2)}) collective-permute-start(bf16[512,128]{1,0:T(8,128)(2,1)S(1)} %copy-done.19), channel_id=1, source_target_pairs={{4,0},{8,4},{12,8},{16,12},{20,16},{24,20},{28,24},{5,1},{9,5},{13... | collective-permute-start | bytes 393224 | tf_op jit(solution)/shard_map/ppermute | solution.py:234
  81.2 4.2 %copy-start.11 = (bf16[8,256]{1,0:T(8,128)(2,1)}, bf16[8,256]{1,0:T(8,128)(2,1)S(1)}, u32[]{:S(2)}) copy-start(bf16[8,256]{1,0:T(8,128)(2,1)S(1)} %collective-permute-done.14.refs_6_) | copy-start | bytes 12292
  81.2 6.8 %collective-permute-start.15 = (bf16[8,256]{1,0:T(8,128)(2,1)S(1)}, bf16[8,256]{1,0:T(8,128)(2,1)S(1)}, u32[]{:S(2)}, u32[]{:S(2)}) collective-permute-start(bf16[8,256]{1,0:T(8,128)(2,1)S(1)} %copy-done.21), channel_id=1, source_target_pairs={{4,224},{8,228},{12,232},{16,236},{20,240},{24,244},{28,248},{36,0... | collective-permute-start | bytes 12296 | tf_op jit(solution)/shard_map/ppermute | solution.py:245
  87.9 8.4 %copy-start.12 = (bf16[8,256]{1,0:T(8,128)(2,1)}, bf16[8,256]{1,0:T(8,128)(2,1)S(1)}, u32[]{:S(2)}) copy-start(bf16[8,256]{1,0:T(8,128)(2,1)S(1)} %collective-permute-done.15.refs_7_) | copy-start | bytes 12292
  87.9 18.1 %collective-permute-start.16 = (bf16[2304,256]{1,0:T(8,128)(2,1)}, bf16[2304,256]{1,0:T(8,128)(2,1)S(1)}, u32[]{:S(2)}, u32[]{:S(2)}) collective-permute-start(bf16[2304,256]{1,0:T(8,128)(2,1)} %bitcast_convert_fusion.1), channel_id=1, source_target_pairs={{1,0},{3,2},{5,4},{7,6},{9,8},{11,10},{13,12},{15,14},{17,16},{19,... | collective-permute-start | bytes 3538952 | tf_op jit(solution)/shard_map/ppermute | solution.py:287
  101.6 8.0 %copy-start = (f32[9,256,256]{2,1,0:T(8,128)S(1)}, f32[9,256,256]{2,1,0:T(8,128)}, u32[]{:S(2)}) copy-start(f32[9,256,256]{2,1,0:T(8,128)} %grad_one.1) | copy-start | bytes 7077892
  104.6 5.1 %collective-permute-start.17 = (bf16[2304,256]{1,0:T(8,128)(2,1)}, bf16[2304,256]{1,0:T(8,128)(2,1)}, u32[]{:S(2)}, u32[]{:S(2)}) collective-permute-start(bf16[2304,256]{1,0:T(8,128)(2,1)} %bitcast_convert_fusion), channel_id=1, source_target_pairs={{0,1},{2,3},{4,5},{6,7},{8,9},{10,11},{12,13},{14,15},{16,17},{18,... | collective-permute-start | bytes 3538952 | tf_op jit(solution)/shard_map/ppermute | solution.py:288
  113.5 14.8 %collective-permute-start.18 = (bf16[1152,256]{1,0:T(8,128)(2,1)S(1)}, bf16[1152,256]{1,0:T(8,128)(2,1)S(1)}, u32[]{:S(2)}, u32[]{:S(2)}) collective-permute-start(bf16[1152,256]{1,0:T(8,128)(2,1)S(1)} %dynamic-slice_convert_fusion), channel_id=1, source_target_pairs={{0,2},{1,3},{2,0},{3,1},{4,6},{5,7},{6,4},{7,5},{8,10},{9,11},{10,... | collective-permute-start | bytes 1769480 | tf_op jit(solution)/shard_map/ppermute | solution.py:293
  187.8 9.4 %collective-permute-start.19 = (bf16[1152,256]{1,0:T(8,128)(2,1)S(1)}, bf16[1152,256]{1,0:T(8,128)(2,1)S(1)}, u32[]{:S(2)}, u32[]{:S(2)}) collective-permute-start(bf16[1152,256]{1,0:T(8,128)(2,1)S(1)} %bitcast.38), channel_id=1, source_target_pairs={{0,2},{1,3},{2,0},{3,1},{4,6},{5,7},{6,4},{7,5},{8,10},{9,11},{10,... | collective-permute-start | bytes 1769480 | tf_op jit(solution)/shard_map/ppermute | solution.py:297
  197.4 16.8 %collective-permute-start.20 = (bf16[2304,256]{1,0:T(8,128)(2,1)S(1)}, bf16[2304,256]{1,0:T(8,128)(2,1)S(1)}, u32[]{:S(2)}, u32[]{:S(2)}) collective-permute-start(bf16[2304,256]{1,0:T(8,128)(2,1)S(1)} %maximum_select_fusion), channel_id=1, source_target_pairs={{0,1},{1,0},{2,3},{3,2},{4,5},{5,4},{6,7},{7,6},{8,9},{9,8},{10,11... | collective-permute-start | bytes 3538952 | tf_op jit(solution)/shard_map/ppermute | solution.py:301
  (11 other events, 9.0 us)

commit v2 on v1

v2 whole, which is shorter than its diff:
```python
import jax
import jax.numpy as jnp
from jax import lax
from jax.experimental import pallas as pl
from jax.experimental.pallas import tpu as pltpu
from jax.sharding import PartitionSpec as P

F32 = jnp.float32
BF16 = jnp.bfloat16
LANES = 128
ROWS = 8
CELLS = ROWS * LANES
PADDED = CELLS + 2 * LANES
NT = (((1,), (1,)), ((), ()))
TN = (((0,), (0,)), ((), ()))


def iota(shape, dim):
    return lax.broadcasted_iota(jnp.int32, shape, dim)


def one_hot(cond):
    return jnp.where(cond, 1.0, 0.0).astype(BF16)


def dot(a, b):
    return jnp.dot(a, b, preferred_element_type=F32)


def edge_flags(flips):
    a, o = (lax.axis_index("lat"), lax.axis_index("lon"))
    edges, lons = flips.shape

    def upper(col):
        return jnp.where(a > 0, flips[jnp.maximum(a - 1, 0), col], 0)

    def lower(col):
        return jnp.where(a < edges, flips[jnp.minimum(a, edges - 1), col], 0)

    west, east = (lax.rem(o + lons - 1, lons), lax.rem(o + 1, lons))
    return (upper(o), lower(o), upper(west), upper(east), lower(west), lower(east))


def rims(first, second, flags, outs):
    east, west, south, north = outs
    shape = (2 * ROWS, CELLS)
    row, cell = (iota(shape, 0), iota(shape, 1))
    pick = one_hot(cell == jnp.where(row < ROWS, row * LANES + LANES - 1, (row - ROWS) * LANES))
    one = lax.dot_general(pick, first, NT, preferred_element_type=F32)
    two = lax.dot_general(pick, second, NT, preferred_element_type=F32)
    chans = first.shape[0]
    upper, lower = (flags[0] == 1, flags[1] == 1)
    end = ROWS - 1

    def side(out, base, far):
        top = jnp.where(upper, two[far : far + 1], two[base : base + 1])
        low = jnp.where(lower, two[far + end : far + ROWS], two[base + end : base + ROWS])
        at = iota((ROWS, chans), 0)
        corners = jnp.where(at == 0, jnp.broadcast_to(top, at.shape), jnp.broadcast_to(low, at.shape))
        out[...] = jnp.concatenate(
            [one[base : base + ROWS], two[base : base + ROWS], corners, corners], 0
        ).astype(BF16)

    side(east, 0, ROWS)
    side(west, ROWS, 0)
    south[:chans] = first[:, CELLS - LANES :]
    south[chans:] = second[:, CELLS - LANES :]
    north[:chans] = first[:, :LANES]
    north[chans:] = second[:, :LANES]


def join_kernel(south, north, from_w, from_e, south_out, north_out):
    rows = south.shape[0]
    west, east = (from_w[...].astype(F32), from_e[...].astype(F32))
    at = iota((16, west.shape[1]), 0)
    for rim, out, near, corner in ((south, south_out, 7, 17), (north, north_out, 0, 16)):
        out[:rows] = rim[...]
        spread = [
            jnp.broadcast_to(side[k : k + 1], at.shape)
            for side in (west, east)
            for k in (near, corner)
        ]
        block = jnp.where(
            at == 0, spread[0], jnp.where(at == 1, spread[1], jnp.where(at == 2, spread[2], spread[3]))
        ).astype(BF16)
        out[rows : rows + 16] = block[:, :LANES]
        out[rows + 16 :] = block[:, LANES:]


def corners_of(line, chans):
    rows = 2 * chans
    return jnp.concatenate([line[rows : rows + 16], line[rows + 16 : rows + 32]], 1)


def turned(line, flip):
    shape = (LANES, LANES)
    a, b = (iota(shape, 0), iota(shape, 1))
    turn = one_hot(b == a + flip * (LANES - 1 - 2 * a))
    return dot(line, turn)


def shifted(out, centre, top, bottom, west, east, swap_top=None, swap_bottom=None):
    chans = centre.shape[0]
    k, lane = (iota((16, PADDED), 0), iota((16, PADDED), 1))
    placed_west = lax.dot_general(
        west, one_hot(lane == k * LANES), TN, preferred_element_type=F32
    )
    placed_east = lax.dot_general(
        east, one_hot(lane == k * LANES + LANES - 1), TN, preferred_element_type=F32
    )
    lane_in = iota((chans, LANES), 1)
    for block in range(ROWS + 2):
        span = slice(block * LANES, (block + 1) * LANES)
        if block == 0:
            line = top
        elif block == ROWS + 1:
            line = bottom
        else:
            line = centre[:, (block - 1) * LANES : block * LANES].astype(F32)
        left = jnp.where(lane_in == 0, placed_west[:, span], pltpu.roll(line, 1, 1))
        right = jnp.where(lane_in == LANES - 1, placed_east[:, span], pltpu.roll(line, LANES - 1, 1))
        swap = swap_top if block == 0 else swap_bottom if block == ROWS + 1 else None
        if swap is not None:
            left, right = (jnp.where(swap, right, left), jnp.where(swap, left, right))
        out[0, :, span] = left.astype(BF16)
        out[1, :, span] = line.astype(BF16)
        out[2, :, span] = right.astype(BF16)


def lines(top, mid, bottom):
    return jnp.concatenate([top, mid, bottom, jnp.zeros((6, mid.shape[1]), F32)], 0).astype(BF16)


def pad_forward(out, centre, flags, halo):
    from_w, from_e, from_n, from_s = halo
    chans = centre.shape[0]
    upper, lower = (flags[0] == 1, flags[1] == 1)
    above, below = (corners_of(ref, chans).astype(F32) for ref in (from_n, from_s))
    nw, ne, sw, se = (above[:1], above[2:3], below[:1], below[2:3])
    west = lines(jnp.where(upper, ne, nw), from_w[...].astype(F32)[:ROWS], jnp.where(lower, se, sw))
    east = lines(jnp.where(upper, nw, ne), from_e[...].astype(F32)[:ROWS], jnp.where(lower, sw, se))
    top = turned(from_n[:chans], flags[0])
    bottom = turned(from_s[:chans], flags[1])
    shifted(out, centre, top, bottom, west, east)


def pad_backward(out, centre, flags, halo):
    from_w, from_e, from_n, from_s = halo
    chans = centre.shape[0]
    upper, lower = (flags[0] == 1, flags[1] == 1)
    none = jnp.zeros((1, chans), F32)
    west = lines(none, from_w[...].astype(F32)[ROWS : 2 * ROWS], none)
    east = lines(none, from_e[...].astype(F32)[ROWS : 2 * ROWS], none)
    top = turned(from_n[chans : 2 * chans], flags[0])
    bottom = turned(from_s[chans : 2 * chans], flags[1])
    shifted(out, centre, top, bottom, west, east, upper, lower)


def conv(weight, pads):
    total = None
    for tap in range(9):
        r, s = divmod(tap, 3)
        term = dot(weight[tap], pads[s, :, r * LANES : r * LANES + CELLS])
        total = term if total is None else total + term
    return total


def conv_adjoint(weight, pads, flags, halo):
    total = None
    for tap in range(9):
        r, s = divmod(tap, 3)
        start = (2 - r) * LANES
        term = lax.dot_general(
            weight[tap], pads[2 - s, :, start : start + CELLS], TN, preferred_element_type=F32
        )
        total = term if total is None else total + term
    chans = total.shape[0]
    above, below = (corners_of(ref, chans) for ref in halo[2:])
    k, lane = (iota((16, LANES), 0), iota((16, LANES), 1))

    def corner(block, which, at, tap):
        spread = lax.dot_general(
            block, one_hot((k == which) & (lane == at)), TN, preferred_element_type=F32
        ).astype(BF16)
        return lax.dot_general(weight[tap], spread, TN, preferred_element_type=F32)

    east = LANES - 1
    top = corner(above, 1, 0, 8 - 2 * flags[2]) + corner(above, 3, east, 6 + 2 * flags[3])
    bottom = corner(below, 1, 0, 2 - 2 * flags[4]) + corner(below, 3, east, 2 * flags[5])
    return jnp.concatenate(
        [total[:, :LANES] + top, total[:, LANES : CELLS - LANES], total[:, CELLS - LANES :] + bottom],
        1,
    )


def prepare_kernel(flips, field, cotangent, *outs):
    flat_field, flat_cot = outs[:2]
    for row in range(ROWS):
        span = slice(row * LANES, (row + 1) * LANES)
        flat_field[:, span] = field[:, row, :]
        flat_cot[:, span] = cotangent[:, row, :]
    rims(flat_field[...], flat_cot[...], edge_flags(flips), outs[2:])


def hidden_kernel(flips, field, cotangent, one, two, *refs):
    halo, outs, back_pads = (refs[:4], refs[4:-1], refs[-1])
    act_out, back_out, pads = outs[:3]
    flags = edge_flags(flips)
    pad_forward(pads, field[...], flags, halo)
    pad_backward(back_pads, cotangent[...], flags, halo)
    hidden = conv(one, pads)
    back_act = conv_adjoint(two, back_pads, flags, halo)
    sigma = 1.0 / (1.0 + jnp.exp(-hidden))
    act_out[...] = (hidden * sigma).astype(BF16)
    back_out[...] = (back_act * sigma * (1.0 + hidden * (1.0 - sigma))).astype(BF16)
    rims(act_out[...], back_out[...], flags, outs[3:])


def grad_kernel(grad_tile, pads, out, out_low):
    for tap in range(9):
        r, s = divmod(tap, 3)
        term = lax.dot_general(
            grad_tile[...], pads[s, :, r * LANES : r * LANES + CELLS], NT, preferred_element_type=F32
        )
        chans = term.shape[0]
        for part in range(2):
            rows = slice((2 * tap + part) * chans, (2 * tap + part + 1) * chans)
            piece = term[:, part * LANES : (part + 1) * LANES]
            out[rows] = piece
            out_low[rows] = piece.astype(BF16)


def grad_two_kernel(flips, act, cotangent, *refs):
    halo, pads, outs = (refs[:4], refs[4], refs[5:])
    pad_forward(pads, act[...], edge_flags(flips), halo)
    grad_kernel(cotangent, pads, *outs)


def result_kernel(flips, field, cotangent, back, one, two, pads, *refs):
    halo, (output, grad_fields, back_pads) = (refs[:4], refs[4:])
    flags = edge_flags(flips)
    total = (field[...].astype(F32) + conv(two, pads)).astype(BF16)
    pad_backward(back_pads, back[...], flags, halo)
    grads = (cotangent[...].astype(F32) + conv_adjoint(one, back_pads, flags, halo)).astype(BF16)
    for row in range(ROWS):
        span = slice(row * LANES, (row + 1) * LANES)
        output[:, row, :] = total[:, span]
        grad_fields[:, row, :] = grads[:, span]


def finish_kernel(mine, beside, paired, across, out_one, out_two):
    place = lax.axis_index("dp")
    core, side = (lax.rem(place, 2) == 1, place >= 2)
    chans = out_one.shape[1]
    for group in range(mine.shape[0] // chans):
        rows = slice(group * chans, (group + 1) * chans)
        a, b, c, d = (ref[rows].astype(F32) for ref in (mine, beside, paired, across))
        near, far = (jnp.where(core, c, a), jnp.where(core, d, b))
        low_one, high_one = (jnp.where(side, far, near), jnp.where(side, near, far))
        near, far = (jnp.where(core, a, c), jnp.where(core, b, d))
        low_two, high_two = (jnp.where(side, far, near), jnp.where(side, near, far))
        for out, pieces in ((out_one, (low_one, high_one)), (out_two, (low_two, high_two))):
            for half, piece in enumerate(pieces):
                tap, part = divmod(group + half * 9, 2)
                out[tap, :, part * LANES : (part + 1) * LANES] = piece


SMEM = pl.BlockSpec(memory_space=pltpu.SMEM)
VMEM = pl.BlockSpec(memory_space=pltpu.VMEM)


def call(kernel, name, out_shape, args, scratch=(), flags=True):
    return pl.pallas_call(
        kernel,
        name=name,
        out_shape=out_shape,
        in_specs=([SMEM] if flags else []) + [VMEM] * (len(args) - (1 if flags else 0)),
        out_specs=jax.tree.map(lambda _: VMEM, out_shape),
        scratch_shapes=list(scratch),
        compiler_params=pltpu.CompilerParams(vmem_limit_bytes=56 * 1024 * 1024),
    )(*args)


def struct(*shape, dtype=BF16):
    return jax.ShapeDtypeStruct(shape, dtype)


def rim_shapes(chans):
    side = struct(4 * ROWS, chans)
    line = struct(2 * chans, LANES)
    return (side, side, line, line)


def exchange(rim):
    east, west, south, north = rim
    lons, lats = (lax.axis_size("lon"), lax.axis_size("lat"))

    def along(value, step):
        return lax.ppermute(value, "lon", [(i, (i + step) % lons) for i in range(lons)])

    def across(value, step):
        return lax.ppermute(
            value, "lat", [(i, i + step) for i in range(lats) if 0 <= i + step < lats]
        )

    from_w, from_e = (along(east, 1), along(west, -1))
    line = struct(south.shape[0] + 32, LANES)
    south, north = call(join_kernel, "join", (line, line), (south, north, from_w, from_e), flags=False)
    return (from_w, from_e, across(south, 1), across(north, -1))


def beside(value):
    return lax.ppermute(value, "dp", [(i, (i + 2) % 4) for i in range(4)])


def paired(value):
    return lax.ppermute(value, "dp", [(0, 1), (1, 0), (2, 3), (3, 2)])


def reduce_grads(one, two):
    (one, one_low), (two, two_low) = (one, two)
    place = lax.axis_index("dp")
    core, side = (place % 2, place // 2)
    got_one = lax.ppermute(one_low, "dp", [(1, 0), (3, 2)])
    got_two = lax.ppermute(two_low, "dp", [(0, 1), (2, 3)])
    mine = jnp.where(core == 0, one + got_one.astype(F32), two + got_two.astype(F32))
    half = mine.shape[0] // 2
    away = lax.dynamic_slice_in_dim(mine, (1 - side) * half, half, 0).astype(BF16)
    kept = lax.dynamic_slice_in_dim(mine, side * half, half, 0)
    tiles = lax.axis_size("lon") * lax.axis_size("lat")
    part = (kept + beside(away).astype(F32)).astype(BF16).reshape(tiles, half // tiles, LANES)
    part = lax.all_to_all(part, ("lon", "lat"), 0, 0)
    total = jnp.sum(part.astype(F32), 0).astype(BF16)
    part = lax.all_to_all(jnp.broadcast_to(total[None], part.shape), ("lon", "lat"), 0, 0)
    part = part.reshape(half, LANES)
    other = beside(part)
    return (part, other, paired(part), paired(other))


def per_device(fields, weight_one, weight_two, edge_flips, cotangent):
    chans = fields.shape[1]
    tile = struct(chans, ROWS, LANES)
    flat = struct(chans, CELLS)
    pads = struct(3, chans, PADDED)
    scratch = [pltpu.VMEM((3, chans, PADDED), BF16)]
    field, cot, *rim = call(
        prepare_kernel,
        "prepare",
        (flat, flat) + rim_shapes(chans),
        (edge_flips, fields.reshape(tile.shape), cotangent.reshape(tile.shape)),
    )
    halo = exchange(rim)
    act, back, pads_in, *rim = call(
        hidden_kernel,
        "hidden",
        (flat, flat, pads) + rim_shapes(chans),
        (edge_flips, field, cot, weight_one, weight_two) + halo,
        scratch,
    )
    halo = exchange(rim)
    local = (struct(18 * chans, LANES, dtype=F32), struct(18 * chans, LANES))
    local_one = call(grad_kernel, "grad_one", local, (back, pads_in), flags=False)
    pads_act, *local_two = call(
        grad_two_kernel, "grad_two", (pads,) + local, (edge_flips, act, cot) + halo
    )
    quarters = reduce_grads(local_one, local_two)
    output, grad_fields = call(
        result_kernel,
        "result",
        (tile, tile),
        (edge_flips, field, cot, back, weight_one, weight_two, pads_act) + halo,
        scratch,
    )
    grad = struct(9, chans, chans, dtype=F32)
    grad_one, grad_two = call(finish_kernel, "finish", (grad, grad), quarters, flags=False)
    return (output.reshape(fields.shape), grad_fields.reshape(fields.shape), grad_one, grad_two)


def solution(mesh):
    in_specs = (P("dp", None, "lat", "lon"), P(), P(), P(), P("dp", None, "lat", "lon"))
    out_specs = (P("dp", None, "lat", "lon"), P("dp", None, "lat", "lon"), P(), P())
    return jax.shard_map(
        per_device, mesh=mesh, in_specs=in_specs, out_specs=out_specs, check_vma=False
    )
```

time: 219 us -> 179 us (0.82)
  starting transfers between devices: 66.5 us -> 40.5 us
  Pallas kernels: 26.2 us -> 38.7 us
  other arithmetic: 14.2 us -> 3.38 us
  local copies, waits for them, and re-layouts: 14 us -> 5.6 us
  waiting for transfers between devices: 37.9 us -> 30.7 us
    ppermute x13 -> x6, starting transfers between devices: 46.7 us -> 20 us  [the longest x2 10.2 us: paired(): return lax.ppermute(value, 'dp', [(0, 1), (1, 0), (2, 3), (3, 2)])]
    ppermute x13 -> x6, waiting for transfers between devices: 37.9 us -> 21.9 us  [the longest x2 18.5 us: beside(): return lax.ppermute(value, 'dp', [(i, (i + 2) % 4) for i in range(4)])]
    pallas_call x5 -> x8, Pallas kernels: 26.2 us -> 38.7 us  [call(): pl.pallas_call(kernel, name=name, out_shape=out_shape, in_specs=([SMEM] i...]
    convert_element_type x3 -> x1, other arithmetic: 7.2 us -> 0.12 us  [reduce_grads(): (kept + beside(away).astype(F32)).astype(BF16)]
    ppermute x4, waiting for transfers between devices: 0.01 us -> 6.22 us  [across(): lax.ppermute(value, 'lat', [(i, i + step) for i in range(lats) if 0 <= i...]
    another operation x2 -> x0, local copies, waits for them, and re-layouts: 4.37 us -> none  [the longest x1 4.37 us: edge_flags(): jnp.stack([near[0, 1], near[1, 1], near[0, 0], near[0, 2], near[1, 0], ne...]
    ppermute x4, starting transfers between devices: 5.95 us -> 9.31 us  [along(): lax.ppermute(value, 'lon', [(i, (i + step) % lons) for i in range(lons)])]
    reshape x2 -> x0, other arithmetic: 3.26 us -> none  [reduce_grads(): return (out_one.reshape(9, chans, chans), out_two.reshape(9, chans, chans))]
  transfers between devices with their start and end apart: 21 -> 14, of which waited for: 6 -> 7; matrix products, arithmetic and copies ran while one was open for 4% -> 0% of each run, Pallas kernels for 7% -> 11%
where the time goes in v2:
time: 179 us
  blocking collectives  58.9 us (33%)
  starting transfers between devices  40.5 us (23%)
  Pallas kernels  38.7 us (22%)
  waiting for transfers between devices  30.7 us (17%)
  local copies, waits for them, and re-layouts  5.6 us (3%)
  other arithmetic  3.38 us (2%)
    pallas_call x8, Pallas kernels, call(): pl.pallas_call(kernel, name=name, out_shape=out_shape, in_specs=([SMEM] i...  38.7 us
    all_to_all x1, blocking collectives, reduce_grads(): part = lax.all_to_all(part, ('lon', 'lat'), 0, 0)  32.9 us
    all_to_all x1, blocking collectives, reduce_grads(): lax.all_to_all(jnp.broadcast_to(total[None], part.shape), ('lon', 'lat'),...  26.1 us
    ppermute x2, waiting for transfers between devices, beside(): return lax.ppermute(value, 'dp', [(i, (i + 2) % 4) for i in range(4)])  18.5 us
    ppermute x4, starting transfers between devices, across(): lax.ppermute(value, 'lat', [(i, i + step) for i in range(lats) if 0 <= i...  11.2 us
    ppermute x2, starting transfers between devices, paired(): return lax.ppermute(value, 'dp', [(0, 1), (1, 0), (2, 3), (3, 2)])  10.2 us
    ppermute x4, starting transfers between devices, along(): lax.ppermute(value, 'lon', [(i, (i + step) % lons) for i in range(lons)])  9.31 us
    ppermute x1, starting transfers between devices, reduce_grads(): got_one = lax.ppermute(one_low, 'dp', [(1, 0), (3, 2)])  6.37 us
  transfers between devices with their start and end apart: 14, of which 7 were waited for; matrix products, arithmetic and copies ran while one was open for 0% of the time, Pallas kernels for 11%

profile of v2, /device:TPU:1, one launch (start us, length us, event | category | flops | bytes accessed | tf_op | source)
XLA Modules:
  0.0 178.6 jit_solution(13070054286758222354)
XLA Ops:
  0.6 3.8 %prepare.1 = (bf16[256,1024]{1,0:T(8,128)(2,1)}, bf16[256,1024]{1,0:T(8,128)(2,1)}, bf16[32,256]{1,0:T(8,128)(2,1)}, bf16[32,256]{1,0:T(8,128)(2,1)}, bf16[512,1...) custom-call(s32[7,8]{1,0:T(8,128)} %flips.7, bf16[256,8,128]{2,1,0:T(8,128)(2,1)} %bitcast.4, bf16[256,8,128]{2,1,0:T(8,128)(2,1)} %bitcast.5), custom_call_target="tpu_custom_call" | custom-call | tf_op jit(solution)/shard_map/prepare/pallas_call | solution.py:273
  4.4 2.5 %collective-permute-start = (bf16[32,256]{1,0:T(8,128)(2,1)}, bf16[32,256]{1,0:T(8,128)(2,1)S(1)}, u32[]{:S(2)}, u32[]{:S(2)}) collective-permute-start(bf16[32,256]{1,0:T(8,128)(2,1)} %get-tuple-element.32), channel_id=1, source_target_pairs={{0,32},{32,64},{64,96},{96,128},{128,160},{160,192},{192,224},{224... | collective-permute-start | bytes 49160 | tf_op jit(solution)/shard_map/ppermute | solution.py:299
  6.9 4.0 %collective-permute-start.1 = (bf16[32,256]{1,0:T(8,128)(2,1)}, bf16[32,256]{1,0:T(8,128)(2,1)S(1)}, u32[]{:S(2)}, u32[]{:S(2)}) collective-permute-start(bf16[32,256]{1,0:T(8,128)(2,1)} %get-tuple-element.33), channel_id=1, source_target_pairs={{0,224},{32,0},{64,32},{96,64},{128,96},{160,128},{192,160},{224,1... | collective-permute-start | bytes 49160 | tf_op jit(solution)/shard_map/ppermute | solution.py:299
  10.9 1.3 collective-permute-done.from_w.refs_0_
  12.7 1.7 join.2
  14.4 4.8 %collective-permute-start.2 = (bf16[544,128]{1,0:T(8,128)(2,1)}, bf16[544,128]{1,0:T(8,128)(2,1)S(1)}, u32[]{:S(2)}, u32[]{:S(2)}) collective-permute-start(bf16[544,128]{1,0:T(8,128)(2,1)} %get-tuple-element.36), channel_id=1, source_target_pairs={{0,4},{4,8},{8,12},{12,16},{16,20},{20,24},{24,28},{1,5},{5,9},{9,... | collective-permute-start | bytes 417800 | tf_op jit(solution)/shard_map/ppermute | solution.py:302
  19.2 1.3 collective-permute-start.3
  20.6 1.0 collective-permute-done.2.refs_2_
  21.6 5.2 %collective-permute-done.3.refs_3_ = bf16[544,128]{1,0:T(8,128)(2,1)S(1)} collective-permute-done((bf16[544,128]{1,0:T(8,128)(2,1)}, bf16[544,128]{1,0:T(8,128)(2,1)S(1)}, u32[]{:S(2)}, u32[]{:S(2)}) %collective-permute-start.3) | collective-permute-done | bytes 139296 | tf_op jit(solution)/shard_map/ppermute | solution.py:302
  27.4 7.6 %hidden.1 = (bf16[256,1024]{1,0:T(8,128)(2,1)}, bf16[256,1024]{1,0:T(8,128)(2,1)}, bf16[3,256,1280]{2,1,0:T(8,128)(2,1)}, bf16[32,256]{1,0:T(8,128)(2,1)}, bf16[...) custom-call(s32[7,8]{1,0:T(8,128)} %flips.7, bf16[256,1024]{1,0:T(8,128)(2,1)} %get-tuple-element.30.field, ...), custom_call_target="tpu_custom_call" | custom-call | tf_op jit(solution)/shard_map/hidden/pallas_call | solution.py:273
  35.1 2.8 %collective-permute-start.5 = (bf16[32,256]{1,0:T(8,128)(2,1)}, bf16[32,256]{1,0:T(8,128)(2,1)S(1)}, u32[]{:S(2)}, u32[]{:S(2)}) collective-permute-start(bf16[32,256]{1,0:T(8,128)(2,1)} %get-tuple-element.41), channel_id=1, source_target_pairs={{0,224},{32,0},{64,32},{96,64},{128,96},{160,128},{192,160},{224,1... | collective-permute-start | bytes 49160 | tf_op jit(solution)/shard_map/ppermute | solution.py:299
  37.9 1.3 collective-permute-done.4.from_w.refs_0_
  39.8 1.7 join.3
  41.4 3.8 %collective-permute-start.6 = (bf16[544,128]{1,0:T(8,128)(2,1)}, bf16[544,128]{1,0:T(8,128)(2,1)S(1)}, u32[]{:S(2)}, u32[]{:S(2)}) collective-permute-start(bf16[544,128]{1,0:T(8,128)(2,1)} %get-tuple-element.44), channel_id=1, source_target_pairs={{0,4},{4,8},{8,12},{12,16},{16,20},{20,24},{24,28},{1,5},{5,9},{9,... | collective-permute-start | bytes 417800 | tf_op jit(solution)/shard_map/ppermute | solution.py:302
  45.2 1.3 collective-permute-start.7
  46.5 4.9 %grad_one.1 = (f32[4608,128]{1,0:T(8,128)}, bf16[4608,128]{1,0:T(8,128)(2,1)}) custom-call(bf16[256,1024]{1,0:T(8,128)(2,1)} %get-tuple-element.38.back.grad_tile, bf16[3,256,1280]{2,1,0:T(8,128)(2,1)} %get-tuple-element.49.pads), custom_call_target="tpu_custom_call" | custom-call | tf_op jit(solution)/shard_map/grad_one/pallas_call | solution.py:273
  51.5 6.4 %collective-permute-start.8 = (bf16[4608,128]{1,0:T(8,128)(2,1)}, bf16[4608,128]{1,0:T(8,128)(2,1)S(1)}, u32[]{:S(2)}, u32[]{:S(2)}) collective-permute-start(bf16[4608,128]{1,0:T(8,128)(2,1)} %get-tuple-element.51), channel_id=1, source_target_pairs={{1,0},{3,2},{5,4},{7,6},{9,8},{11,10},{13,12},{15,14},{17,16},{19,... | collective-permute-start | bytes 3538952 | tf_op jit(solution)/shard_map/ppermute | solution.py:324
  58.6 5.0 %grad_two.1 = (bf16[3,256,1280]{2,1,0:T(8,128)(2,1)}, f32[4608,128]{1,0:T(8,128)}, bf16[4608,128]{1,0:T(8,128)(2,1)}) custom-call(s32[7,8]{1,0:T(8,128)} %flips.7, bf16[256,1024]{1,0:T(8,128)(2,1)} %get-tuple-element.39.act, bf16[256,1024]{1,0:T(8,128)(2,1)} %get-tuple-element.31.cotangent, bf16[32,256]{1,0:T(8,128)(2,1)} %copy-done.7, ...), custom_call_target="tpu_custom_call" | custom-call | tf_op jit(solution)/shard_map/grad_two/pallas_call | solution.py:273
  63.5 1.5 collective-permute-start.9
  65.0 3.4 %collective-permute-done.9 = bf16[4608,128]{1,0:T(8,128)(2,1)S(1)} collective-permute-done((bf16[4608,128]{1,0:T(8,128)(2,1)}, bf16[4608,128]{1,0:T(8,128)(2,1)S(1)}, u32[]{:S(2)}, u32[]{:S(2)}) %collective-permute-start.9) | collective-permute-done | bytes 1179680 | tf_op jit(solution)/shard_map/ppermute | solution.py:325
  68.5 1.0 copy-done.1
  69.5 3.1 %add_select_fusion = f32[4608,128]{1,0:T(8,128)S(1)} fusion(f32[4608,128]{1,0:T(8,128)} %get-tuple-element.52, bf16[4608,128]{1,0:T(8,128)(2,1)} %copy-done.1, f32[4608,128]{1,0:T(8,128)} %get-tuple-element.50, bf16[4608,128]{1,0:T(8,128)(2,1)S(1)} %collective-permute-done.8, pred[]{:T(512)S(6)} %eq.5), kind=kLoop, calls=%fused_computation | loop fusion | flops 2949120 | bytes 9437185 | tf_op jit(solution)/shard_map/jit(_where)/select_n | solution.py:326
  72.7 1.4 collective-permute-start.10
  74.1 13.4 %collective-permute-done.10 = bf16[2304,128]{1,0:T(8,128)(2,1)S(1)} collective-permute-done((bf16[2304,128]{1,0:T(8,128)(2,1)S(1)}, bf16[2304,128]{1,0:T(8,128)(2,1)S(1)}, u32[]{:S(2)}, u32[]{:S(2)}) %collective-permute-start.10) | collective-permute-done | bytes 589856 | tf_op jit(solution)/shard_map/ppermute | solution.py:313
  87.8 32.9 %all_to_all.10 = bf16[64,36,128]{2,1,0:T(8,128)(2,1)S(1)} all-to-all(bf16[64,36,128]{2,1,0:T(8,128)(2,1)S(1)} %reshape.31), channel_id=1, replica_groups=mesh['lon'=8,'lat'=8,'dp'=4] {'lon','lat'}, dimensions={0} | all-to-all | bytes 1179648 | tf_op jit(solution)/shard_map/all_to_all | solution.py:332
  120.9 26.1 %all_to_all.11 = bf16[64,36,128]{2,1,0:T(8,128)(2,1)S(1)} all-to-all(bf16[64,36,128]{2,1,0:T(8,128)(2,1)S(1)} %broadcast_in_dim.2), channel_id=1, replica_groups=mesh['lon'=8,'lat'=8,'dp'=4] {'lon','lat'}, dimensions={0} | all-to-all | bytes 1179648 | tf_op jit(solution)/shard_map/all_to_all | solution.py:334
  147.7 4.8 %collective-permute-start.12 = (bf16[2304,128]{1,0:T(8,128)(2,1)S(1)}, bf16[2304,128]{1,0:T(8,128)(2,1)S(1)}, u32[]{:S(2)}, u32[]{:S(2)}) collective-permute-start(bf16[2304,128]{1,0:T(8,128)(2,1)S(1)} %reshape.32.mine), channel_id=1, source_target_pairs={{0,1},{1,0},{2,3},{3,2},{4,5},{5,4},{6,7},{7,6},{8,9},{9,8},{10,11... | collective-permute-start | bytes 1769480 | tf_op jit(solution)/shard_map/ppermute | solution.py:317
  152.5 5.0 %collective-permute-done.11.beside = bf16[2304,128]{1,0:T(8,128)(2,1)S(1)} collective-permute-done((bf16[2304,128]{1,0:T(8,128)(2,1)S(1)}, bf16[2304,128]{1,0:T(8,128)(2,1)S(1)}, u32[]{:S(2)}, u32[]{:S(2)}) %collective-permute-start.11) | collective-permute-done | bytes 589856 | tf_op jit(solution)/shard_map/ppermute | solution.py:313
  157.5 5.4 %collective-permute-start.13 = (bf16[2304,128]{1,0:T(8,128)(2,1)S(1)}, bf16[2304,128]{1,0:T(8,128)(2,1)S(1)}, u32[]{:S(2)}, u32[]{:S(2)}) collective-permute-start(bf16[2304,128]{1,0:T(8,128)(2,1)S(1)} %collective-permute-done.11.beside), channel_id=1, source_target_pairs={{0,1},{1,0},{2,3},{3,2},{4,5},{5,4},{6,7},{7,6},{8,9},{9,8},{10,11... | collective-permute-start | bytes 1769480 | tf_op jit(solution)/shard_map/ppermute | solution.py:317
  162.9 9.6 %result.1 = (bf16[256,8,128]{2,1,0:T(8,128)(2,1)}, bf16[256,8,128]{2,1,0:T(8,128)(2,1)}) custom-call(s32[7,8]{1,0:T(8,128)} %flips.7, bf16[256,1024]{1,0:T(8,128)(2,1)} %get-tuple-element.30.field, bf16[256,1024]{1,0:T(8,128)(2,1)} %get-tuple-element.31.cotangent, bf16[256,1024]{1,0:T(8,128)(2,1)} %get-tuple-element.38.back.grad_tile, ...), custom_call_target="tpu_custom_call" | custom-call | tf_op jit(solution)/shard_map/result/pallas_call | solution.py:273
  173.4 0.8 copy-done.4
  174.2 4.5 %finish.1 = (f32[9,256,256]{2,1,0:T(8,128)}, f32[9,256,256]{2,1,0:T(8,128)}) custom-call(bf16[2304,128]{1,0:T(8,128)(2,1)} %copy-done, bf16[2304,128]{1,0:T(8,128)(2,1)} %copy-done.2, bf16[2304,128]{1,0:T(8,128)(2,1)} %copy-done.3, bf16[2304,128]{1,0:T(8,128)(2,1)} %copy-done.4), custom_call_target="tpu_custom_call" | custom-call | tf_op jit(solution)/shard_map/finish/pallas_call | solution.py:273
  (39 shorter events, 4.6 us)
Async XLA Ops:
  4.4 7.7 %collective-permute-start = (bf16[32,256]{1,0:T(8,128)(2,1)}, bf16[32,256]{1,0:T(8,128)(2,1)S(1)}, u32[]{:S(2)}, u32[]{:S(2)}) collective-permute-start(bf16[32,256]{1,0:T(8,128)(2,1)} %get-tuple-element.32), channel_id=1, source_target_pairs={{0,32},{32,64},{64,96},{96,128},{128,160},{160,192},{192,224},{224... | collective-permute-start | bytes 49160 | tf_op jit(solution)/shard_map/ppermute | solution.py:299
  6.9 5.3 %collective-permute-start.1 = (bf16[32,256]{1,0:T(8,128)(2,1)}, bf16[32,256]{1,0:T(8,128)(2,1)S(1)}, u32[]{:S(2)}, u32[]{:S(2)}) collective-permute-start(bf16[32,256]{1,0:T(8,128)(2,1)} %get-tuple-element.33), channel_id=1, source_target_pairs={{0,224},{32,0},{64,32},{96,64},{128,96},{160,128},{192,160},{224,1... | collective-permute-start | bytes 49160 | tf_op jit(solution)/shard_map/ppermute | solution.py:299
  12.1 0.6 copy-start.11
  12.1 0.6 copy-start.12
  14.4 7.1 %collective-permute-start.2 = (bf16[544,128]{1,0:T(8,128)(2,1)}, bf16[544,128]{1,0:T(8,128)(2,1)S(1)}, u32[]{:S(2)}, u32[]{:S(2)}) collective-permute-start(bf16[544,128]{1,0:T(8,128)(2,1)} %get-tuple-element.36), channel_id=1, source_target_pairs={{0,4},{4,8},{8,12},{12,16},{16,20},{20,24},{24,28},{1,5},{5,9},{9,... | collective-permute-start | bytes 417800 | tf_op jit(solution)/shard_map/ppermute | solution.py:302
  19.2 7.5 %collective-permute-start.3 = (bf16[544,128]{1,0:T(8,128)(2,1)}, bf16[544,128]{1,0:T(8,128)(2,1)S(1)}, u32[]{:S(2)}, u32[]{:S(2)}) collective-permute-start(bf16[544,128]{1,0:T(8,128)(2,1)} %get-tuple-element.37), channel_id=1, source_target_pairs={{4,0},{8,4},{12,8},{16,12},{20,16},{24,20},{28,24},{5,1},{9,5},{13... | collective-permute-start | bytes 417800 | tf_op jit(solution)/shard_map/ppermute | solution.py:302
  21.6 5.2 %copy-start.9 = (bf16[544,128]{1,0:T(8,128)(2,1)}, bf16[544,128]{1,0:T(8,128)(2,1)S(1)}, u32[]{:S(2)}) copy-start(bf16[544,128]{1,0:T(8,128)(2,1)S(1)} %collective-permute-done.2.refs_2_) | copy-start | bytes 417796
  26.8 0.7 copy-start.10
  35.1 4.1 %collective-permute-start.4 = (bf16[32,256]{1,0:T(8,128)(2,1)}, bf16[32,256]{1,0:T(8,128)(2,1)S(1)}, u32[]{:S(2)}, u32[]{:S(2)}) collective-permute-start(bf16[32,256]{1,0:T(8,128)(2,1)} %get-tuple-element.40), channel_id=1, source_target_pairs={{0,32},{32,64},{64,96},{96,128},{128,160},{160,192},{192,224},{224... | collective-permute-start | bytes 49160 | tf_op jit(solution)/shard_map/ppermute | solution.py:299
  35.1 4.1 %collective-permute-start.5 = (bf16[32,256]{1,0:T(8,128)(2,1)}, bf16[32,256]{1,0:T(8,128)(2,1)S(1)}, u32[]{:S(2)}, u32[]{:S(2)}) collective-permute-start(bf16[32,256]{1,0:T(8,128)(2,1)} %get-tuple-element.41), channel_id=1, source_target_pairs={{0,224},{32,0},{64,32},{96,64},{128,96},{160,128},{192,160},{224,1... | collective-permute-start | bytes 49160 | tf_op jit(solution)/shard_map/ppermute | solution.py:299
  39.1 0.6 copy-start.7
  39.2 0.6 copy-start.8
  41.4 16.4 %collective-permute-start.6 = (bf16[544,128]{1,0:T(8,128)(2,1)}, bf16[544,128]{1,0:T(8,128)(2,1)S(1)}, u32[]{:S(2)}, u32[]{:S(2)}) collective-permute-start(bf16[544,128]{1,0:T(8,128)(2,1)} %get-tuple-element.44), channel_id=1, source_target_pairs={{0,4},{4,8},{8,12},{12,16},{16,20},{20,24},{24,28},{1,5},{5,9},{9,... | collective-permute-start | bytes 417800 | tf_op jit(solution)/shard_map/ppermute | solution.py:302
  45.2 12.6 %collective-permute-start.7 = (bf16[544,128]{1,0:T(8,128)(2,1)}, bf16[544,128]{1,0:T(8,128)(2,1)S(1)}, u32[]{:S(2)}, u32[]{:S(2)}) collective-permute-start(bf16[544,128]{1,0:T(8,128)(2,1)} %get-tuple-element.45), channel_id=1, source_target_pairs={{4,0},{8,4},{12,8},{16,12},{20,16},{24,20},{28,24},{5,1},{9,5},{13... | collective-permute-start | bytes 417800 | tf_op jit(solution)/shard_map/ppermute | solution.py:302
  51.5 13.6 %collective-permute-start.8 = (bf16[4608,128]{1,0:T(8,128)(2,1)}, bf16[4608,128]{1,0:T(8,128)(2,1)S(1)}, u32[]{:S(2)}, u32[]{:S(2)}) collective-permute-start(bf16[4608,128]{1,0:T(8,128)(2,1)} %get-tuple-element.51), channel_id=1, source_target_pairs={{1,0},{3,2},{5,4},{7,6},{9,8},{11,10},{13,12},{15,14},{17,16},{19,... | collective-permute-start | bytes 3538952 | tf_op jit(solution)/shard_map/ppermute | solution.py:324
  57.9 0.7 copy-start.5
  57.9 0.7 copy-start.6
  63.5 4.9 %collective-permute-start.9 = (bf16[4608,128]{1,0:T(8,128)(2,1)}, bf16[4608,128]{1,0:T(8,128)(2,1)S(1)}, u32[]{:S(2)}, u32[]{:S(2)}) collective-permute-start(bf16[4608,128]{1,0:T(8,128)(2,1)} %get-tuple-element.53), channel_id=1, source_target_pairs={{0,1},{2,3},{4,5},{6,7},{8,9},{10,11},{12,13},{14,15},{16,17},{18,... | collective-permute-start | bytes 3538952 | tf_op jit(solution)/shard_map/ppermute | solution.py:325
  68.5 1.0 copy-start.1
  72.7 14.8 %collective-permute-start.10 = (bf16[2304,128]{1,0:T(8,128)(2,1)S(1)}, bf16[2304,128]{1,0:T(8,128)(2,1)S(1)}, u32[]{:S(2)}, u32[]{:S(2)}) collective-permute-start(bf16[2304,128]{1,0:T(8,128)(2,1)S(1)} %dynamic-slice_convert_fusion), channel_id=1, source_target_pairs={{0,2},{1,3},{2,0},{3,1},{4,6},{5,7},{6,4},{7,5},{8,10},{9,11},{10,... | collective-permute-start | bytes 1769480 | tf_op jit(solution)/shard_map/ppermute | solution.py:313
  147.1 25.4 %copy-start = (bf16[2304,128]{1,0:T(8,128)(2,1)}, bf16[2304,128]{1,0:T(8,128)(2,1)S(1)}, u32[]{:S(2)}) copy-start(bf16[2304,128]{1,0:T(8,128)(2,1)S(1)} %reshape.32.mine) | copy-start | bytes 1769476
  147.1 10.4 %collective-permute-start.11 = (bf16[2304,128]{1,0:T(8,128)(2,1)S(1)}, bf16[2304,128]{1,0:T(8,128)(2,1)S(1)}, u32[]{:S(2)}, u32[]{:S(2)}) collective-permute-start(bf16[2304,128]{1,0:T(8,128)(2,1)S(1)} %reshape.32.mine), channel_id=1, source_target_pairs={{0,2},{1,3},{2,0},{3,1},{4,6},{5,7},{6,4},{7,5},{8,10},{9,11},{10,... | collective-permute-start | bytes 1769480 | tf_op jit(solution)/shard_map/ppermute | solution.py:313
  147.7 24.8 %collective-permute-start.12 = (bf16[2304,128]{1,0:T(8,128)(2,1)S(1)}, bf16[2304,128]{1,0:T(8,128)(2,1)S(1)}, u32[]{:S(2)}, u32[]{:S(2)}) collective-permute-start(bf16[2304,128]{1,0:T(8,128)(2,1)S(1)} %reshape.32.mine), channel_id=1, source_target_pairs={{0,1},{1,0},{2,3},{3,2},{4,5},{5,4},{6,7},{7,6},{8,9},{9,8},{10,11... | collective-permute-start | bytes 1769480 | tf_op jit(solution)/shard_map/ppermute | solution.py:317
  157.5 15.0 %copy-start.2 = (bf16[2304,128]{1,0:T(8,128)(2,1)}, bf16[2304,128]{1,0:T(8,128)(2,1)S(1)}, u32[]{:S(2)}) copy-start(bf16[2304,128]{1,0:T(8,128)(2,1)S(1)} %collective-permute-done.11.beside) | copy-start | bytes 1769476
  157.5 15.0 %collective-permute-start.13 = (bf16[2304,128]{1,0:T(8,128)(2,1)S(1)}, bf16[2304,128]{1,0:T(8,128)(2,1)S(1)}, u32[]{:S(2)}, u32[]{:S(2)}) collective-permute-start(bf16[2304,128]{1,0:T(8,128)(2,1)S(1)} %collective-permute-done.11.beside), channel_id=1, source_target_pairs={{0,1},{1,0},{2,3},{3,2},{4,5},{5,4},{6,7},{7,6},{8,9},{9,8},{10,11... | collective-permute-start | bytes 1769480 | tf_op jit(solution)/shard_map/ppermute | solution.py:317
  172.5 0.8 copy-start.3
  173.3 0.8 copy-start.4

commit v3 on v2

--- a/solution.py
+++ b/solution.py
@@ -4,6 +4,7 @@
 from jax.experimental import pallas as pl
 from jax.experimental.pallas import tpu as pltpu
 from jax.sharding import PartitionSpec as P
+
 
 F32 = jnp.float32
 BF16 = jnp.bfloat16
@@ -216,18 +217,33 @@
     rims(act_out[...], back_out[...], flags, outs[3:])
 
 
-def grad_kernel(grad_tile, pads, out, out_low):
+def grad_kernel(grad_tile, pads, keep, away):
+    core = lax.rem(lax.axis_index("dp"), 2)
     for tap in range(9):
         r, s = divmod(tap, 3)
         term = lax.dot_general(
             grad_tile[...], pads[s, :, r * LANES : r * LANES + CELLS], NT, preferred_element_type=F32
         )
-        chans = term.shape[0]
         for part in range(2):
-            rows = slice((2 * tap + part) * chans, (2 * tap + part + 1) * chans)
-            piece = term[:, part * LANES : (part + 1) * LANES]
-            out[rows] = piece
-            out_low[rows] = piece.astype(BF16)
+            half, group = divmod(2 * tap + part, 9)
+            sides, tiles, rows, lanes = keep.shape
+            shape = (sides, tiles, rows // 9, lanes)
+            piece = term[:, part * LANES : (part + 1) * LANES].reshape(shape)
+            span = slice(group * shape[2], (group + 1) * shape[2])
+
+            @pl.when(core == half)
+            def _():
+                keep[:, :, span, :] = piece
+
+            @pl.when(core != half)
+            def _():
+                away[:, :, span, :] = piece.astype(BF16)
+
+
+def fold_kernel(keep, got, kept, away):
+    side = lax.div(lax.axis_index("dp"), 2)
+    kept[...] = keep[side] + got[side].astype(F32)
+    away[...] = (keep[1 - side] + got[1 - side].astype(F32)).astype(BF16)
 
 
 def grad_two_kernel(flips, act, cotangent, *refs):
@@ -251,28 +267,32 @@
 def finish_kernel(mine, beside, paired, across, out_one, out_two):
     place = lax.axis_index("dp")
     core, side = (lax.rem(place, 2) == 1, place >= 2)
-    chans = out_one.shape[1]
-    for group in range(mine.shape[0] // chans):
-        rows = slice(group * chans, (group + 1) * chans)
-        a, b, c, d = (ref[rows].astype(F32) for ref in (mine, beside, paired, across))
-        near, far = (jnp.where(core, c, a), jnp.where(core, d, b))
-        low_one, high_one = (jnp.where(side, far, near), jnp.where(side, near, far))
-        near, far = (jnp.where(core, a, c), jnp.where(core, b, d))
-        low_two, high_two = (jnp.where(side, far, near), jnp.where(side, near, far))
-        for out, pieces in ((out_one, (low_one, high_one)), (out_two, (low_two, high_two))):
-            for half, piece in enumerate(pieces):
+    rows = out_one.shape[1] // 2
+    _, depth = mine.shape[:2]
+    thick = depth // 18
+    for which, out in enumerate((out_one, out_two)):
+        for group in range(9):
+            start = (which * 9 + group) * thick
+            a, b, c, d = (
+                ref[:, start : start + thick, :].astype(F32).reshape(rows, LANES)
+                for ref in (mine, beside, paired, across)
+            )
+            for half in range(2):
                 tap, part = divmod(group + half * 9, 2)
-                out[tap, :, part * LANES : (part + 1) * LANES] = piece
+                other = core if half == 0 else jnp.logical_not(core)
+                near, far = (jnp.where(other, c, a), jnp.where(other, d, b))
+                lanes = slice(part * LANES, (part + 1) * LANES)
+                out[tap, :rows, lanes] = jnp.where(side, far, near)
+                out[tap, rows:, lanes] = jnp.where(side, near, far)
 
 
 SMEM = pl.BlockSpec(memory_space=pltpu.SMEM)
 VMEM = pl.BlockSpec(memory_space=pltpu.VMEM)
 
 
-def call(kernel, name, out_shape, args, scratch=(), flags=True):
+def call(kernel, out_shape, args, scratch=(), flags=True):
     return pl.pallas_call(
         kernel,
-        name=name,
         out_shape=out_shape,
         in_specs=([SMEM] if flags else []) + [VMEM] * (len(args) - (1 if flags else 0)),
         out_specs=jax.tree.map(lambda _: VMEM, out_shape),
@@ -305,8 +325,10 @@
 
     from_w, from_e = (along(east, 1), along(west, -1))
     line = struct(south.shape[0] + 32, LANES)
-    south, north = call(join_kernel, "join", (line, line), (south, north, from_w, from_e), flags=False)
-    return (from_w, from_e, across(south, 1), across(north, -1))
+    south, north = call(join_kernel, (line, line), (south, north, from_w, from_e), flags=False)
+    from_n = across(south, 1)
+    from_s = across(north, -1)
+    return (from_w, from_e, from_n, from_s)
 
 
 def beside(value):
@@ -317,24 +339,35 @@
     return lax.ppermute(value, "dp", [(0, 1), (1, 0), (2, 3), (3, 2)])
 
 
+def over(value, axis):
+    return lax.all_to_all(value, axis, 0, 0)
+
+
+def total(parts):
+    return jnp.sum(parts.astype(F32), 0)
+
+
+def fold(grad):
+    keep, away = grad
+    shape = keep.shape[1:]
+    return call(fold_kernel, (struct(*shape, dtype=F32), struct(*shape)), (keep, paired(away)), flags=False)
+
+
+def lat_sum(kept, away):
+    got = beside(away)
+    return total(over((kept + got.astype(F32)).astype(BF16), "lat"))
+
+
+def gathered(value, axis):
+    return over(jnp.broadcast_to(value[None], (lax.axis_size(axis),) + value.shape), axis)
+
+
 def reduce_grads(one, two):
-    (one, one_low), (two, two_low) = (one, two)
-    place = lax.axis_index("dp")
-    core, side = (place % 2, place // 2)
-    got_one = lax.ppermute(one_low, "dp", [(1, 0), (3, 2)])
-    got_two = lax.ppermute(two_low, "dp", [(0, 1), (2, 3)])
-    mine = jnp.where(core == 0, one + got_one.astype(F32), two + got_two.astype(F32))
-    half = mine.shape[0] // 2
-    away = lax.dynamic_slice_in_dim(mine, (1 - side) * half, half, 0).astype(BF16)
-    kept = lax.dynamic_slice_in_dim(mine, side * half, half, 0)
-    tiles = lax.axis_size("lon") * lax.axis_size("lat")
-    part = (kept + beside(away).astype(F32)).astype(BF16).reshape(tiles, half // tiles, LANES)
-    part = lax.all_to_all(part, ("lon", "lat"), 0, 0)
-    total = jnp.sum(part.astype(F32), 0).astype(BF16)
-    part = lax.all_to_all(jnp.broadcast_to(total[None], part.shape), ("lon", "lat"), 0, 0)
-    part = part.reshape(half, LANES)
-    other = beside(part)
-    return (part, other, paired(part), paired(other))
+    share = jnp.concatenate([lat_sum(*one), lat_sum(*two)], 0)
+    lons = lax.axis_size("lon")
+    share = total(over(share.reshape(lons, share.shape[0] // lons, LANES), "lon")).astype(BF16)
+    share = gathered(share, "lon")
+    return gathered(share.reshape(-1, LANES), "lat")
 
 
 def per_device(fields, weight_one, weight_two, edge_flips, cotangent):
@@ -345,40 +378,39 @@
     scratch = [pltpu.VMEM((3, chans, PADDED), BF16)]
     field, cot, *rim = call(
         prepare_kernel,
-        "prepare",
         (flat, flat) + rim_shapes(chans),
         (edge_flips, fields.reshape(tile.shape), cotangent.reshape(tile.shape)),
     )
     halo = exchange(rim)
     act, back, pads_in, *rim = call(
         hidden_kernel,
-        "hidden",
         (flat, flat, pads) + rim_shapes(chans),
         (edge_flips, field, cot, weight_one, weight_two) + halo,
         scratch,
     )
     halo = exchange(rim)
-    local = (struct(18 * chans, LANES, dtype=F32), struct(18 * chans, LANES))
-    local_one = call(grad_kernel, "grad_one", local, (back, pads_in), flags=False)
-    pads_act, *local_two = call(
-        grad_two_kernel, "grad_two", (pads,) + local, (edge_flips, act, cot) + halo
-    )
-    quarters = reduce_grads(local_one, local_two)
+    local = (2, lax.axis_size("lat"), 9 * chans // (2 * lax.axis_size("lat")), LANES)
+    local = (struct(*local, dtype=F32), struct(*local))
+    one = call(grad_kernel, local, (back, pads_in), flags=False)
+    one = fold(one)
+    act, _ = lax.optimization_barrier((act, one[0]))
+    pads_act, *two = call(grad_two_kernel, (pads,) + local, (edge_flips, act, cot) + halo)
+    quarter = reduce_grads(one, fold(two))
+    quarter, back = lax.optimization_barrier((quarter, back))
+    other = beside(quarter)
     output, grad_fields = call(
-        result_kernel,
-        "result",
-        (tile, tile),
-        (edge_flips, field, cot, back, weight_one, weight_two, pads_act) + halo,
-        scratch,
+        result_kernel, (tile, tile), (edge_flips, field, cot, back, weight_one, weight_two, pads_act) + halo, scratch
     )
     grad = struct(9, chans, chans, dtype=F32)
-    grad_one, grad_two = call(finish_kernel, "finish", (grad, grad), quarters, flags=False)
+    grad_one, grad_two = call(
+        finish_kernel, (grad, grad), (quarter, other, paired(quarter), paired(other)), flags=False
+    )
     return (output.reshape(fields.shape), grad_fields.reshape(fields.shape), grad_one, grad_two)
 
 
 def solution(mesh):
     in_specs = (P("dp", None, "lat", "lon"), P(), P(), P(), P("dp", None, "lat", "lon"))
     out_specs = (P("dp", None, "lat", "lon"), P("dp", None, "lat", "lon"), P(), P())
-    return jax.shard_map(
-        per_device, mesh=mesh, in_specs=in_specs, out_specs=out_specs, check_vma=False
-    )
+
+
+    return jax.shard_map(per_device, mesh=mesh, in_specs=in_specs, out_specs=out_specs, check_vma=False)

time: 179 us -> 178 us (level)
  blocking collectives: 58.9 us -> 36 us
  starting transfers between devices: 40.5 us -> 54.9 us
  Pallas kernels: 38.7 us -> 48.2 us
    all_to_all x2 -> x3, blocking collectives: 58.9 us -> 36 us  [over(): return lax.all_to_all(value, axis, 0, 0)]
    ppermute x2 -> x3, waiting for transfers between devices: 18.5 us -> 3.78 us  [beside(): return lax.ppermute(value, 'dp', [(i, (i + 2) % 4) for i in range(4)])]
    all_to_all x0 -> x2, waiting for transfers between devices: none -> 13.9 us  [over(): return lax.all_to_all(value, axis, 0, 0)]
    ppermute x2 -> x4, starting transfers between devices: 10.2 us -> 21.1 us  [paired(): return lax.ppermute(value, 'dp', [(0, 1), (1, 0), (2, 3), (3, 2)])]
    all_to_all x0 -> x2, starting transfers between devices: none -> 9.77 us  [over(): return lax.all_to_all(value, axis, 0, 0)]
    pallas_call x8 -> x10, Pallas kernels: 38.7 us -> 48.2 us  [call(): pl.pallas_call(kernel, out_shape=out_shape, in_specs=([SMEM] if flags els...]
    ppermute x2 -> x0, starting transfers between devices: 7.83 us -> none  [the longest x1 6.37 us: reduce_grads(): got_one = lax.ppermute(one_low, 'dp', [(1, 0), (3, 2)])]
    ppermute x2 -> x0, waiting for transfers between devices: 3.44 us -> none  [the longest x1 3.43 us: reduce_grads(): got_two = lax.ppermute(two_low, 'dp', [(0, 1), (2, 3)])]
  transfers between devices with their start and end apart: 14 -> 17, of which waited for: 7 -> 10; matrix products, arithmetic and copies ran while one was open for 0% -> 1% of each run, Pallas kernels for 11% -> 9%
where the time goes in v3:
time: 178 us; the launch traced here: 177 us
  starting transfers between devices  54.9 us (31%)
  Pallas kernels  48.2 us (27%)
  blocking collectives  36 us (20%)
  waiting for transfers between devices  29.8 us (17%)
  local copies, waits for them, and re-layouts  5.94 us (3%)
    pallas_call x10, Pallas kernels, call(): pl.pallas_call(kernel, out_shape=out_shape, in_specs=([SMEM] if flags els...  48.2 us
    all_to_all x3, blocking collectives, over(): return lax.all_to_all(value, axis, 0, 0)  36 us
    ppermute x4, starting transfers between devices, paired(): return lax.ppermute(value, 'dp', [(0, 1), (1, 0), (2, 3), (3, 2)])  21.1 us
    all_to_all x2, waiting for transfers between devices, over(): return lax.all_to_all(value, axis, 0, 0)  13.9 us
    ppermute x4, starting transfers between devices, across(): lax.ppermute(value, 'lat', [(i, i + step) for i in range(lats) if 0 <= i...  11.2 us
    all_to_all x2, starting transfers between devices, over(): return lax.all_to_all(value, axis, 0, 0)  9.77 us
    ppermute x4, starting transfers between devices, along(): lax.ppermute(value, 'lon', [(i, (i + step) % lons) for i in range(lons)])  9.55 us
    ppermute x4, waiting for transfers between devices, across(): lax.ppermute(value, 'lat', [(i, i + step) for i in range(lats) if 0 <= i...  9.18 us
  transfers between devices with their start and end apart: 17, of which 10 were waited for; matrix products, arithmetic and copies ran while one was open for 1% of the time, Pallas kernels for 9%

profile of v3, /device:TPU:1, one launch (start us, length us, event | category | flops | bytes accessed | tf_op | source)
XLA Modules:
  0.0 177.3 jit_solution(7798009169239809820)
XLA Ops:
  0.6 3.8 %shard_map.84 = (bf16[256,1024]{1,0:T(8,128)(2,1)}, bf16[256,1024]{1,0:T(8,128)(2,1)}, bf16[32,256]{1,0:T(8,128)(2,1)}, bf16[32,256]{1,0:T(8,128)(2,1)}, bf16[51...) custom-call(s32[7,8]{1,0:T(8,128)} %flips.7, bf16[256,8,128]{2,1,0:T(8,128)(2,1)} %bitcast.4, bf16[256,8,128]{2,1,0:T(8,128)(2,1)} %bitcast.5), custom_call_target="tpu_custom_call" | custom-call | tf_op jit(solution)/shard_map/pallas_call | solution.py:294
  4.4 2.5 %collective-permute-start = (bf16[32,256]{1,0:T(8,128)(2,1)}, bf16[32,256]{1,0:T(8,128)(2,1)S(1)}, u32[]{:S(2)}, u32[]{:S(2)}) collective-permute-start(bf16[32,256]{1,0:T(8,128)(2,1)} %get-tuple-element.39), channel_id=1, source_target_pairs={{0,32},{32,64},{64,96},{96,128},{128,160},{160,192},{192,224},{224... | collective-permute-start | bytes 49160 | tf_op jit(solution)/shard_map/ppermute | solution.py:319
  6.8 4.0 %collective-permute-start.1 = (bf16[32,256]{1,0:T(8,128)(2,1)}, bf16[32,256]{1,0:T(8,128)(2,1)S(1)}, u32[]{:S(2)}, u32[]{:S(2)}) collective-permute-start(bf16[32,256]{1,0:T(8,128)(2,1)} %get-tuple-element.40), channel_id=1, source_target_pairs={{0,224},{32,0},{64,32},{96,64},{128,96},{160,128},{192,160},{224,1... | collective-permute-start | bytes 49160 | tf_op jit(solution)/shard_map/ppermute | solution.py:319
  12.7 1.7 shard_map.85
  14.4 4.8 %collective-permute-start.2 = (bf16[544,128]{1,0:T(8,128)(2,1)}, bf16[544,128]{1,0:T(8,128)(2,1)S(1)}, u32[]{:S(2)}, u32[]{:S(2)}) collective-permute-start(bf16[544,128]{1,0:T(8,128)(2,1)} %get-tuple-element.43), channel_id=1, source_target_pairs={{0,4},{4,8},{8,12},{12,16},{16,20},{20,24},{24,28},{1,5},{5,9},{9,... | collective-permute-start | bytes 417800 | tf_op jit(solution)/shard_map/ppermute | solution.py:322
  19.3 1.3 collective-permute-start.3
  21.6 5.2 %collective-permute-done.3.refs_3_ = bf16[544,128]{1,0:T(8,128)(2,1)S(1)} collective-permute-done((bf16[544,128]{1,0:T(8,128)(2,1)}, bf16[544,128]{1,0:T(8,128)(2,1)S(1)}, u32[]{:S(2)}, u32[]{:S(2)}) %collective-permute-start.3) | collective-permute-done | bytes 139296 | tf_op jit(solution)/shard_map/ppermute | solution.py:322
  27.4 7.6 %shard_map.86 = (bf16[256,1024]{1,0:T(8,128)(2,1)}, bf16[256,1024]{1,0:T(8,128)(2,1)}, bf16[3,256,1280]{2,1,0:T(8,128)(2,1)}, bf16[32,256]{1,0:T(8,128)(2,1)}, b...) custom-call(s32[7,8]{1,0:T(8,128)} %flips.7, ...), custom_call_target="tpu_custom_call" | custom-call | tf_op jit(solution)/shard_map/pallas_call | solution.py:294
  35.1 7.0 %shard_map.87 = (f32[2,8,144,128]{3,2,1,0:T(8,128)}, bf16[2,8,144,128]{3,2,1,0:T(8,128)(2,1)}) custom-call(bf16[256,1024]{1,0:T(8,128)(2,1)} %get-tuple-element.63.grad_tile.back, bf16[3,256,1280]{2,1,0:T(8,128)(2,1)} %get-tuple-element.46.pads), custom_call_target="tpu_custom_call" | custom-call | tf_op jit(solution)/shard_map/pallas_call | solution.py:294
  42.1 3.0 %collective-permute-start.4 = (bf16[2,8,144,128]{3,2,1,0:T(8,128)(2,1)}, bf16[2,8,144,128]{3,2,1,0:T(8,128)(2,1)S(1)}, u32[]{:S(2)}, u32[]{:S(2)}) collective-permute-start(bf16[2,8,144,128]{3,2,1,0:T(8,128)(2,1)} %get-tuple-element.48), channel_id=1, source_target_pairs={{0,1},{1,0},{2,3},{3,2},{4,5},{5,4},{6,7},{7,6},{8,9},{9,8},{10,11... | collective-permute-start | bytes 1769480 | tf_op jit(solution)/shard_map/ppermute | solution.py:339
  45.0 3.1 %collective-permute-start.7 = (bf16[32,256]{1,0:T(8,128)(2,1)S(1)}, bf16[32,256]{1,0:T(8,128)(2,1)S(1)}, u32[]{:S(2)}, u32[]{:S(2)}) collective-permute-start(bf16[32,256]{1,0:T(8,128)(2,1)S(1)} %copy-done.16), channel_id=1, source_target_pairs={{0,224},{32,0},{64,32},{96,64},{128,96},{160,128},{192,160},{224,1... | collective-permute-start | bytes 49160 | tf_op jit(solution)/shard_map/ppermute | solution.py:319
  49.8 1.7 shard_map.89
  51.5 3.8 %collective-permute-start.8 = (bf16[544,128]{1,0:T(8,128)(2,1)}, bf16[544,128]{1,0:T(8,128)(2,1)S(1)}, u32[]{:S(2)}, u32[]{:S(2)}) collective-permute-start(bf16[544,128]{1,0:T(8,128)(2,1)} %get-tuple-element.57), channel_id=1, source_target_pairs={{0,4},{4,8},{8,12},{12,16},{16,20},{20,24},{24,28},{1,5},{5,9},{9,... | collective-permute-start | bytes 417800 | tf_op jit(solution)/shard_map/ppermute | solution.py:322
  55.3 1.3 collective-permute-start.9
  57.4 2.4 %shard_map.88 = (f32[8,144,128]{2,1,0:T(8,128)}, bf16[8,144,128]{2,1,0:T(8,128)(2,1)}) custom-call(f32[2,8,144,128]{3,2,1,0:T(8,128)} %get-tuple-element.47.keep, bf16[2,8,144,128]{3,2,1,0:T(8,128)(2,1)} %copy-done.1), custom_call_target="tpu_custom_call" | custom-call | tf_op jit(solution)/shard_map/pallas_call | solution.py:294
  59.8 3.0 %collective-permute-done.9.refs_3_ = bf16[544,128]{1,0:T(8,128)(2,1)S(1)} collective-permute-done((bf16[544,128]{1,0:T(8,128)(2,1)}, bf16[544,128]{1,0:T(8,128)(2,1)S(1)}, u32[]{:S(2)}, u32[]{:S(2)}) %collective-permute-start.9) | collective-permute-done | bytes 139296 | tf_op jit(solution)/shard_map/ppermute | solution.py:322
  63.5 7.9 %shard_map.90 = (bf16[3,256,1280]{2,1,0:T(8,128)(2,1)}, f32[2,8,144,128]{3,2,1,0:T(8,128)}, bf16[2,8,144,128]{3,2,1,0:T(8,128)(2,1)}) custom-call(s32[7,8]{1,0:T(8,128)} %flips.7, bf16[256,1024]{1,0:T(8,128)(2,1)} %get-tuple-element.52.act, bf16[256,1024]{1,0:T(8,128)(2,1)} %get-tuple-element.38.cotangent, bf16[32,256]{1,0:T(8,128)(2,1)} %copy-done.10, ...), custom_call_target="tpu_custom_call" | custom-call | tf_op jit(solution)/shard_map/pallas_call | solution.py:294
  71.4 2.3 %collective-permute-start.10 = (bf16[2,8,144,128]{3,2,1,0:T(8,128)(2,1)}, bf16[2,8,144,128]{3,2,1,0:T(8,128)(2,1)S(1)}, u32[]{:S(2)}, u32[]{:S(2)}) collective-permute-start(bf16[2,8,144,128]{3,2,1,0:T(8,128)(2,1)} %get-tuple-element.60), channel_id=1, source_target_pairs={{0,1},{1,0},{2,3},{3,2},{4,5},{5,4},{6,7},{7,6},{8,9},{9,8},{10,11... | collective-permute-start | bytes 1769480 | tf_op jit(solution)/shard_map/ppermute | solution.py:339
  76.4 2.4 %shard_map.91 = (f32[8,144,128]{2,1,0:T(8,128)}, bf16[8,144,128]{2,1,0:T(8,128)(2,1)}) custom-call(f32[2,8,144,128]{3,2,1,0:T(8,128)} %get-tuple-element.59.keep, bf16[2,8,144,128]{3,2,1,0:T(8,128)(2,1)} %copy-done.2), custom_call_target="tpu_custom_call" | custom-call | tf_op jit(solution)/shard_map/pallas_call | solution.py:294
  80.1 2.4 %collective-permute-done.5 = bf16[8,144,128]{2,1,0:T(8,128)(2,1)S(1)} collective-permute-done((bf16[8,144,128]{2,1,0:T(8,128)(2,1)}, bf16[8,144,128]{2,1,0:T(8,128)(2,1)S(1)}, u32[]{:S(2)}, u32[]{:S(2)}) %collective-permute-start.5) | collective-permute-done | bytes 294944 | tf_op jit(solution)/shard_map/ppermute | solution.py:335
  83.2 6.3 %all-to-all-start = ((bf16[8,144,128]{2,1,0:T(8,128)(2,1)}), bf16[8,144,128]{2,1,0:T(8,128)(2,1)S(1)}, u32[]{:S(2)}, u32[]{:S(2)}) async-start(bf16[8,144,128]{2,1,0:T(8,128)(2,1)} %add_convert_fusion.1), calls=%async_computation | async-start | bytes 589824 | tf_op jit(solution)/shard_map/all_to_all | solution.py:343
  90.4 6.6 %all-to-all-done = bf16[8,144,128]{2,1,0:T(8,128)(2,1)S(1)} async-done(((bf16[8,144,128]{2,1,0:T(8,128)(2,1)}), bf16[8,144,128]{2,1,0:T(8,128)(2,1)S(1)}, u32[]{:S(2)}, u32[]{:S(2)}) %all-to-all-start) | async-done | bytes 294944 | tf_op jit(solution)/shard_map/all_to_all | solution.py:343
  97.0 3.4 %all-to-all-start.1 = ((bf16[8,144,128]{2,1,0:T(8,128)(2,1)}), bf16[8,144,128]{2,1,0:T(8,128)(2,1)S(1)}, u32[]{:S(2)}, u32[]{:S(2)}) async-start(bf16[8,144,128]{2,1,0:T(8,128)(2,1)} %add_convert_fusion), calls=%async_computation.1 | async-start | bytes 589824 | tf_op jit(solution)/shard_map/all_to_all | solution.py:343
  100.5 7.3 %all-to-all-done.1 = bf16[8,144,128]{2,1,0:T(8,128)(2,1)S(1)} async-done(((bf16[8,144,128]{2,1,0:T(8,128)(2,1)}), bf16[8,144,128]{2,1,0:T(8,128)(2,1)S(1)}, u32[]{:S(2)}, u32[]{:S(2)}) %all-to-all-start.1) | async-done | bytes 294944 | tf_op jit(solution)/shard_map/all_to_all | solution.py:343
  107.9 14.2 %all_to_all.25 = f32[8,36,128]{2,1,0:T(8,128)S(1)} all-to-all(f32[8,36,128]{2,1,0:T(8,128)S(1)} %reshape.29), channel_id=1, replica_groups=mesh['lon'=8,'lat'=8,'dp'=4] {'lon'}, dimensions={0} | all-to-all | bytes 294912 | tf_op jit(solution)/shard_map/all_to_all | solution.py:343
  122.1 9.8 %all_to_all.26 = bf16[8,36,128]{2,1,0:T(8,128)(2,1)S(1)} all-to-all(bf16[8,36,128]{2,1,0:T(8,128)(2,1)S(1)} %broadcast_in_dim.6), channel_id=1, replica_groups=mesh['lon'=8,'lat'=8,'dp'=4] {'lon'}, dimensions={0} | all-to-all | bytes 147456 | tf_op jit(solution)/shard_map/all_to_all | solution.py:343
  132.0 12.0 %all_to_all.27.mine = bf16[8,288,128]{2,1,0:T(8,128)(2,1)S(1)} all-to-all(bf16[8,288,128]{2,1,0:T(8,128)(2,1)S(1)} %broadcast_in_dim.15), channel_id=1, replica_groups=mesh['lon'=8,'lat'=8,'dp'=4] {'lat'}, dimensions={0} | all-to-all | bytes 1179648 | tf_op jit(solution)/shard_map/all_to_all | solution.py:343
  144.8 8.0 %collective-permute-start.13 = (bf16[8,288,128]{2,1,0:T(8,128)(2,1)S(1)}, bf16[8,288,128]{2,1,0:T(8,128)(2,1)S(1)}, u32[]{:S(2)}, u32[]{:S(2)}) collective-permute-start(bf16[8,288,128]{2,1,0:T(8,128)(2,1)S(1)} %all_to_all.27.mine), channel_id=1, source_target_pairs={{0,1},{1,0},{2,3},{3,2},{4,5},{5,4},{6,7},{7,6},{8,9},{9,8},{10,11... | collective-permute-start | bytes 1769480 | tf_op jit(solution)/shard_map/ppermute | solution.py:339
  152.8 1.4 collective-permute-done.12.beside
  154.1 7.8 %collective-permute-start.14 = (bf16[8,288,128]{2,1,0:T(8,128)(2,1)S(1)}, bf16[8,288,128]{2,1,0:T(8,128)(2,1)S(1)}, u32[]{:S(2)}, u32[]{:S(2)}) collective-permute-start(bf16[8,288,128]{2,1,0:T(8,128)(2,1)S(1)} %collective-permute-done.12.beside), channel_id=1, source_target_pairs={{0,1},{1,0},{2,3},{3,2},{4,5},{5,4},{6,7},{7,6},{8,9},{9,8},{10,11... | collective-permute-start | bytes 1769480 | tf_op jit(solution)/shard_map/ppermute | solution.py:339
  162.0 9.6 %shard_map.92 = (bf16[256,8,128]{2,1,0:T(8,128)(2,1)}, bf16[256,8,128]{2,1,0:T(8,128)(2,1)}) custom-call(s32[7,8]{1,0:T(8,128)} %flips.7, bf16[256,1024]{1,0:T(8,128)(2,1)} %get-tuple-element.37.field, bf16[256,1024]{1,0:T(8,128)(2,1)} %get-tuple-element.38.cotangent, bf16[256,1024]{1,0:T(8,128)(2,1)} %get-tuple-element.63.grad_tile.back, ...), custom_call_target="tpu_custom_call" | custom-call | tf_op jit(solution)/shard_map/pallas_call | solution.py:294
  173.2 4.1 %shard_map.93 = (f32[9,256,256]{2,1,0:T(8,128)}, f32[9,256,256]{2,1,0:T(8,128)}) custom-call(bf16[8,288,128]{2,1,0:T(8,128)(2,1)} %copy-done, bf16[8,288,128]{2,1,0:T(8,128)(2,1)} %copy-done.5, bf16[8,288,128]{2,1,0:T(8,128)(2,1)} %copy-done.6, bf16[8,288,128]{2,1,0:T(8,128)(2,1)} %copy-done.7), custom_call_target="tpu_custom_call" | custom-call | tf_op jit(solution)/shard_map/pallas_call | solution.py:294
  (61 shorter events, 14.8 us)
Async XLA Ops:
  4.4 7.7 %collective-permute-start = (bf16[32,256]{1,0:T(8,128)(2,1)}, bf16[32,256]{1,0:T(8,128)(2,1)S(1)}, u32[]{:S(2)}, u32[]{:S(2)}) collective-permute-start(bf16[32,256]{1,0:T(8,128)(2,1)} %get-tuple-element.39), channel_id=1, source_target_pairs={{0,32},{32,64},{64,96},{96,128},{128,160},{160,192},{192,224},{224... | collective-permute-start | bytes 49160 | tf_op jit(solution)/shard_map/ppermute | solution.py:319
  6.8 5.3 %collective-permute-start.1 = (bf16[32,256]{1,0:T(8,128)(2,1)}, bf16[32,256]{1,0:T(8,128)(2,1)S(1)}, u32[]{:S(2)}, u32[]{:S(2)}) collective-permute-start(bf16[32,256]{1,0:T(8,128)(2,1)} %get-tuple-element.40), channel_id=1, source_target_pairs={{0,224},{32,0},{64,32},{96,64},{128,96},{160,128},{192,160},{224,1... | collective-permute-start | bytes 49160 | tf_op jit(solution)/shard_map/ppermute | solution.py:319
  12.1 0.6 copy-start.15
  14.4 7.1 %collective-permute-start.2 = (bf16[544,128]{1,0:T(8,128)(2,1)}, bf16[544,128]{1,0:T(8,128)(2,1)S(1)}, u32[]{:S(2)}, u32[]{:S(2)}) collective-permute-start(bf16[544,128]{1,0:T(8,128)(2,1)} %get-tuple-element.43), channel_id=1, source_target_pairs={{0,4},{4,8},{8,12},{12,16},{16,20},{20,24},{24,28},{1,5},{5,9},{9,... | collective-permute-start | bytes 417800 | tf_op jit(solution)/shard_map/ppermute | solution.py:322
  19.3 7.5 %collective-permute-start.3 = (bf16[544,128]{1,0:T(8,128)(2,1)}, bf16[544,128]{1,0:T(8,128)(2,1)S(1)}, u32[]{:S(2)}, u32[]{:S(2)}) collective-permute-start(bf16[544,128]{1,0:T(8,128)(2,1)} %get-tuple-element.44), channel_id=1, source_target_pairs={{4,0},{8,4},{12,8},{16,12},{20,16},{24,20},{28,24},{5,1},{9,5},{13... | collective-permute-start | bytes 417800 | tf_op jit(solution)/shard_map/ppermute | solution.py:322
  21.6 5.2 %copy-start.12 = (bf16[544,128]{1,0:T(8,128)(2,1)}, bf16[544,128]{1,0:T(8,128)(2,1)S(1)}, u32[]{:S(2)}) copy-start(bf16[544,128]{1,0:T(8,128)(2,1)S(1)} %collective-permute-done.2.refs_2_) | copy-start | bytes 417796
  26.8 0.7 copy-start.13
  35.1 10.0 %copy-start.17 = (bf16[32,256]{1,0:T(8,128)(2,1)S(1)}, bf16[32,256]{1,0:T(8,128)(2,1)}, u32[]{:S(2)}) copy-start(bf16[32,256]{1,0:T(8,128)(2,1)} %get-tuple-element.53) | copy-start | bytes 49156
  35.1 10.0 %copy-start.16 = (bf16[32,256]{1,0:T(8,128)(2,1)S(1)}, bf16[32,256]{1,0:T(8,128)(2,1)}, u32[]{:S(2)}) copy-start(bf16[32,256]{1,0:T(8,128)(2,1)} %get-tuple-element.54) | copy-start | bytes 49156
  42.1 14.5 %collective-permute-start.4 = (bf16[2,8,144,128]{3,2,1,0:T(8,128)(2,1)}, bf16[2,8,144,128]{3,2,1,0:T(8,128)(2,1)S(1)}, u32[]{:S(2)}, u32[]{:S(2)}) collective-permute-start(bf16[2,8,144,128]{3,2,1,0:T(8,128)(2,1)} %get-tuple-element.48), channel_id=1, source_target_pairs={{0,1},{1,0},{2,3},{3,2},{4,5},{5,4},{6,7},{7,6},{8,9},{9,8},{10,11... | collective-permute-start | bytes 1769480 | tf_op jit(solution)/shard_map/ppermute | solution.py:339
  45.0 4.1 %collective-permute-start.6 = (bf16[32,256]{1,0:T(8,128)(2,1)S(1)}, bf16[32,256]{1,0:T(8,128)(2,1)S(1)}, u32[]{:S(2)}, u32[]{:S(2)}) collective-permute-start(bf16[32,256]{1,0:T(8,128)(2,1)S(1)} %copy-done.17), channel_id=1, source_target_pairs={{0,32},{32,64},{64,96},{96,128},{128,160},{160,192},{192,224},{224... | collective-permute-start | bytes 49160 | tf_op jit(solution)/shard_map/ppermute | solution.py:319
  45.0 4.1 %collective-permute-start.7 = (bf16[32,256]{1,0:T(8,128)(2,1)S(1)}, bf16[32,256]{1,0:T(8,128)(2,1)S(1)}, u32[]{:S(2)}, u32[]{:S(2)}) collective-permute-start(bf16[32,256]{1,0:T(8,128)(2,1)S(1)} %copy-done.16), channel_id=1, source_target_pairs={{0,224},{32,0},{64,32},{96,64},{128,96},{160,128},{192,160},{224,1... | collective-permute-start | bytes 49160 | tf_op jit(solution)/shard_map/ppermute | solution.py:319
  51.5 8.3 %collective-permute-start.8 = (bf16[544,128]{1,0:T(8,128)(2,1)}, bf16[544,128]{1,0:T(8,128)(2,1)S(1)}, u32[]{:S(2)}, u32[]{:S(2)}) collective-permute-start(bf16[544,128]{1,0:T(8,128)(2,1)} %get-tuple-element.57), channel_id=1, source_target_pairs={{0,4},{4,8},{8,12},{12,16},{16,20},{20,24},{24,28},{1,5},{5,9},{9,... | collective-permute-start | bytes 417800 | tf_op jit(solution)/shard_map/ppermute | solution.py:322
  55.3 7.5 %collective-permute-start.9 = (bf16[544,128]{1,0:T(8,128)(2,1)}, bf16[544,128]{1,0:T(8,128)(2,1)S(1)}, u32[]{:S(2)}, u32[]{:S(2)}) collective-permute-start(bf16[544,128]{1,0:T(8,128)(2,1)} %get-tuple-element.58), channel_id=1, source_target_pairs={{4,0},{8,4},{12,8},{16,12},{20,16},{24,20},{28,24},{5,1},{9,5},{13... | collective-permute-start | bytes 417800 | tf_op jit(solution)/shard_map/ppermute | solution.py:322
  56.6 0.8 copy-start.1
  59.8 22.6 %copy-start.3 = (f32[8,144,128]{2,1,0:T(8,128)S(1)}, f32[8,144,128]{2,1,0:T(8,128)}, u32[]{:S(2)}) copy-start(f32[8,144,128]{2,1,0:T(8,128)} %get-tuple-element.49) | copy-start | bytes 1769476
  59.8 3.0 %copy-start.8 = (bf16[544,128]{1,0:T(8,128)(2,1)}, bf16[544,128]{1,0:T(8,128)(2,1)S(1)}, u32[]{:S(2)}) copy-start(bf16[544,128]{1,0:T(8,128)(2,1)S(1)} %collective-permute-done.8.refs_2_) | copy-start | bytes 417796
  62.8 0.7 copy-start.9
  71.4 4.2 %collective-permute-start.10 = (bf16[2,8,144,128]{3,2,1,0:T(8,128)(2,1)}, bf16[2,8,144,128]{3,2,1,0:T(8,128)(2,1)S(1)}, u32[]{:S(2)}, u32[]{:S(2)}) collective-permute-start(bf16[2,8,144,128]{3,2,1,0:T(8,128)(2,1)} %get-tuple-element.60), channel_id=1, source_target_pairs={{0,1},{1,0},{2,3},{3,2},{4,5},{5,4},{6,7},{7,6},{8,9},{9,8},{10,11... | collective-permute-start | bytes 1769480 | tf_op jit(solution)/shard_map/ppermute | solution.py:339
  73.7 8.8 %collective-permute-start.5 = (bf16[8,144,128]{2,1,0:T(8,128)(2,1)}, bf16[8,144,128]{2,1,0:T(8,128)(2,1)S(1)}, u32[]{:S(2)}, u32[]{:S(2)}) collective-permute-start(bf16[8,144,128]{2,1,0:T(8,128)(2,1)} %get-tuple-element.50), channel_id=1, source_target_pairs={{0,2},{1,3},{2,0},{3,1},{4,6},{5,7},{6,4},{7,5},{8,10},{9,11},{10,... | collective-permute-start | bytes 884744 | tf_op jit(solution)/shard_map/ppermute | solution.py:335
  75.5 0.8 copy-start.2
  78.8 10.8 %copy-start.4 = (f32[8,144,128]{2,1,0:T(8,128)S(1)}, f32[8,144,128]{2,1,0:T(8,128)}, u32[]{:S(2)}) copy-start(f32[8,144,128]{2,1,0:T(8,128)} %get-tuple-element.61) | copy-start | bytes 1769476
  78.8 10.8 %collective-permute-start.11 = (bf16[8,144,128]{2,1,0:T(8,128)(2,1)}, bf16[8,144,128]{2,1,0:T(8,128)(2,1)S(1)}, u32[]{:S(2)}, u32[]{:S(2)}) collective-permute-start(bf16[8,144,128]{2,1,0:T(8,128)(2,1)} %get-tuple-element.62), channel_id=1, source_target_pairs={{0,2},{1,3},{2,0},{3,1},{4,6},{5,7},{6,4},{7,5},{8,10},{9,11},{10,... | collective-permute-start | bytes 884744 | tf_op jit(solution)/shard_map/ppermute | solution.py:335
  83.2 13.8 %all-to-all-start = ((bf16[8,144,128]{2,1,0:T(8,128)(2,1)}), bf16[8,144,128]{2,1,0:T(8,128)(2,1)S(1)}, u32[]{:S(2)}, u32[]{:S(2)}) async-start(bf16[8,144,128]{2,1,0:T(8,128)(2,1)} %add_convert_fusion.1), calls=%async_computation | async-start | bytes 589824 | tf_op jit(solution)/shard_map/all_to_all | solution.py:343
  97.0 10.8 %all-to-all-start.1 = ((bf16[8,144,128]{2,1,0:T(8,128)(2,1)}), bf16[8,144,128]{2,1,0:T(8,128)(2,1)S(1)}, u32[]{:S(2)}, u32[]{:S(2)}) async-start(bf16[8,144,128]{2,1,0:T(8,128)(2,1)} %add_convert_fusion), calls=%async_computation.1 | async-start | bytes 589824 | tf_op jit(solution)/shard_map/all_to_all | solution.py:343
  144.1 27.5 %copy-start = (bf16[8,288,128]{2,1,0:T(8,128)(2,1)}, bf16[8,288,128]{2,1,0:T(8,128)(2,1)S(1)}, u32[]{:S(2)}) copy-start(bf16[8,288,128]{2,1,0:T(8,128)(2,1)S(1)} %all_to_all.27.mine) | copy-start | bytes 1769476
  144.1 10.1 %collective-permute-start.12 = (bf16[8,288,128]{2,1,0:T(8,128)(2,1)S(1)}, bf16[8,288,128]{2,1,0:T(8,128)(2,1)S(1)}, u32[]{:S(2)}, u32[]{:S(2)}) collective-permute-start(bf16[8,288,128]{2,1,0:T(8,128)(2,1)S(1)} %all_to_all.27.mine), channel_id=1, source_target_pairs={{0,2},{1,3},{2,0},{3,1},{4,6},{5,7},{6,4},{7,5},{8,10},{9,11},{10,... | collective-permute-start | bytes 1769480 | tf_op jit(solution)/shard_map/ppermute | solution.py:335
  144.8 26.8 %collective-permute-start.13 = (bf16[8,288,128]{2,1,0:T(8,128)(2,1)S(1)}, bf16[8,288,128]{2,1,0:T(8,128)(2,1)S(1)}, u32[]{:S(2)}, u32[]{:S(2)}) collective-permute-start(bf16[8,288,128]{2,1,0:T(8,128)(2,1)S(1)} %all_to_all.27.mine), channel_id=1, source_target_pairs={{0,1},{1,0},{2,3},{3,2},{4,5},{5,4},{6,7},{7,6},{8,9},{9,8},{10,11... | collective-permute-start | bytes 1769480 | tf_op jit(solution)/shard_map/ppermute | solution.py:339
  154.1 17.4 %copy-start.5 = (bf16[8,288,128]{2,1,0:T(8,128)(2,1)}, bf16[8,288,128]{2,1,0:T(8,128)(2,1)S(1)}, u32[]{:S(2)}) copy-start(bf16[8,288,128]{2,1,0:T(8,128)(2,1)S(1)} %collective-permute-done.12.beside) | copy-start | bytes 1769476
  154.1 17.4 %collective-permute-start.14 = (bf16[8,288,128]{2,1,0:T(8,128)(2,1)S(1)}, bf16[8,288,128]{2,1,0:T(8,128)(2,1)S(1)}, u32[]{:S(2)}, u32[]{:S(2)}) collective-permute-start(bf16[8,288,128]{2,1,0:T(8,128)(2,1)S(1)} %collective-permute-done.12.beside), channel_id=1, source_target_pairs={{0,1},{1,0},{2,3},{3,2},{4,5},{5,4},{6,7},{7,6},{8,9},{9,8},{10,11... | collective-permute-start | bytes 1769480 | tf_op jit(solution)/shard_map/ppermute | solution.py:339
  171.6 0.8 copy-start.6
  172.4 0.8 copy-start.7
  (3 other events, 1.8 us)

commit v4 on v3

--- a/solution.py
+++ b/solution.py
@@ -224,26 +224,19 @@
         term = lax.dot_general(
             grad_tile[...], pads[s, :, r * LANES : r * LANES + CELLS], NT, preferred_element_type=F32
         )
+        chans = term.shape[0]
         for part in range(2):
             half, group = divmod(2 * tap + part, 9)
-            sides, tiles, rows, lanes = keep.shape
-            shape = (sides, tiles, rows // 9, lanes)
-            piece = term[:, part * LANES : (part + 1) * LANES].reshape(shape)
-            span = slice(group * shape[2], (group + 1) * shape[2])
+            piece = term[:, part * LANES : (part + 1) * LANES]
+            rows = slice(group * chans, (group + 1) * chans)
 
             @pl.when(core == half)
             def _():
-                keep[:, :, span, :] = piece
+                keep[rows] = piece
 
             @pl.when(core != half)
             def _():
-                away[:, :, span, :] = piece.astype(BF16)
-
-
-def fold_kernel(keep, got, kept, away):
-    side = lax.div(lax.axis_index("dp"), 2)
-    kept[...] = keep[side] + got[side].astype(F32)
-    away[...] = (keep[1 - side] + got[1 - side].astype(F32)).astype(BF16)
+                away[rows] = piece.astype(BF16)
 
 
 def grad_two_kernel(flips, act, cotangent, *refs):
@@ -252,38 +245,44 @@
     grad_kernel(cotangent, pads, *outs)
 
 
-def result_kernel(flips, field, cotangent, back, one, two, pads, *refs):
-    halo, (output, grad_fields, back_pads) = (refs[:4], refs[4:])
+def output_kernel(field, weight, pads, output):
+    total = (field[...].astype(F32) + conv(weight, pads)).astype(BF16)
+    for row in range(ROWS):
+        output[:, row, :] = total[:, row * LANES : (row + 1) * LANES]
+
+
+def grad_fields_kernel(flips, cotangent, back, weight, *refs):
+    halo, (grad_fields, back_pads) = (refs[:4], refs[4:])
     flags = edge_flags(flips)
-    total = (field[...].astype(F32) + conv(two, pads)).astype(BF16)
     pad_backward(back_pads, back[...], flags, halo)
-    grads = (cotangent[...].astype(F32) + conv_adjoint(one, back_pads, flags, halo)).astype(BF16)
+    total = (cotangent[...].astype(F32) + conv_adjoint(weight, back_pads, flags, halo)).astype(BF16)
     for row in range(ROWS):
-        span = slice(row * LANES, (row + 1) * LANES)
-        output[:, row, :] = total[:, span]
-        grad_fields[:, row, :] = grads[:, span]
-
-
-def finish_kernel(mine, beside, paired, across, out_one, out_two):
+        grad_fields[:, row, :] = total[:, row * LANES : (row + 1) * LANES]
+
+
+def finish_kernel(mine, beside, paired, across, out_one, out_two, flat):
     place = lax.axis_index("dp")
     core, side = (lax.rem(place, 2) == 1, place >= 2)
-    rows = out_one.shape[1] // 2
-    _, depth = mine.shape[:2]
-    thick = depth // 18
+    chans = out_one.shape[1]
+    tiles, depth = mine.shape[:2]
+    depth = depth // 2
     for which, out in enumerate((out_one, out_two)):
-        for group in range(9):
-            start = (which * 9 + group) * thick
+        for tile in range(tiles):
             a, b, c, d = (
-                ref[:, start : start + thick, :].astype(F32).reshape(rows, LANES)
+                ref[tile, which * depth : (which + 1) * depth, :]
                 for ref in (mine, beside, paired, across)
             )
+            low, high = (tile * depth, (tiles + tile) * depth)
+            for half, (near, far) in enumerate(((a, b), (c, d))):
+                flat[half, low : low + depth] = jnp.where(side, far, near)
+                flat[half, high : high + depth] = jnp.where(side, near, far)
+        for group in range(9):
+            rows = slice(group * chans, (group + 1) * chans)
+            own, other = (flat[0, rows].astype(F32), flat[1, rows].astype(F32))
             for half in range(2):
                 tap, part = divmod(group + half * 9, 2)
-                other = core if half == 0 else jnp.logical_not(core)
-                near, far = (jnp.where(other, c, a), jnp.where(other, d, b))
-                lanes = slice(part * LANES, (part + 1) * LANES)
-                out[tap, :rows, lanes] = jnp.where(side, far, near)
-                out[tap, rows:, lanes] = jnp.where(side, near, far)
+                piece = jnp.where(core, other, own) if half == 0 else jnp.where(core, own, other)
+                out[tap, :, part * LANES : (part + 1) * LANES] = piece
 
 
 SMEM = pl.BlockSpec(memory_space=pltpu.SMEM)
@@ -349,13 +348,15 @@
 
 def fold(grad):
     keep, away = grad
-    shape = keep.shape[1:]
-    return call(fold_kernel, (struct(*shape, dtype=F32), struct(*shape)), (keep, paired(away)), flags=False)
-
-
-def lat_sum(kept, away):
-    got = beside(away)
-    return total(over((kept + got.astype(F32)).astype(BF16), "lat"))
+    got = paired(away)
+    side = lax.shift_right_logical(lax.axis_index("dp"), 1)
+    half = keep.shape[0] // 2
+
+    def rows(which):
+        pick = lambda value: lax.dynamic_slice_in_dim(value, which * half, half, 0).astype(F32)
+        return pick(keep) + pick(got)
+
+    return (rows(side), beside(rows(1 - side).astype(BF16)))
 
 
 def gathered(value, axis):
@@ -363,8 +364,11 @@
 
 
 def reduce_grads(one, two):
-    share = jnp.concatenate([lat_sum(*one), lat_sum(*two)], 0)
-    lons = lax.axis_size("lon")
+    lats, lons = (lax.axis_size("lat"), lax.axis_size("lon"))
+    parts = [
+        (kept + got.astype(F32)).astype(BF16).reshape(lats, -1, LANES) for kept, got in (one, two)
+    ]
+    share = total(over(jnp.concatenate(parts, 1), "lat"))
     share = total(over(share.reshape(lons, share.shape[0] // lons, LANES), "lon")).astype(BF16)
     share = gathered(share, "lon")
     return gathered(share.reshape(-1, LANES), "lat")
@@ -389,21 +393,24 @@
         scratch,
     )
     halo = exchange(rim)
-    local = (2, lax.axis_size("lat"), 9 * chans // (2 * lax.axis_size("lat")), LANES)
-    local = (struct(*local, dtype=F32), struct(*local))
+    local = (struct(9 * chans, LANES, dtype=F32), struct(9 * chans, LANES))
     one = call(grad_kernel, local, (back, pads_in), flags=False)
     one = fold(one)
-    act, _ = lax.optimization_barrier((act, one[0]))
     pads_act, *two = call(grad_two_kernel, (pads,) + local, (edge_flips, act, cot) + halo)
-    quarter = reduce_grads(one, fold(two))
-    quarter, back = lax.optimization_barrier((quarter, back))
+    two = fold(two)
+    output = call(output_kernel, tile, (field, weight_two, pads_act), flags=False)
+    quarter = reduce_grads(one, two)
     other = beside(quarter)
-    output, grad_fields = call(
-        result_kernel, (tile, tile), (edge_flips, field, cot, back, weight_one, weight_two, pads_act) + halo, scratch
+    grad_fields = call(
+        grad_fields_kernel, tile, (edge_flips, cot, back, weight_one) + halo, scratch
     )
     grad = struct(9, chans, chans, dtype=F32)
     grad_one, grad_two = call(
-        finish_kernel, (grad, grad), (quarter, other, paired(quarter), paired(other)), flags=False
+        finish_kernel,
+        (grad, grad),
+        (quarter, other, paired(quarter), paired(other)),
+        [pltpu.VMEM((2, 9 * chans, LANES), BF16)],
+        flags=False,
     )
     return (output.reshape(fields.shape), grad_fields.reshape(fields.shape), grad_one, grad_two)
 
@@ -413,4 +420,6 @@
     out_specs = (P("dp", None, "lat", "lon"), P("dp", None, "lat", "lon"), P(), P())
 
 
-    return jax.shard_map(per_device, mesh=mesh, in_specs=in_specs, out_specs=out_specs, check_vma=False)
+    return jax.shard_map(
+        per_device, mesh=mesh, in_specs=in_specs, out_specs=out_specs, check_vma=False
+    )

time: 178 us -> 177 us (level)
  blocking collectives: 36 us -> 52.9 us
  starting transfers between devices: 54.9 us -> 42.5 us
  Pallas kernels: 48.2 us -> 45.5 us
    all_to_all x3 -> x4, blocking collectives: 36 us -> 52.9 us  [over(): return lax.all_to_all(value, axis, 0, 0)]
    all_to_all x2 -> x0, waiting for transfers between devices: 13.9 us -> none  [over(): return lax.all_to_all(value, axis, 0, 0)]
    ppermute x3, waiting for transfers between devices: 3.78 us -> 13.7 us  [beside(): return lax.ppermute(value, 'dp', [(i, (i + 2) % 4) for i in range(4)])]
    all_to_all x2 -> x0, starting transfers between devices: 9.77 us -> none  [over(): return lax.all_to_all(value, axis, 0, 0)]
    ppermute x4, waiting for transfers between devices: 9.18 us -> 12.4 us  [across(): lax.ppermute(value, 'lat', [(i, i + step) for i in range(lats) if 0 <= i...]
    pallas_call x10 -> x9, Pallas kernels: 48.2 us -> 45.5 us  [call(): pl.pallas_call(kernel, out_shape=out_shape, in_specs=([SMEM] if flags els...]
    ppermute x4, starting transfers between devices: 21.1 us -> 18.7 us  [paired(): return lax.ppermute(value, 'dp', [(0, 1), (1, 0), (2, 3), (3, 2)])]
    unnamed x36 -> x32, local copies, waits for them, and re-layouts: 5.82 us -> 4.2 us
  transfers between devices with their start and end apart: 17 -> 15, of which waited for: 10 -> 9; matrix products, arithmetic and copies ran while one was open for 1% -> 1% of each run, Pallas kernels for 9% -> 12%
where the time goes in v4:
time: 177 us
  blocking collectives  52.9 us (30%)
  Pallas kernels  45.5 us (26%)
  starting transfers between devices  42.5 us (24%)
  waiting for transfers between devices  28.4 us (16%)
  local copies, waits for them, and re-layouts  4.33 us (2%)
  other arithmetic  2.13 us (1%)
    all_to_all x4, blocking collectives, over(): return lax.all_to_all(value, axis, 0, 0)  52.9 us
    pallas_call x9, Pallas kernels, call(): pl.pallas_call(kernel, out_shape=out_shape, in_specs=([SMEM] if flags els...  45.5 us
    ppermute x4, starting transfers between devices, paired(): return lax.ppermute(value, 'dp', [(0, 1), (1, 0), (2, 3), (3, 2)])  18.7 us
    ppermute x3, waiting for transfers between devices, beside(): return lax.ppermute(value, 'dp', [(i, (i + 2) % 4) for i in range(4)])  13.7 us
    ppermute x4, waiting for transfers between devices, across(): lax.ppermute(value, 'lat', [(i, i + step) for i in range(lats) if 0 <= i...  12.4 us
    ppermute x4, starting transfers between devices, across(): lax.ppermute(value, 'lat', [(i, i + step) for i in range(lats) if 0 <= i...  11.2 us
    ppermute x4, starting transfers between devices, along(): lax.ppermute(value, 'lon', [(i, (i + step) % lons) for i in range(lons)])  9.56 us
    unnamed x32, local copies, waits for them, and re-layouts  4.2 us
  transfers between devices with their start and end apart: 15, of which 9 were waited for; matrix products, arithmetic and copies ran while one was open for 1% of the time, Pallas kernels for 12%

profile of v4, /device:TPU:1, one launch (start us, length us, event | category | flops | bytes accessed | tf_op | source)
XLA Modules:
  0.0 176.5 jit_solution(4677138734599354745)
XLA Ops:
  0.6 3.8 %shard_map.84 = (bf16[256,1024]{1,0:T(8,128)(2,1)}, bf16[256,1024]{1,0:T(8,128)(2,1)}, bf16[32,256]{1,0:T(8,128)(2,1)}, bf16[32,256]{1,0:T(8,128)(2,1)}, bf16[51...) custom-call(s32[7,8]{1,0:T(8,128)} %flips.7, bf16[256,8,128]{2,1,0:T(8,128)(2,1)} %bitcast.8, bf16[256,8,128]{2,1,0:T(8,128)(2,1)} %bitcast.9), custom_call_target="tpu_custom_call" | custom-call | tf_op jit(solution)/shard_map/pallas_call | solution.py:293
  4.4 2.5 %collective-permute-start = (bf16[32,256]{1,0:T(8,128)(2,1)}, bf16[32,256]{1,0:T(8,128)(2,1)S(1)}, u32[]{:S(2)}, u32[]{:S(2)}) collective-permute-start(bf16[32,256]{1,0:T(8,128)(2,1)} %get-tuple-element.30), channel_id=1, source_target_pairs={{0,32},{32,64},{64,96},{96,128},{128,160},{160,192},{192,224},{224... | collective-permute-start | bytes 49160 | tf_op jit(solution)/shard_map/ppermute | solution.py:318
  6.8 4.0 %collective-permute-start.1 = (bf16[32,256]{1,0:T(8,128)(2,1)}, bf16[32,256]{1,0:T(8,128)(2,1)S(1)}, u32[]{:S(2)}, u32[]{:S(2)}) collective-permute-start(bf16[32,256]{1,0:T(8,128)(2,1)} %get-tuple-element.31), channel_id=1, source_target_pairs={{0,224},{32,0},{64,32},{96,64},{128,96},{160,128},{192,160},{224,1... | collective-permute-start | bytes 49160 | tf_op jit(solution)/shard_map/ppermute | solution.py:318
  10.9 1.3 collective-permute-done.from_w.refs_0_
  12.7 1.7 shard_map.85
  14.4 4.8 %collective-permute-start.2 = (bf16[544,128]{1,0:T(8,128)(2,1)}, bf16[544,128]{1,0:T(8,128)(2,1)S(1)}, u32[]{:S(2)}, u32[]{:S(2)}) collective-permute-start(bf16[544,128]{1,0:T(8,128)(2,1)} %get-tuple-element.34), channel_id=1, source_target_pairs={{0,4},{4,8},{8,12},{12,16},{16,20},{20,24},{24,28},{1,5},{5,9},{9,... | collective-permute-start | bytes 417800 | tf_op jit(solution)/shard_map/ppermute | solution.py:321
  19.2 1.3 collective-permute-start.3
  21.6 5.2 %collective-permute-done.3.refs_3_ = bf16[544,128]{1,0:T(8,128)(2,1)S(1)} collective-permute-done((bf16[544,128]{1,0:T(8,128)(2,1)}, bf16[544,128]{1,0:T(8,128)(2,1)S(1)}, u32[]{:S(2)}, u32[]{:S(2)}) %collective-permute-start.3) | collective-permute-done | bytes 139296 | tf_op jit(solution)/shard_map/ppermute | solution.py:321
  27.4 7.6 %shard_map.86 = (bf16[256,1024]{1,0:T(8,128)(2,1)}, bf16[256,1024]{1,0:T(8,128)(2,1)}, bf16[3,256,1280]{2,1,0:T(8,128)(2,1)}, bf16[32,256]{1,0:T(8,128)(2,1)}, b...) custom-call(s32[7,8]{1,0:T(8,128)} %flips.7, ...), custom_call_target="tpu_custom_call" | custom-call | tf_op jit(solution)/shard_map/pallas_call | solution.py:293
  35.1 7.0 %shard_map.91 = (f32[2304,128]{1,0:T(8,128)}, bf16[2304,128]{1,0:T(8,128)(2,1)}) custom-call(bf16[256,1024]{1,0:T(8,128)(2,1)} %get-tuple-element.44.back.grad_tile, bf16[3,256,1280]{2,1,0:T(8,128)(2,1)} %get-tuple-element.45.pads), custom_call_target="tpu_custom_call" | custom-call | tf_op jit(solution)/shard_map/pallas_call | solution.py:293
  42.1 3.0 %collective-permute-start.8 = (bf16[2304,128]{1,0:T(8,128)(2,1)}, bf16[2304,128]{1,0:T(8,128)(2,1)S(1)}, u32[]{:S(2)}, u32[]{:S(2)}) collective-permute-start(bf16[2304,128]{1,0:T(8,128)(2,1)} %get-tuple-element.47), channel_id=1, source_target_pairs={{0,1},{1,0},{2,3},{3,2},{4,5},{5,4},{6,7},{7,6},{8,9},{9,8},{10,11... | collective-permute-start | bytes 1769480 | tf_op jit(solution)/shard_map/ppermute | solution.py:338
  45.1 3.1 %collective-permute-start.5 = (bf16[32,256]{1,0:T(8,128)(2,1)S(1)}, bf16[32,256]{1,0:T(8,128)(2,1)S(1)}, u32[]{:S(2)}, u32[]{:S(2)}) collective-permute-start(bf16[32,256]{1,0:T(8,128)(2,1)S(1)} %copy-done.14), channel_id=1, source_target_pairs={{0,224},{32,0},{64,32},{96,64},{128,96},{160,128},{192,160},{224,1... | collective-permute-start | bytes 49160 | tf_op jit(solution)/shard_map/ppermute | solution.py:318
  49.8 1.7 shard_map.87
  51.5 3.8 %collective-permute-start.6 = (bf16[544,128]{1,0:T(8,128)(2,1)}, bf16[544,128]{1,0:T(8,128)(2,1)S(1)}, u32[]{:S(2)}, u32[]{:S(2)}) collective-permute-start(bf16[544,128]{1,0:T(8,128)(2,1)} %get-tuple-element.41), channel_id=1, source_target_pairs={{0,4},{4,8},{8,12},{12,16},{16,20},{20,24},{24,28},{1,5},{5,9},{9,... | collective-permute-start | bytes 417800 | tf_op jit(solution)/shard_map/ppermute | solution.py:321
  55.3 1.3 collective-permute-start.7
  57.6 5.2 %collective-permute-done.7.refs_3_ = bf16[544,128]{1,0:T(8,128)(2,1)S(1)} collective-permute-done((bf16[544,128]{1,0:T(8,128)(2,1)}, bf16[544,128]{1,0:T(8,128)(2,1)S(1)}, u32[]{:S(2)}, u32[]{:S(2)}) %collective-permute-start.7) | collective-permute-done | bytes 139296 | tf_op jit(solution)/shard_map/ppermute | solution.py:321
  63.5 7.9 %shard_map.88 = (bf16[3,256,1280]{2,1,0:T(8,128)(2,1)}, f32[2304,128]{1,0:T(8,128)}, bf16[2304,128]{1,0:T(8,128)(2,1)}) custom-call(s32[7,8]{1,0:T(8,128)} %flips.7, bf16[256,1024]{1,0:T(8,128)(2,1)} %get-tuple-element.36.act, bf16[256,1024]{1,0:T(8,128)(2,1)} %get-tuple-element.29.cotangent, bf16[32,256]{1,0:T(8,128)(2,1)} %copy-done.8, ...), custom_call_target="tpu_custom_call" | custom-call | tf_op jit(solution)/shard_map/pallas_call | solution.py:293
  71.3 2.4 %collective-permute-start.10 = (bf16[2304,128]{1,0:T(8,128)(2,1)}, bf16[2304,128]{1,0:T(8,128)(2,1)S(1)}, u32[]{:S(2)}, u32[]{:S(2)}) collective-permute-start(bf16[2304,128]{1,0:T(8,128)(2,1)} %get-tuple-element.49), channel_id=1, source_target_pairs={{0,1},{1,0},{2,3},{3,2},{4,5},{5,4},{6,7},{7,6},{8,9},{9,8},{10,11... | collective-permute-start | bytes 1769480 | tf_op jit(solution)/shard_map/ppermute | solution.py:338
  74.5 1.3 collective-permute-start.9
  75.8 1.1 collective-permute-start.11
  77.0 6.3 %collective-permute-done.9 = bf16[1152,128]{1,0:T(8,128)(2,1)} collective-permute-done((bf16[1152,128]{1,0:T(8,128)(2,1)}, bf16[1152,128]{1,0:T(8,128)(2,1)}, u32[]{:S(2)}, u32[]{:S(2)}) %collective-permute-start.9) | collective-permute-done | bytes 294944 | tf_op jit(solution)/shard_map/ppermute | solution.py:334
  84.4 5.1 %collective-permute-done.11 = bf16[1152,128]{1,0:T(8,128)(2,1)S(1)} collective-permute-done((bf16[1152,128]{1,0:T(8,128)(2,1)S(1)}, bf16[1152,128]{1,0:T(8,128)(2,1)S(1)}, u32[]{:S(2)}, u32[]{:S(2)}) %collective-permute-start.11) | collective-permute-done | bytes 294944 | tf_op jit(solution)/shard_map/ppermute | solution.py:334
  89.7 16.9 %all_to_all.20 = bf16[8,288,128]{2,1,0:T(8,128)(2,1)S(1)} all-to-all(bf16[8,288,128]{2,1,0:T(8,128)(2,1)S(1)} %pad_maximum_fusion), channel_id=1, replica_groups=mesh['lon'=8,'lat'=8,'dp'=4] {'lat'}, dimensions={0} | all-to-all | bytes 1179648 | tf_op jit(solution)/shard_map/all_to_all | solution.py:342
  106.7 14.3 %all_to_all.21 = f32[8,36,128]{2,1,0:T(8,128)S(1)} all-to-all(f32[8,36,128]{2,1,0:T(8,128)S(1)} %reshape.39), channel_id=1, replica_groups=mesh['lon'=8,'lat'=8,'dp'=4] {'lon'}, dimensions={0} | all-to-all | bytes 294912 | tf_op jit(solution)/shard_map/all_to_all | solution.py:342
  121.0 9.8 %all_to_all.22 = bf16[8,36,128]{2,1,0:T(8,128)(2,1)S(1)} all-to-all(bf16[8,36,128]{2,1,0:T(8,128)(2,1)S(1)} %broadcast_in_dim.6), channel_id=1, replica_groups=mesh['lon'=8,'lat'=8,'dp'=4] {'lon'}, dimensions={0} | all-to-all | bytes 147456 | tf_op jit(solution)/shard_map/all_to_all | solution.py:342
  130.9 11.9 %all_to_all.23.mine = bf16[8,288,128]{2,1,0:T(8,128)(2,1)S(1)} all-to-all(bf16[8,288,128]{2,1,0:T(8,128)(2,1)S(1)} %broadcast_in_dim.15), channel_id=1, replica_groups=mesh['lon'=8,'lat'=8,'dp'=4] {'lat'}, dimensions={0} | all-to-all | bytes 1179648 | tf_op jit(solution)/shard_map/all_to_all | solution.py:342
  143.5 6.3 %collective-permute-start.13 = (bf16[8,288,128]{2,1,0:T(8,128)(2,1)S(1)}, bf16[8,288,128]{2,1,0:T(8,128)(2,1)S(1)}, u32[]{:S(2)}, u32[]{:S(2)}) collective-permute-start(bf16[8,288,128]{2,1,0:T(8,128)(2,1)S(1)} %all_to_all.23.mine), channel_id=1, source_target_pairs={{0,1},{1,0},{2,3},{3,2},{4,5},{5,4},{6,7},{7,6},{8,9},{9,8},{10,11... | collective-permute-start | bytes 1769480 | tf_op jit(solution)/shard_map/ppermute | solution.py:338
  149.8 2.2 %collective-permute-done.12.beside = bf16[8,288,128]{2,1,0:T(8,128)(2,1)S(1)} collective-permute-done((bf16[8,288,128]{2,1,0:T(8,128)(2,1)S(1)}, bf16[8,288,128]{2,1,0:T(8,128)(2,1)S(1)}, u32[]{:S(2)}, u32[]{:S(2)}) %collective-permute-start.12) | collective-permute-done | bytes 589856 | tf_op jit(solution)/shard_map/ppermute | solution.py:334
  152.0 7.0 %collective-permute-start.14 = (bf16[8,288,128]{2,1,0:T(8,128)(2,1)S(1)}, bf16[8,288,128]{2,1,0:T(8,128)(2,1)S(1)}, u32[]{:S(2)}, u32[]{:S(2)}) collective-permute-start(bf16[8,288,128]{2,1,0:T(8,128)(2,1)S(1)} %collective-permute-done.12.beside), channel_id=1, source_target_pairs={{0,1},{1,0},{2,3},{3,2},{4,5},{5,4},{6,7},{7,6},{8,9},{9,8},{10,11... | collective-permute-start | bytes 1769480 | tf_op jit(solution)/shard_map/ppermute | solution.py:338
  159.0 5.5 %shard_map.89 = bf16[256,8,128]{2,1,0:T(8,128)(2,1)} custom-call(bf16[256,1024]{1,0:T(8,128)(2,1)} %get-tuple-element.28.field, bf16[9,256,256]{2,1,0:T(8,128)(2,1)} %weight.2, bf16[3,256,1280]{2,1,0:T(8,128)(2,1)} %get-tuple-element.43.pads), custom_call_target="tpu_custom_call" | custom-call | tf_op jit(solution)/shard_map/pallas_call | solution.py:293
  164.5 5.9 %shard_map.90 = bf16[256,8,128]{2,1,0:T(8,128)(2,1)} custom-call(s32[7,8]{1,0:T(8,128)} %flips.7, bf16[256,1024]{1,0:T(8,128)(2,1)} %get-tuple-element.29.cotangent, bf16[256,1024]{1,0:T(8,128)(2,1)} %get-tuple-element.44.back.grad_tile, bf16[9,256,256]{2,1,0:T(8,128)(2,1)} %weight.3, bf16[32,256]{1,0:T(8,128)(2,1)} %copy-done.8, bf16[32,256]{1,0:T(8,128)(2,1)} %copy-done.9, ...), custom_call_target="tpu_custom_call" | custom-call | tf_op jit(solution)/shard_map/pallas_call | solution.py:293
  172.1 4.4 %shard_map.92 = (f32[9,256,256]{2,1,0:T(8,128)}, f32[9,256,256]{2,1,0:T(8,128)}) custom-call(bf16[8,288,128]{2,1,0:T(8,128)(2,1)} %copy-done, bf16[8,288,128]{2,1,0:T(8,128)(2,1)} %copy-done.3, bf16[8,288,128]{2,1,0:T(8,128)(2,1)} %copy-done.4, bf16[8,288,128]{2,1,0:T(8,128)(2,1)} %copy-done.5), custom_call_target="tpu_custom_call" | custom-call | tf_op jit(solution)/shard_map/pallas_call | solution.py:293
  (54 shorter events, 10.2 us)
Async XLA Ops:
  4.4 7.7 %collective-permute-start = (bf16[32,256]{1,0:T(8,128)(2,1)}, bf16[32,256]{1,0:T(8,128)(2,1)S(1)}, u32[]{:S(2)}, u32[]{:S(2)}) collective-permute-start(bf16[32,256]{1,0:T(8,128)(2,1)} %get-tuple-element.30), channel_id=1, source_target_pairs={{0,32},{32,64},{64,96},{96,128},{128,160},{160,192},{192,224},{224... | collective-permute-start | bytes 49160 | tf_op jit(solution)/shard_map/ppermute | solution.py:318
  6.8 5.3 %collective-permute-start.1 = (bf16[32,256]{1,0:T(8,128)(2,1)}, bf16[32,256]{1,0:T(8,128)(2,1)S(1)}, u32[]{:S(2)}, u32[]{:S(2)}) collective-permute-start(bf16[32,256]{1,0:T(8,128)(2,1)} %get-tuple-element.31), channel_id=1, source_target_pairs={{0,224},{32,0},{64,32},{96,64},{128,96},{160,128},{192,160},{224,1... | collective-permute-start | bytes 49160 | tf_op jit(solution)/shard_map/ppermute | solution.py:318
  12.1 0.6 copy-start.12
  12.1 0.6 copy-start.13
  14.4 7.1 %collective-permute-start.2 = (bf16[544,128]{1,0:T(8,128)(2,1)}, bf16[544,128]{1,0:T(8,128)(2,1)S(1)}, u32[]{:S(2)}, u32[]{:S(2)}) collective-permute-start(bf16[544,128]{1,0:T(8,128)(2,1)} %get-tuple-element.34), channel_id=1, source_target_pairs={{0,4},{4,8},{8,12},{12,16},{16,20},{20,24},{24,28},{1,5},{5,9},{9,... | collective-permute-start | bytes 417800 | tf_op jit(solution)/shard_map/ppermute | solution.py:321
  19.2 7.5 %collective-permute-start.3 = (bf16[544,128]{1,0:T(8,128)(2,1)}, bf16[544,128]{1,0:T(8,128)(2,1)S(1)}, u32[]{:S(2)}, u32[]{:S(2)}) collective-permute-start(bf16[544,128]{1,0:T(8,128)(2,1)} %get-tuple-element.35), channel_id=1, source_target_pairs={{4,0},{8,4},{12,8},{16,12},{20,16},{24,20},{28,24},{5,1},{9,5},{13... | collective-permute-start | bytes 417800 | tf_op jit(solution)/shard_map/ppermute | solution.py:321
  21.6 5.2 %copy-start.10 = (bf16[544,128]{1,0:T(8,128)(2,1)}, bf16[544,128]{1,0:T(8,128)(2,1)S(1)}, u32[]{:S(2)}) copy-start(bf16[544,128]{1,0:T(8,128)(2,1)S(1)} %collective-permute-done.2.refs_2_) | copy-start | bytes 417796
  26.8 0.7 copy-start.11
  35.1 10.0 %copy-start.15 = (bf16[32,256]{1,0:T(8,128)(2,1)S(1)}, bf16[32,256]{1,0:T(8,128)(2,1)}, u32[]{:S(2)}) copy-start(bf16[32,256]{1,0:T(8,128)(2,1)} %get-tuple-element.37) | copy-start | bytes 49156
  35.1 10.0 %copy-start.14 = (bf16[32,256]{1,0:T(8,128)(2,1)S(1)}, bf16[32,256]{1,0:T(8,128)(2,1)}, u32[]{:S(2)}) copy-start(bf16[32,256]{1,0:T(8,128)(2,1)} %get-tuple-element.38) | copy-start | bytes 49156
  42.1 31.6 %copy-start.1 = (f32[2304,128]{1,0:T(8,128)S(1)}, f32[2304,128]{1,0:T(8,128)}, u32[]{:S(2)}) copy-start(f32[2304,128]{1,0:T(8,128)} %get-tuple-element.46) | copy-start | bytes 3538948
  42.1 31.6 %collective-permute-start.8 = (bf16[2304,128]{1,0:T(8,128)(2,1)}, bf16[2304,128]{1,0:T(8,128)(2,1)S(1)}, u32[]{:S(2)}, u32[]{:S(2)}) collective-permute-start(bf16[2304,128]{1,0:T(8,128)(2,1)} %get-tuple-element.47), channel_id=1, source_target_pairs={{0,1},{1,0},{2,3},{3,2},{4,5},{5,4},{6,7},{7,6},{8,9},{9,8},{10,11... | collective-permute-start | bytes 1769480 | tf_op jit(solution)/shard_map/ppermute | solution.py:338
  45.1 4.2 %collective-permute-start.4 = (bf16[32,256]{1,0:T(8,128)(2,1)S(1)}, bf16[32,256]{1,0:T(8,128)(2,1)S(1)}, u32[]{:S(2)}, u32[]{:S(2)}) collective-permute-start(bf16[32,256]{1,0:T(8,128)(2,1)S(1)} %copy-done.15), channel_id=1, source_target_pairs={{0,32},{32,64},{64,96},{96,128},{128,160},{160,192},{192,224},{224... | collective-permute-start | bytes 49160 | tf_op jit(solution)/shard_map/ppermute | solution.py:318
  45.1 4.1 %collective-permute-start.5 = (bf16[32,256]{1,0:T(8,128)(2,1)S(1)}, bf16[32,256]{1,0:T(8,128)(2,1)S(1)}, u32[]{:S(2)}, u32[]{:S(2)}) collective-permute-start(bf16[32,256]{1,0:T(8,128)(2,1)S(1)} %copy-done.14), channel_id=1, source_target_pairs={{0,224},{32,0},{64,32},{96,64},{128,96},{160,128},{192,160},{224,1... | collective-permute-start | bytes 49160 | tf_op jit(solution)/shard_map/ppermute | solution.py:318
  49.2 0.6 copy-start.8
  49.2 0.6 copy-start.9
  51.5 6.1 %collective-permute-start.6 = (bf16[544,128]{1,0:T(8,128)(2,1)}, bf16[544,128]{1,0:T(8,128)(2,1)S(1)}, u32[]{:S(2)}, u32[]{:S(2)}) collective-permute-start(bf16[544,128]{1,0:T(8,128)(2,1)} %get-tuple-element.41), channel_id=1, source_target_pairs={{0,4},{4,8},{8,12},{12,16},{16,20},{20,24},{24,28},{1,5},{5,9},{9,... | collective-permute-start | bytes 417800 | tf_op jit(solution)/shard_map/ppermute | solution.py:321
  55.3 7.5 %collective-permute-start.7 = (bf16[544,128]{1,0:T(8,128)(2,1)}, bf16[544,128]{1,0:T(8,128)(2,1)S(1)}, u32[]{:S(2)}, u32[]{:S(2)}) collective-permute-start(bf16[544,128]{1,0:T(8,128)(2,1)} %get-tuple-element.42), channel_id=1, source_target_pairs={{4,0},{8,4},{12,8},{16,12},{20,16},{24,20},{28,24},{5,1},{9,5},{13... | collective-permute-start | bytes 417800 | tf_op jit(solution)/shard_map/ppermute | solution.py:321
  57.6 5.2 %copy-start.6 = (bf16[544,128]{1,0:T(8,128)(2,1)}, bf16[544,128]{1,0:T(8,128)(2,1)S(1)}, u32[]{:S(2)}) copy-start(bf16[544,128]{1,0:T(8,128)(2,1)S(1)} %collective-permute-done.6.refs_2_) | copy-start | bytes 417796
  62.8 0.7 copy-start.7
  71.3 4.5 %copy-start.2 = (f32[2304,128]{1,0:T(8,128)S(1)}, f32[2304,128]{1,0:T(8,128)}, u32[]{:S(2)}) copy-start(f32[2304,128]{1,0:T(8,128)} %get-tuple-element.48) | copy-start | bytes 3538948
  71.3 4.5 %collective-permute-start.10 = (bf16[2304,128]{1,0:T(8,128)(2,1)}, bf16[2304,128]{1,0:T(8,128)(2,1)S(1)}, u32[]{:S(2)}, u32[]{:S(2)}) collective-permute-start(bf16[2304,128]{1,0:T(8,128)(2,1)} %get-tuple-element.49), channel_id=1, source_target_pairs={{0,1},{1,0},{2,3},{3,2},{4,5},{5,4},{6,7},{7,6},{8,9},{9,8},{10,11... | collective-permute-start | bytes 1769480 | tf_op jit(solution)/shard_map/ppermute | solution.py:338
  74.5 8.9 %collective-permute-start.9 = (bf16[1152,128]{1,0:T(8,128)(2,1)}, bf16[1152,128]{1,0:T(8,128)(2,1)}, u32[]{:S(2)}, u32[]{:S(2)}) collective-permute-start(bf16[1152,128]{1,0:T(8,128)(2,1)} %add_convert_fusion.3), channel_id=1, source_target_pairs={{0,2},{1,3},{2,0},{3,1},{4,6},{5,7},{6,4},{7,5},{8,10},{9,11},{10,... | collective-permute-start | bytes 884744 | tf_op jit(solution)/shard_map/ppermute | solution.py:334
  75.8 13.7 %collective-permute-start.11 = (bf16[1152,128]{1,0:T(8,128)(2,1)S(1)}, bf16[1152,128]{1,0:T(8,128)(2,1)S(1)}, u32[]{:S(2)}, u32[]{:S(2)}) collective-permute-start(bf16[1152,128]{1,0:T(8,128)(2,1)S(1)} %add_convert_fusion.1), channel_id=1, source_target_pairs={{0,2},{1,3},{2,0},{3,1},{4,6},{5,7},{6,4},{7,5},{8,10},{9,11},{10,... | collective-permute-start | bytes 884744 | tf_op jit(solution)/shard_map/ppermute | solution.py:334
  142.8 21.7 %copy-start = (bf16[8,288,128]{2,1,0:T(8,128)(2,1)}, bf16[8,288,128]{2,1,0:T(8,128)(2,1)S(1)}, u32[]{:S(2)}) copy-start(bf16[8,288,128]{2,1,0:T(8,128)(2,1)S(1)} %all_to_all.23.mine) | copy-start | bytes 1769476
  142.8 9.2 %collective-permute-start.12 = (bf16[8,288,128]{2,1,0:T(8,128)(2,1)S(1)}, bf16[8,288,128]{2,1,0:T(8,128)(2,1)S(1)}, u32[]{:S(2)}, u32[]{:S(2)}) collective-permute-start(bf16[8,288,128]{2,1,0:T(8,128)(2,1)S(1)} %all_to_all.23.mine), channel_id=1, source_target_pairs={{0,2},{1,3},{2,0},{3,1},{4,6},{5,7},{6,4},{7,5},{8,10},{9,11},{10,... | collective-permute-start | bytes 1769480 | tf_op jit(solution)/shard_map/ppermute | solution.py:334
  143.5 26.9 %collective-permute-start.13 = (bf16[8,288,128]{2,1,0:T(8,128)(2,1)S(1)}, bf16[8,288,128]{2,1,0:T(8,128)(2,1)S(1)}, u32[]{:S(2)}, u32[]{:S(2)}) collective-permute-start(bf16[8,288,128]{2,1,0:T(8,128)(2,1)S(1)} %all_to_all.23.mine), channel_id=1, source_target_pairs={{0,1},{1,0},{2,3},{3,2},{4,5},{5,4},{6,7},{7,6},{8,9},{9,8},{10,11... | collective-permute-start | bytes 1769480 | tf_op jit(solution)/shard_map/ppermute | solution.py:338
  152.0 12.5 %copy-start.3 = (bf16[8,288,128]{2,1,0:T(8,128)(2,1)}, bf16[8,288,128]{2,1,0:T(8,128)(2,1)S(1)}, u32[]{:S(2)}) copy-start(bf16[8,288,128]{2,1,0:T(8,128)(2,1)S(1)} %collective-permute-done.12.beside) | copy-start | bytes 1769476
  152.0 18.4 %collective-permute-start.14 = (bf16[8,288,128]{2,1,0:T(8,128)(2,1)S(1)}, bf16[8,288,128]{2,1,0:T(8,128)(2,1)S(1)}, u32[]{:S(2)}, u32[]{:S(2)}) collective-permute-start(bf16[8,288,128]{2,1,0:T(8,128)(2,1)S(1)} %collective-permute-done.12.beside), channel_id=1, source_target_pairs={{0,1},{1,0},{2,3},{3,2},{4,5},{5,4},{6,7},{7,6},{8,9},{9,8},{10,11... | collective-permute-start | bytes 1769480 | tf_op jit(solution)/shard_map/ppermute | solution.py:338
  170.4 0.8 copy-start.4
  171.3 0.8 copy-start.5

commit v5 on v4

--- a/solution.py
+++ b/solution.py
@@ -1,3 +1,5 @@
+import functools
+
 import jax
 import jax.numpy as jnp
 from jax import lax
@@ -65,27 +67,33 @@
     side(east, 0, ROWS)
     side(west, ROWS, 0)
     south[:chans] = first[:, CELLS - LANES :]
-    south[chans:] = second[:, CELLS - LANES :]
+    south[chans : 2 * chans] = second[:, CELLS - LANES :]
     north[:chans] = first[:, :LANES]
-    north[chans:] = second[:, :LANES]
-
-
-def join_kernel(south, north, from_w, from_e, south_out, north_out):
-    rows = south.shape[0]
+    north[chans : 2 * chans] = second[:, :LANES]
+
+
+def join_kernel(south, north, from_w, from_e, south_out, north_out, block, sems):
+    rows = south_out.shape[0] - 32
     west, east = (from_w[...].astype(F32), from_e[...].astype(F32))
     at = iota((16, west.shape[1]), 0)
-    for rim, out, near, corner in ((south, south_out, 7, 17), (north, north_out, 0, 16)):
-        out[:rows] = rim[...]
+    copies = []
+    for index, (out, near, corner) in enumerate(((south_out, 7, 17), (north_out, 0, 16))):
         spread = [
             jnp.broadcast_to(side[k : k + 1], at.shape)
             for side in (west, east)
             for k in (near, corner)
         ]
-        block = jnp.where(
+        cells = jnp.where(
             at == 0, spread[0], jnp.where(at == 1, spread[1], jnp.where(at == 2, spread[2], spread[3]))
         ).astype(BF16)
-        out[rows : rows + 16] = block[:, :LANES]
-        out[rows + 16 :] = block[:, LANES:]
+        block[index, :16] = cells[:, :LANES]
+        block[index, 16:] = cells[:, LANES:]
+        copies.append(
+            pltpu.make_async_copy(block.at[index], out.at[pl.ds(rows, 32)], sems.at[index])
+        )
+        copies[-1].start()
+    for copy in copies:
+        copy.wait()
 
 
 def corners_of(line, chans):
@@ -217,7 +225,7 @@
     rims(act_out[...], back_out[...], flags, outs[3:])
 
 
-def grad_kernel(grad_tile, pads, keep, away):
+def grad_kernel(grad_tile, pads, keep, away, both):
     core = lax.rem(lax.axis_index("dp"), 2)
     for tap in range(9):
         r, s = divmod(tap, 3)
@@ -227,16 +235,10 @@
         chans = term.shape[0]
         for part in range(2):
             half, group = divmod(2 * tap + part, 9)
-            piece = term[:, part * LANES : (part + 1) * LANES]
-            rows = slice(group * chans, (group + 1) * chans)
-
-            @pl.when(core == half)
-            def _():
-                keep[rows] = piece
-
-            @pl.when(core != half)
-            def _():
-                away[rows] = piece.astype(BF16)
+            place = core if half == 0 else 1 - core
+            both[place, group * chans : (group + 1) * chans] = term[:, part * LANES : (part + 1) * LANES]
+    keep[...] = both[0]
+    away[...] = both[1].astype(BF16)
 
 
 def grad_two_kernel(flips, act, cotangent, *refs):
@@ -260,33 +262,76 @@
         grad_fields[:, row, :] = total[:, row * LANES : (row + 1) * LANES]
 
 
-def finish_kernel(mine, beside, paired, across, out_one, out_two, flat):
+def finish_kernel(own, near, far, *refs):
+    outs, (flat, stage, sems) = (refs[-5:-3], refs[-3:])
     place = lax.axis_index("dp")
-    core, side = (lax.rem(place, 2) == 1, place >= 2)
-    chans = out_one.shape[1]
-    tiles, depth = mine.shape[:2]
+    side, core = (lax.shift_right_logical(place, 1), lax.rem(place, 2))
+    half = core if own else 1 - core
+    chans = stage.shape[2]
+    tiles, depth = near.shape[:2]
     depth = depth // 2
-    for which, out in enumerate((out_one, out_two)):
+    size = tiles * depth
+    for which in range(2):
         for tile in range(tiles):
-            a, b, c, d = (
-                ref[tile, which * depth : (which + 1) * depth, :]
-                for ref in (mine, beside, paired, across)
-            )
-            low, high = (tile * depth, (tiles + tile) * depth)
-            for half, (near, far) in enumerate(((a, b), (c, d))):
-                flat[half, low : low + depth] = jnp.where(side, far, near)
-                flat[half, high : high + depth] = jnp.where(side, near, far)
-        for group in range(9):
-            rows = slice(group * chans, (group + 1) * chans)
-            own, other = (flat[0, rows].astype(F32), flat[1, rows].astype(F32))
-            for half in range(2):
-                tap, part = divmod(group + half * 9, 2)
-                piece = jnp.where(core, other, own) if half == 0 else jnp.where(core, own, other)
-                out[tap, :, part * LANES : (part + 1) * LANES] = piece
+            rows = slice(which * depth, (which + 1) * depth)
+            for ref, to in ((near, side), (far, 1 - side)):
+                start = pl.multiple_of(to * size + tile * depth, 16)
+                flat[which, pl.ds(start, depth)] = ref[tile, rows, :]
+
+    def place_half(odd):
+        copies = []
+        for which, out in enumerate(outs):
+            for slot in range(5):
+                lanes = slice(0, 2 * LANES)
+                for part in range(2):
+                    group = 2 * slot + part - odd
+                    if 0 <= group < 9:
+                        span = slice(part * LANES, (part + 1) * LANES)
+                        rows = slice(group * chans, (group + 1) * chans)
+                        stage[which, slot, :, span] = flat[which, rows].astype(F32)
+                    else:
+                        lanes = slice((1 - part) * LANES, (2 - part) * LANES)
+                copies.append(
+                    pltpu.make_async_copy(
+                        stage.at[which, slot, :, lanes],
+                        out.at[slot + 4 * odd, :, lanes],
+                        sems.at[which, slot],
+                    )
+                )
+                copies[-1].start()
+        for copy in copies:
+            copy.wait()
+
+    @pl.when(half == 0)
+    def _():
+        place_half(0)
+
+    @pl.when(half == 1)
+    def _():
+        place_half(1)
+
+
+def finish(own, near, far, *partial):
+    chans = partial[0].shape[1] if partial else 2 * LANES
+    grad = struct(9, chans, chans, dtype=F32)
+    return pl.pallas_call(
+        functools.partial(finish_kernel, own),
+        out_shape=(grad, grad),
+        in_specs=[VMEM, VMEM] + [ANY] * len(partial),
+        out_specs=(ANY, ANY),
+        input_output_aliases={2 + k: k for k in range(len(partial))},
+        scratch_shapes=[
+            pltpu.VMEM((2, 9 * chans, LANES), BF16),
+            pltpu.VMEM((2, 5, chans, chans), F32),
+            pltpu.SemaphoreType.DMA((2, 5)),
+        ],
+        compiler_params=pltpu.CompilerParams(vmem_limit_bytes=56 * 1024 * 1024),
+    )(near, far, *partial)
 
 
 SMEM = pl.BlockSpec(memory_space=pltpu.SMEM)
 VMEM = pl.BlockSpec(memory_space=pltpu.VMEM)
+ANY = pl.BlockSpec(memory_space=pl.ANY)
 
 
 def call(kernel, out_shape, args, scratch=(), flags=True):
@@ -306,7 +351,7 @@
 
 def rim_shapes(chans):
     side = struct(4 * ROWS, chans)
-    line = struct(2 * chans, LANES)
+    line = struct(2 * chans + 32, LANES)
     return (side, side, line, line)
 
 
@@ -323,8 +368,16 @@
         )
 
     from_w, from_e = (along(east, 1), along(west, -1))
-    line = struct(south.shape[0] + 32, LANES)
-    south, north = call(join_kernel, (line, line), (south, north, from_w, from_e), flags=False)
+    line = struct(*south.shape)
+    south, north = pl.pallas_call(
+        join_kernel,
+        name="join",
+        out_shape=(line, line),
+        in_specs=[ANY, ANY, VMEM, VMEM],
+        out_specs=(ANY, ANY),
+        input_output_aliases={0: 0, 1: 1},
+        scratch_shapes=[pltpu.VMEM((2, 32, LANES), BF16), pltpu.SemaphoreType.DMA((2,))],
+    )(south, north, from_w, from_e)
     from_n = across(south, 1)
     from_s = across(north, -1)
     return (from_w, from_e, from_n, from_s)
@@ -394,9 +447,10 @@
     )
     halo = exchange(rim)
     local = (struct(9 * chans, LANES, dtype=F32), struct(9 * chans, LANES))
-    one = call(grad_kernel, local, (back, pads_in), flags=False)
+    halves = [pltpu.VMEM((2, 9 * chans, LANES), F32)]
+    one = call(grad_kernel, local, (back, pads_in), halves, flags=False)
     one = fold(one)
-    pads_act, *two = call(grad_two_kernel, (pads,) + local, (edge_flips, act, cot) + halo)
+    pads_act, *two = call(grad_two_kernel, (pads,) + local, (edge_flips, act, cot) + halo, halves)
     two = fold(two)
     output = call(output_kernel, tile, (field, weight_two, pads_act), flags=False)
     quarter = reduce_grads(one, two)
@@ -404,14 +458,10 @@
     grad_fields = call(
         grad_fields_kernel, tile, (edge_flips, cot, back, weight_one) + halo, scratch
     )
-    grad = struct(9, chans, chans, dtype=F32)
-    grad_one, grad_two = call(
-        finish_kernel,
-        (grad, grad),
-        (quarter, other, paired(quarter), paired(other)),
-        [pltpu.VMEM((2, 9 * chans, LANES), BF16)],
-        flags=False,
-    )
+    pair = paired(quarter)
+    across = paired(other)
+    grads = finish(True, quarter, other)
+    grad_one, grad_two = finish(False, pair, across, *grads)
     return (output.reshape(fields.shape), grad_fields.reshape(fields.shape), grad_one, grad_two)
 
 

time: 177 us -> 172 us (0.972)
  Pallas kernels: 45.5 us -> 40.7 us
    pallas_call x9 -> x6, Pallas kernels: 45.5 us -> 32.3 us  [call(): pl.pallas_call(kernel, out_shape=out_shape, in_specs=([SMEM] if flags els...]
    pallas_call x0 -> x4, Pallas kernels: none -> 8.37 us  [the longest x2 5.65 us: finish(): pl.pallas_call(functools.partial(finish_kernel, own), out_shape=(grad, gr...]
where the time goes in v5:
time: 172 us; the launch traced here: 171 us
  blocking collectives  52.9 us (31%)
  starting transfers between devices  42.7 us (25%)
  Pallas kernels  40.7 us (24%)
  waiting for transfers between devices  28.3 us (16%)
  local copies, waits for them, and re-layouts  3.66 us (2%)
  other arithmetic  2.13 us (1%)
    all_to_all x4, blocking collectives, over(): return lax.all_to_all(value, axis, 0, 0)  52.9 us
    pallas_call x6, Pallas kernels, call(): pl.pallas_call(kernel, out_shape=out_shape, in_specs=([SMEM] if flags els...  32.3 us
    ppermute x4, starting transfers between devices, paired(): return lax.ppermute(value, 'dp', [(0, 1), (1, 0), (2, 3), (3, 2)])  18.7 us
    ppermute x3, waiting for transfers between devices, beside(): return lax.ppermute(value, 'dp', [(i, (i + 2) % 4) for i in range(4)])  13.7 us
    ppermute x4, waiting for transfers between devices, across(): lax.ppermute(value, 'lat', [(i, i + step) for i in range(lats) if 0 <= i...  12.2 us
    ppermute x4, starting transfers between devices, across(): lax.ppermute(value, 'lat', [(i, i + step) for i in range(lats) if 0 <= i...  11.4 us
    ppermute x4, starting transfers between devices, along(): lax.ppermute(value, 'lon', [(i, (i + step) % lons) for i in range(lons)])  9.54 us
    pallas_call x2, Pallas kernels, finish(): pl.pallas_call(functools.partial(finish_kernel, own), out_shape=(grad, gr...  5.65 us
  transfers between devices with their start and end apart: 15, of which 9 were waited for; matrix products, arithmetic and copies ran while one was open for 1% of the time, Pallas kernels for 12%

profile of v5, /device:TPU:1, one launch (start us, length us, event | category | flops | bytes accessed | tf_op | source)
XLA Modules:
  0.0 171.3 jit_solution(9128274660676870928)
XLA Ops:
  0.6 3.8 %shard_map.84 = (bf16[256,1024]{1,0:T(8,128)(2,1)}, bf16[256,1024]{1,0:T(8,128)(2,1)}, bf16[32,256]{1,0:T(8,128)(2,1)}, bf16[32,256]{1,0:T(8,128)(2,1)}, bf16[54...) custom-call(s32[7,8]{1,0:T(8,128)} %flips.7, bf16[256,8,128]{2,1,0:T(8,128)(2,1)} %bitcast.8, bf16[256,8,128]{2,1,0:T(8,128)(2,1)} %bitcast.9), custom_call_target="tpu_custom_call" | custom-call | tf_op jit(solution)/shard_map/pallas_call | solution.py:338
  4.4 2.5 %collective-permute-start = (bf16[32,256]{1,0:T(8,128)(2,1)}, bf16[32,256]{1,0:T(8,128)(2,1)S(1)}, u32[]{:S(2)}, u32[]{:S(2)}) collective-permute-start(bf16[32,256]{1,0:T(8,128)(2,1)} %get-tuple-element.32), channel_id=1, source_target_pairs={{0,32},{32,64},{64,96},{96,128},{128,160},{160,192},{192,224},{224... | collective-permute-start | bytes 49160 | tf_op jit(solution)/shard_map/ppermute | solution.py:363
  6.9 4.0 %collective-permute-start.1 = (bf16[32,256]{1,0:T(8,128)(2,1)}, bf16[32,256]{1,0:T(8,128)(2,1)S(1)}, u32[]{:S(2)}, u32[]{:S(2)}) collective-permute-start(bf16[32,256]{1,0:T(8,128)(2,1)} %get-tuple-element.33), channel_id=1, source_target_pairs={{0,224},{32,0},{64,32},{96,64},{128,96},{160,128},{192,160},{224,1... | collective-permute-start | bytes 49160 | tf_op jit(solution)/shard_map/ppermute | solution.py:363
  10.9 1.3 collective-permute-done.from_w.refs_0_
  12.7 1.4 join.2
  14.1 4.8 %collective-permute-start.2 = (bf16[544,128]{1,0:T(8,128)(2,1)}, bf16[544,128]{1,0:T(8,128)(2,1)S(1)}, u32[]{:S(2)}, u32[]{:S(2)}) collective-permute-start(bf16[544,128]{1,0:T(8,128)(2,1)} %get-tuple-element.36), channel_id=1, source_target_pairs={{0,4},{4,8},{8,12},{12,16},{16,20},{20,24},{24,28},{1,5},{5,9},{9,... | collective-permute-start | bytes 417800 | tf_op jit(solution)/shard_map/ppermute | solution.py:366
  18.9 1.3 collective-permute-start.3
  21.3 5.2 %collective-permute-done.3.refs_3_ = bf16[544,128]{1,0:T(8,128)(2,1)S(1)} collective-permute-done((bf16[544,128]{1,0:T(8,128)(2,1)}, bf16[544,128]{1,0:T(8,128)(2,1)S(1)}, u32[]{:S(2)}, u32[]{:S(2)}) %collective-permute-start.3) | collective-permute-done | bytes 139296 | tf_op jit(solution)/shard_map/ppermute | solution.py:366
  27.1 7.6 %shard_map.85 = (bf16[256,1024]{1,0:T(8,128)(2,1)}, bf16[256,1024]{1,0:T(8,128)(2,1)}, bf16[3,256,1280]{2,1,0:T(8,128)(2,1)}, bf16[32,256]{1,0:T(8,128)(2,1)}, b...) custom-call(s32[7,8]{1,0:T(8,128)} %flips.7, ...), custom_call_target="tpu_custom_call" | custom-call | tf_op jit(solution)/shard_map/pallas_call | solution.py:338
  34.8 4.7 %shard_map.89 = (f32[2304,128]{1,0:T(8,128)}, bf16[2304,128]{1,0:T(8,128)(2,1)}) custom-call(bf16[256,1024]{1,0:T(8,128)(2,1)} %get-tuple-element.46.back.grad_tile, bf16[3,256,1280]{2,1,0:T(8,128)(2,1)} %get-tuple-element.47.pads), custom_call_target="tpu_custom_call" | custom-call | tf_op jit(solution)/shard_map/pallas_call | solution.py:338
  39.5 3.0 %collective-permute-start.8 = (bf16[2304,128]{1,0:T(8,128)(2,1)}, bf16[2304,128]{1,0:T(8,128)(2,1)S(1)}, u32[]{:S(2)}, u32[]{:S(2)}) collective-permute-start(bf16[2304,128]{1,0:T(8,128)(2,1)} %get-tuple-element.49), channel_id=1, source_target_pairs={{0,1},{1,0},{2,3},{3,2},{4,5},{5,4},{6,7},{7,6},{8,9},{9,8},{10,11... | collective-permute-start | bytes 1769480 | tf_op jit(solution)/shard_map/ppermute | solution.py:391
  42.4 3.1 %collective-permute-start.5 = (bf16[32,256]{1,0:T(8,128)(2,1)S(1)}, bf16[32,256]{1,0:T(8,128)(2,1)S(1)}, u32[]{:S(2)}, u32[]{:S(2)}) collective-permute-start(bf16[32,256]{1,0:T(8,128)(2,1)S(1)} %copy-done.14), channel_id=1, source_target_pairs={{0,224},{32,0},{64,32},{96,64},{128,96},{160,128},{192,160},{224,1... | collective-permute-start | bytes 49160 | tf_op jit(solution)/shard_map/ppermute | solution.py:363
  47.2 1.4 join.3
  48.5 3.8 %collective-permute-start.6 = (bf16[544,128]{1,0:T(8,128)(2,1)}, bf16[544,128]{1,0:T(8,128)(2,1)S(1)}, u32[]{:S(2)}, u32[]{:S(2)}) collective-permute-start(bf16[544,128]{1,0:T(8,128)(2,1)} %get-tuple-element.43), channel_id=1, source_target_pairs={{0,4},{4,8},{8,12},{12,16},{16,20},{20,24},{24,28},{1,5},{5,9},{9,... | collective-permute-start | bytes 417800 | tf_op jit(solution)/shard_map/ppermute | solution.py:366
  52.3 1.5 collective-permute-start.7
  54.7 5.2 %collective-permute-done.7.refs_3_ = bf16[544,128]{1,0:T(8,128)(2,1)S(1)} collective-permute-done((bf16[544,128]{1,0:T(8,128)(2,1)}, bf16[544,128]{1,0:T(8,128)(2,1)S(1)}, u32[]{:S(2)}, u32[]{:S(2)}) %collective-permute-start.7) | collective-permute-done | bytes 139296 | tf_op jit(solution)/shard_map/ppermute | solution.py:366
  60.5 4.8 %shard_map.86 = (bf16[3,256,1280]{2,1,0:T(8,128)(2,1)}, f32[2304,128]{1,0:T(8,128)}, bf16[2304,128]{1,0:T(8,128)(2,1)}) custom-call(s32[7,8]{1,0:T(8,128)} %flips.7, bf16[256,1024]{1,0:T(8,128)(2,1)} %get-tuple-element.38.act, bf16[256,1024]{1,0:T(8,128)(2,1)} %get-tuple-element.31.cotangent, bf16[32,256]{1,0:T(8,128)(2,1)} %copy-done.8, ...), custom_call_target="tpu_custom_call" | custom-call | tf_op jit(solution)/shard_map/pallas_call | solution.py:338
  65.3 2.4 %collective-permute-start.10 = (bf16[2304,128]{1,0:T(8,128)(2,1)}, bf16[2304,128]{1,0:T(8,128)(2,1)S(1)}, u32[]{:S(2)}, u32[]{:S(2)}) collective-permute-start(bf16[2304,128]{1,0:T(8,128)(2,1)} %get-tuple-element.51), channel_id=1, source_target_pairs={{0,1},{1,0},{2,3},{3,2},{4,5},{5,4},{6,7},{7,6},{8,9},{9,8},{10,11... | collective-permute-start | bytes 1769480 | tf_op jit(solution)/shard_map/ppermute | solution.py:391
  68.5 1.3 collective-permute-start.9
  71.0 6.3 %collective-permute-done.9 = bf16[1152,128]{1,0:T(8,128)(2,1)} collective-permute-done((bf16[1152,128]{1,0:T(8,128)(2,1)}, bf16[1152,128]{1,0:T(8,128)(2,1)}, u32[]{:S(2)}, u32[]{:S(2)}) %collective-permute-start.9) | collective-permute-done | bytes 294944 | tf_op jit(solution)/shard_map/ppermute | solution.py:387
  78.4 5.1 %collective-permute-done.11 = bf16[1152,128]{1,0:T(8,128)(2,1)S(1)} collective-permute-done((bf16[1152,128]{1,0:T(8,128)(2,1)S(1)}, bf16[1152,128]{1,0:T(8,128)(2,1)S(1)}, u32[]{:S(2)}, u32[]{:S(2)}) %collective-permute-start.11) | collective-permute-done | bytes 294944 | tf_op jit(solution)/shard_map/ppermute | solution.py:387
  83.7 16.9 %all_to_all.20 = bf16[8,288,128]{2,1,0:T(8,128)(2,1)S(1)} all-to-all(bf16[8,288,128]{2,1,0:T(8,128)(2,1)S(1)} %pad_maximum_fusion), channel_id=1, replica_groups=mesh['lon'=8,'lat'=8,'dp'=4] {'lat'}, dimensions={0} | all-to-all | bytes 1179648 | tf_op jit(solution)/shard_map/all_to_all | solution.py:395
  100.6 14.3 %all_to_all.21 = f32[8,36,128]{2,1,0:T(8,128)S(1)} all-to-all(f32[8,36,128]{2,1,0:T(8,128)S(1)} %reshape.39), channel_id=1, replica_groups=mesh['lon'=8,'lat'=8,'dp'=4] {'lon'}, dimensions={0} | all-to-all | bytes 294912 | tf_op jit(solution)/shard_map/all_to_all | solution.py:395
  115.0 9.8 %all_to_all.22 = bf16[8,36,128]{2,1,0:T(8,128)(2,1)S(1)} all-to-all(bf16[8,36,128]{2,1,0:T(8,128)(2,1)S(1)} %broadcast_in_dim.6), channel_id=1, replica_groups=mesh['lon'=8,'lat'=8,'dp'=4] {'lon'}, dimensions={0} | all-to-all | bytes 147456 | tf_op jit(solution)/shard_map/all_to_all | solution.py:395
  124.9 11.9 %all_to_all.23.near = bf16[8,288,128]{2,1,0:T(8,128)(2,1)S(1)} all-to-all(bf16[8,288,128]{2,1,0:T(8,128)(2,1)S(1)} %broadcast_in_dim.15), channel_id=1, replica_groups=mesh['lon'=8,'lat'=8,'dp'=4] {'lat'}, dimensions={0} | all-to-all | bytes 1179648 | tf_op jit(solution)/shard_map/all_to_all | solution.py:395
  137.5 6.3 %collective-permute-start.12 = (bf16[8,288,128]{2,1,0:T(8,128)(2,1)S(1)}, bf16[8,288,128]{2,1,0:T(8,128)(2,1)S(1)}, u32[]{:S(2)}, u32[]{:S(2)}) collective-permute-start(bf16[8,288,128]{2,1,0:T(8,128)(2,1)S(1)} %all_to_all.23.near), channel_id=1, source_target_pairs={{0,1},{1,0},{2,3},{3,2},{4,5},{5,4},{6,7},{7,6},{8,9},{9,8},{10,11... | collective-permute-start | bytes 1769480 | tf_op jit(solution)/shard_map/ppermute | solution.py:391
  143.8 2.2 %collective-permute-done.13.far = bf16[8,288,128]{2,1,0:T(8,128)(2,1)S(1)} collective-permute-done((bf16[8,288,128]{2,1,0:T(8,128)(2,1)S(1)}, bf16[8,288,128]{2,1,0:T(8,128)(2,1)S(1)}, u32[]{:S(2)}, u32[]{:S(2)}) %collective-permute-start.13) | collective-permute-done | bytes 589856 | tf_op jit(solution)/shard_map/ppermute | solution.py:387
  146.0 7.0 %collective-permute-start.14 = (bf16[8,288,128]{2,1,0:T(8,128)(2,1)S(1)}, bf16[8,288,128]{2,1,0:T(8,128)(2,1)S(1)}, u32[]{:S(2)}, u32[]{:S(2)}) collective-permute-start(bf16[8,288,128]{2,1,0:T(8,128)(2,1)S(1)} %collective-permute-done.13.far), channel_id=1, source_target_pairs={{0,1},{1,0},{2,3},{3,2},{4,5},{5,4},{6,7},{7,6},{8,9},{9,8},{10,11... | collective-permute-start | bytes 1769480 | tf_op jit(solution)/shard_map/ppermute | solution.py:391
  153.0 5.5 %shard_map.87 = bf16[256,8,128]{2,1,0:T(8,128)(2,1)} custom-call(bf16[256,1024]{1,0:T(8,128)(2,1)} %get-tuple-element.30.field, bf16[9,256,256]{2,1,0:T(8,128)(2,1)} %weight.2, bf16[3,256,1280]{2,1,0:T(8,128)(2,1)} %get-tuple-element.45.pads), custom_call_target="tpu_custom_call" | custom-call | tf_op jit(solution)/shard_map/pallas_call | solution.py:338
  158.5 5.9 %shard_map.88 = bf16[256,8,128]{2,1,0:T(8,128)(2,1)} custom-call(s32[7,8]{1,0:T(8,128)} %flips.7, bf16[256,1024]{1,0:T(8,128)(2,1)} %get-tuple-element.31.cotangent, bf16[256,1024]{1,0:T(8,128)(2,1)} %get-tuple-element.46.back.grad_tile, bf16[9,256,256]{2,1,0:T(8,128)(2,1)} %weight.3, bf16[32,256]{1,0:T(8,128)(2,1)} %copy-done.8, bf16[32,256]{1,0:T(8,128)(2,1)} %copy-done.9, ...), custom_call_target="tpu_custom_call" | custom-call | tf_op jit(solution)/shard_map/pallas_call | solution.py:338
  164.4 2.8 %shard_map.90 = (f32[9,256,256]{2,1,0:T(8,128)}, f32[9,256,256]{2,1,0:T(8,128)}) custom-call(bf16[8,288,128]{2,1,0:T(8,128)(2,1)} %copy-done, bf16[8,288,128]{2,1,0:T(8,128)(2,1)} %copy-done.5), custom_call_target="tpu_custom_call" | custom-call | tf_op jit(solution)/shard_map/pallas_call | solution.py:317
  168.3 2.8 %shard_map.91 = (f32[9,256,256]{2,1,0:T(8,128)}, f32[9,256,256]{2,1,0:T(8,128)}) custom-call(bf16[8,288,128]{2,1,0:T(8,128)(2,1)} %copy-done.3, bf16[8,288,128]{2,1,0:T(8,128)(2,1)} %copy-done.4, f32[9,256,256]{2,1,0:T(8,128)} %get-tuple-element.52.refs_0_, f32[9,256,256]{2,1,0:T(8,128)} %get-tuple-element.53.refs_1_), custom_call_target="tpu_custom_call", output_to_operand_aliasing={{0}: (2, {}), {1}: (3, {})} | custom-call | tf_op jit(solution)/shard_map/pallas_call | solution.py:317
  (55 shorter events, 10.5 us)
Async XLA Ops:
  4.4 7.7 %collective-permute-start = (bf16[32,256]{1,0:T(8,128)(2,1)}, bf16[32,256]{1,0:T(8,128)(2,1)S(1)}, u32[]{:S(2)}, u32[]{:S(2)}) collective-permute-start(bf16[32,256]{1,0:T(8,128)(2,1)} %get-tuple-element.32), channel_id=1, source_target_pairs={{0,32},{32,64},{64,96},{96,128},{128,160},{160,192},{192,224},{224... | collective-permute-start | bytes 49160 | tf_op jit(solution)/shard_map/ppermute | solution.py:363
  6.9 5.3 %collective-permute-start.1 = (bf16[32,256]{1,0:T(8,128)(2,1)}, bf16[32,256]{1,0:T(8,128)(2,1)S(1)}, u32[]{:S(2)}, u32[]{:S(2)}) collective-permute-start(bf16[32,256]{1,0:T(8,128)(2,1)} %get-tuple-element.33), channel_id=1, source_target_pairs={{0,224},{32,0},{64,32},{96,64},{128,96},{160,128},{192,160},{224,1... | collective-permute-start | bytes 49160 | tf_op jit(solution)/shard_map/ppermute | solution.py:363
  12.1 0.6 copy-start.12
  12.1 0.6 copy-start.13
  14.1 7.1 %collective-permute-start.2 = (bf16[544,128]{1,0:T(8,128)(2,1)}, bf16[544,128]{1,0:T(8,128)(2,1)S(1)}, u32[]{:S(2)}, u32[]{:S(2)}) collective-permute-start(bf16[544,128]{1,0:T(8,128)(2,1)} %get-tuple-element.36), channel_id=1, source_target_pairs={{0,4},{4,8},{8,12},{12,16},{16,20},{20,24},{24,28},{1,5},{5,9},{9,... | collective-permute-start | bytes 417800 | tf_op jit(solution)/shard_map/ppermute | solution.py:366
  18.9 7.5 %collective-permute-start.3 = (bf16[544,128]{1,0:T(8,128)(2,1)}, bf16[544,128]{1,0:T(8,128)(2,1)S(1)}, u32[]{:S(2)}, u32[]{:S(2)}) collective-permute-start(bf16[544,128]{1,0:T(8,128)(2,1)} %get-tuple-element.37), channel_id=1, source_target_pairs={{4,0},{8,4},{12,8},{16,12},{20,16},{24,20},{28,24},{5,1},{9,5},{13... | collective-permute-start | bytes 417800 | tf_op jit(solution)/shard_map/ppermute | solution.py:366
  21.3 5.2 %copy-start.10 = (bf16[544,128]{1,0:T(8,128)(2,1)}, bf16[544,128]{1,0:T(8,128)(2,1)S(1)}, u32[]{:S(2)}) copy-start(bf16[544,128]{1,0:T(8,128)(2,1)S(1)} %collective-permute-done.2.refs_2_) | copy-start | bytes 417796
  26.5 0.6 copy-start.11
  34.8 7.7 %copy-start.15 = (bf16[32,256]{1,0:T(8,128)(2,1)S(1)}, bf16[32,256]{1,0:T(8,128)(2,1)}, u32[]{:S(2)}) copy-start(bf16[32,256]{1,0:T(8,128)(2,1)} %get-tuple-element.39) | copy-start | bytes 49156
  34.8 7.7 %copy-start.14 = (bf16[32,256]{1,0:T(8,128)(2,1)S(1)}, bf16[32,256]{1,0:T(8,128)(2,1)}, u32[]{:S(2)}) copy-start(bf16[32,256]{1,0:T(8,128)(2,1)} %get-tuple-element.40) | copy-start | bytes 49156
  39.5 28.2 %copy-start.1 = (f32[2304,128]{1,0:T(8,128)S(1)}, f32[2304,128]{1,0:T(8,128)}, u32[]{:S(2)}) copy-start(f32[2304,128]{1,0:T(8,128)} %get-tuple-element.48) | copy-start | bytes 3538948
  39.5 28.2 %collective-permute-start.8 = (bf16[2304,128]{1,0:T(8,128)(2,1)}, bf16[2304,128]{1,0:T(8,128)(2,1)S(1)}, u32[]{:S(2)}, u32[]{:S(2)}) collective-permute-start(bf16[2304,128]{1,0:T(8,128)(2,1)} %get-tuple-element.49), channel_id=1, source_target_pairs={{0,1},{1,0},{2,3},{3,2},{4,5},{5,4},{6,7},{7,6},{8,9},{9,8},{10,11... | collective-permute-start | bytes 1769480 | tf_op jit(solution)/shard_map/ppermute | solution.py:391
  42.4 4.1 %collective-permute-start.4 = (bf16[32,256]{1,0:T(8,128)(2,1)S(1)}, bf16[32,256]{1,0:T(8,128)(2,1)S(1)}, u32[]{:S(2)}, u32[]{:S(2)}) collective-permute-start(bf16[32,256]{1,0:T(8,128)(2,1)S(1)} %copy-done.15), channel_id=1, source_target_pairs={{0,32},{32,64},{64,96},{96,128},{128,160},{160,192},{192,224},{224... | collective-permute-start | bytes 49160 | tf_op jit(solution)/shard_map/ppermute | solution.py:363
  42.4 4.1 %collective-permute-start.5 = (bf16[32,256]{1,0:T(8,128)(2,1)S(1)}, bf16[32,256]{1,0:T(8,128)(2,1)S(1)}, u32[]{:S(2)}, u32[]{:S(2)}) collective-permute-start(bf16[32,256]{1,0:T(8,128)(2,1)S(1)} %copy-done.14), channel_id=1, source_target_pairs={{0,224},{32,0},{64,32},{96,64},{128,96},{160,128},{192,160},{224,1... | collective-permute-start | bytes 49160 | tf_op jit(solution)/shard_map/ppermute | solution.py:363
  46.6 0.6 copy-start.8
  46.6 0.6 copy-start.9
  48.5 6.1 %collective-permute-start.6 = (bf16[544,128]{1,0:T(8,128)(2,1)}, bf16[544,128]{1,0:T(8,128)(2,1)S(1)}, u32[]{:S(2)}, u32[]{:S(2)}) collective-permute-start(bf16[544,128]{1,0:T(8,128)(2,1)} %get-tuple-element.43), channel_id=1, source_target_pairs={{0,4},{4,8},{8,12},{12,16},{16,20},{20,24},{24,28},{1,5},{5,9},{9,... | collective-permute-start | bytes 417800 | tf_op jit(solution)/shard_map/ppermute | solution.py:366
  52.3 7.5 %collective-permute-start.7 = (bf16[544,128]{1,0:T(8,128)(2,1)}, bf16[544,128]{1,0:T(8,128)(2,1)S(1)}, u32[]{:S(2)}, u32[]{:S(2)}) collective-permute-start(bf16[544,128]{1,0:T(8,128)(2,1)} %get-tuple-element.44), channel_id=1, source_target_pairs={{4,0},{8,4},{12,8},{16,12},{20,16},{24,20},{28,24},{5,1},{9,5},{13... | collective-permute-start | bytes 417800 | tf_op jit(solution)/shard_map/ppermute | solution.py:366
  54.7 5.2 %copy-start.6 = (bf16[544,128]{1,0:T(8,128)(2,1)}, bf16[544,128]{1,0:T(8,128)(2,1)S(1)}, u32[]{:S(2)}) copy-start(bf16[544,128]{1,0:T(8,128)(2,1)S(1)} %collective-permute-done.6.refs_2_) | copy-start | bytes 417796
  59.9 0.7 copy-start.7
  65.3 4.5 %copy-start.2 = (f32[2304,128]{1,0:T(8,128)S(1)}, f32[2304,128]{1,0:T(8,128)}, u32[]{:S(2)}) copy-start(f32[2304,128]{1,0:T(8,128)} %get-tuple-element.50) | copy-start | bytes 3538948
  65.3 4.5 %collective-permute-start.10 = (bf16[2304,128]{1,0:T(8,128)(2,1)}, bf16[2304,128]{1,0:T(8,128)(2,1)S(1)}, u32[]{:S(2)}, u32[]{:S(2)}) collective-permute-start(bf16[2304,128]{1,0:T(8,128)(2,1)} %get-tuple-element.51), channel_id=1, source_target_pairs={{0,1},{1,0},{2,3},{3,2},{4,5},{5,4},{6,7},{7,6},{8,9},{9,8},{10,11... | collective-permute-start | bytes 1769480 | tf_op jit(solution)/shard_map/ppermute | solution.py:391
  68.5 8.9 %collective-permute-start.9 = (bf16[1152,128]{1,0:T(8,128)(2,1)}, bf16[1152,128]{1,0:T(8,128)(2,1)}, u32[]{:S(2)}, u32[]{:S(2)}) collective-permute-start(bf16[1152,128]{1,0:T(8,128)(2,1)} %add_convert_fusion.3), channel_id=1, source_target_pairs={{0,2},{1,3},{2,0},{3,1},{4,6},{5,7},{6,4},{7,5},{8,10},{9,11},{10,... | collective-permute-start | bytes 884744 | tf_op jit(solution)/shard_map/ppermute | solution.py:387
  69.8 13.7 %collective-permute-start.11 = (bf16[1152,128]{1,0:T(8,128)(2,1)S(1)}, bf16[1152,128]{1,0:T(8,128)(2,1)S(1)}, u32[]{:S(2)}, u32[]{:S(2)}) collective-permute-start(bf16[1152,128]{1,0:T(8,128)(2,1)S(1)} %add_convert_fusion.1), channel_id=1, source_target_pairs={{0,2},{1,3},{2,0},{3,1},{4,6},{5,7},{6,4},{7,5},{8,10},{9,11},{10,... | collective-permute-start | bytes 884744 | tf_op jit(solution)/shard_map/ppermute | solution.py:387
  136.8 21.7 %copy-start = (bf16[8,288,128]{2,1,0:T(8,128)(2,1)}, bf16[8,288,128]{2,1,0:T(8,128)(2,1)S(1)}, u32[]{:S(2)}) copy-start(bf16[8,288,128]{2,1,0:T(8,128)(2,1)S(1)} %all_to_all.23.near) | copy-start | bytes 1769476
  136.8 9.2 %collective-permute-start.13 = (bf16[8,288,128]{2,1,0:T(8,128)(2,1)S(1)}, bf16[8,288,128]{2,1,0:T(8,128)(2,1)S(1)}, u32[]{:S(2)}, u32[]{:S(2)}) collective-permute-start(bf16[8,288,128]{2,1,0:T(8,128)(2,1)S(1)} %all_to_all.23.near), channel_id=1, source_target_pairs={{0,2},{1,3},{2,0},{3,1},{4,6},{5,7},{6,4},{7,5},{8,10},{9,11},{10,... | collective-permute-start | bytes 1769480 | tf_op jit(solution)/shard_map/ppermute | solution.py:387
  137.5 29.8 %collective-permute-start.12 = (bf16[8,288,128]{2,1,0:T(8,128)(2,1)S(1)}, bf16[8,288,128]{2,1,0:T(8,128)(2,1)S(1)}, u32[]{:S(2)}, u32[]{:S(2)}) collective-permute-start(bf16[8,288,128]{2,1,0:T(8,128)(2,1)S(1)} %all_to_all.23.near), channel_id=1, source_target_pairs={{0,1},{1,0},{2,3},{3,2},{4,5},{5,4},{6,7},{7,6},{8,9},{9,8},{10,11... | collective-permute-start | bytes 1769480 | tf_op jit(solution)/shard_map/ppermute | solution.py:391
  146.0 12.5 %copy-start.5 = (bf16[8,288,128]{2,1,0:T(8,128)(2,1)}, bf16[8,288,128]{2,1,0:T(8,128)(2,1)S(1)}, u32[]{:S(2)}) copy-start(bf16[8,288,128]{2,1,0:T(8,128)(2,1)S(1)} %collective-permute-done.13.far) | copy-start | bytes 1769476
  146.0 21.3 %collective-permute-start.14 = (bf16[8,288,128]{2,1,0:T(8,128)(2,1)S(1)}, bf16[8,288,128]{2,1,0:T(8,128)(2,1)S(1)}, u32[]{:S(2)}, u32[]{:S(2)}) collective-permute-start(bf16[8,288,128]{2,1,0:T(8,128)(2,1)S(1)} %collective-permute-done.13.far), channel_id=1, source_target_pairs={{0,1},{1,0},{2,3},{3,2},{4,5},{5,4},{6,7},{7,6},{8,9},{9,8},{10,11... | collective-permute-start | bytes 1769480 | tf_op jit(solution)/shard_map/ppermute | solution.py:391
  167.3 0.8 copy-start.3
  167.3 1.0 copy-start.4

commit v6 on v5

--- a/solution.py
+++ b/solution.py
@@ -108,7 +108,9 @@
     return dot(line, turn)
 
 
-def shifted(out, centre, top, bottom, west, east, swap_top=None, swap_bottom=None):
+def shifted(out, centre, top, bottom, west, east, swaps=(None, None)):
+    swap_top, swap_bottom = swaps
+    order = (0, 1, 2) if swap_top is None else (2, 1, 0)
     chans = centre.shape[0]
     k, lane = (iota((16, PADDED), 0), iota((16, PADDED), 1))
     placed_west = lax.dot_general(
@@ -131,9 +133,8 @@
         swap = swap_top if block == 0 else swap_bottom if block == ROWS + 1 else None
         if swap is not None:
             left, right = (jnp.where(swap, right, left), jnp.where(swap, left, right))
-        out[0, :, span] = left.astype(BF16)
-        out[1, :, span] = line.astype(BF16)
-        out[2, :, span] = right.astype(BF16)
+        for slot, cells in zip(order, (left, line, right)):
+            out[slot * chans : (slot + 1) * chans, span] = cells.astype(BF16)
 
 
 def lines(top, mid, bottom):
@@ -162,25 +163,25 @@
     east = lines(none, from_e[...].astype(F32)[ROWS : 2 * ROWS], none)
     top = turned(from_n[chans : 2 * chans], flags[0])
     bottom = turned(from_s[chans : 2 * chans], flags[1])
-    shifted(out, centre, top, bottom, west, east, upper, lower)
+    shifted(out, centre, top, bottom, west, east, (upper, lower))
 
 
 def conv(weight, pads):
     total = None
-    for tap in range(9):
-        r, s = divmod(tap, 3)
-        term = dot(weight[tap], pads[s, :, r * LANES : r * LANES + CELLS])
+    for r in range(3):
+        taps = jnp.concatenate([weight[3 * r + s] for s in range(3)], 1)
+        term = dot(taps, pads[:, r * LANES : r * LANES + CELLS])
         total = term if total is None else total + term
     return total
 
 
 def conv_adjoint(weight, pads, flags, halo):
     total = None
-    for tap in range(9):
-        r, s = divmod(tap, 3)
+    for r in range(3):
         start = (2 - r) * LANES
+        taps = jnp.concatenate([weight[3 * r + s] for s in range(3)], 0)
         term = lax.dot_general(
-            weight[tap], pads[2 - s, :, start : start + CELLS], TN, preferred_element_type=F32
+            taps, pads[:, start : start + CELLS], TN, preferred_element_type=F32
         )
         total = term if total is None else total + term
     chans = total.shape[0]
@@ -227,16 +228,16 @@
 
 def grad_kernel(grad_tile, pads, keep, away, both):
     core = lax.rem(lax.axis_index("dp"), 2)
-    for tap in range(9):
-        r, s = divmod(tap, 3)
-        term = lax.dot_general(
-            grad_tile[...], pads[s, :, r * LANES : r * LANES + CELLS], NT, preferred_element_type=F32
+    chans = grad_tile.shape[0]
+    for r in range(3):
+        terms = lax.dot_general(
+            grad_tile[...], pads[:, r * LANES : r * LANES + CELLS], NT, preferred_element_type=F32
         )
-        chans = term.shape[0]
-        for part in range(2):
-            half, group = divmod(2 * tap + part, 9)
+        for piece in range(6):
+            half, group = divmod(6 * r + piece, 9)
             place = core if half == 0 else 1 - core
-            both[place, group * chans : (group + 1) * chans] = term[:, part * LANES : (part + 1) * LANES]
+            rows = slice(group * chans, (group + 1) * chans)
+            both[place, rows] = terms[:, piece * LANES : (piece + 1) * LANES]
     keep[...] = both[0]
     away[...] = both[1].astype(BF16)
 
@@ -263,7 +264,7 @@
 
 
 def finish_kernel(own, near, far, *refs):
-    outs, (flat, stage, sems) = (refs[-5:-3], refs[-3:])
+    outs, (flat, stage, sems, got) = (refs[-6:-4], refs[-4:])
     place = lax.axis_index("dp")
     side, core = (lax.shift_right_logical(place, 1), lax.rem(place, 2))
     half = core if own else 1 - core
@@ -271,12 +272,21 @@
     tiles, depth = near.shape[:2]
     depth = depth // 2
     size = tiles * depth
+    loads = []
     for which in range(2):
         for tile in range(tiles):
-            rows = slice(which * depth, (which + 1) * depth)
-            for ref, to in ((near, side), (far, 1 - side)):
+            for index, (ref, to) in enumerate(((near, side), (far, 1 - side))):
                 start = pl.multiple_of(to * size + tile * depth, 16)
-                flat[which, pl.ds(start, depth)] = ref[tile, rows, :]
+                loads.append(
+                    pltpu.make_async_copy(
+                        ref.at[tile, pl.ds(which * depth, depth), :],
+                        flat.at[which, pl.ds(start, depth), :],
+                        got.at[which, tile, index],
+                    )
+                )
+                loads[-1].start()
+    for load in loads:
+        load.wait()
 
     def place_half(odd):
         copies = []
@@ -317,13 +327,14 @@
     return pl.pallas_call(
         functools.partial(finish_kernel, own),
         out_shape=(grad, grad),
-        in_specs=[VMEM, VMEM] + [ANY] * len(partial),
+        in_specs=[ANY, ANY] + [ANY] * len(partial),
         out_specs=(ANY, ANY),
         input_output_aliases={2 + k: k for k in range(len(partial))},
         scratch_shapes=[
             pltpu.VMEM((2, 9 * chans, LANES), BF16),
             pltpu.VMEM((2, 5, chans, chans), F32),
             pltpu.SemaphoreType.DMA((2, 5)),
+            pltpu.SemaphoreType.DMA((2, near.shape[0], 2)),
         ],
         compiler_params=pltpu.CompilerParams(vmem_limit_bytes=56 * 1024 * 1024),
     )(near, far, *partial)
@@ -431,8 +442,8 @@
     chans = fields.shape[1]
     tile = struct(chans, ROWS, LANES)
     flat = struct(chans, CELLS)
-    pads = struct(3, chans, PADDED)
-    scratch = [pltpu.VMEM((3, chans, PADDED), BF16)]
+    pads = struct(3 * chans, PADDED)
+    scratch = [pltpu.VMEM((3 * chans, PADDED), BF16)]
     field, cot, *rim = call(
         prepare_kernel,
         (flat, flat) + rim_shapes(chans),

time: 172 us -> 173 us (level)
  no operation moved by 1% of the time
where the time goes in v6:
time: 173 us; the launch traced here: 172 us
  blocking collectives  52.9 us (31%)
  starting transfers between devices  42.7 us (25%)
  Pallas kernels  41.1 us (24%)
  waiting for transfers between devices  28.3 us (16%)
  local copies, waits for them, and re-layouts  3.66 us (2%)
  other arithmetic  2.13 us (1%)
    all_to_all x4, blocking collectives, over(): return lax.all_to_all(value, axis, 0, 0)  52.9 us
    pallas_call x6, Pallas kernels, call(): pl.pallas_call(kernel, out_shape=out_shape, in_specs=([SMEM] if flags els...  32.4 us
    ppermute x4, starting transfers between devices, paired(): return lax.ppermute(value, 'dp', [(0, 1), (1, 0), (2, 3), (3, 2)])  18.7 us
    ppermute x3, waiting for transfers between devices, beside(): return lax.ppermute(value, 'dp', [(i, (i + 2) % 4) for i in range(4)])  13.7 us
    ppermute x4, waiting for transfers between devices, across(): lax.ppermute(value, 'lat', [(i, i + step) for i in range(lats) if 0 <= i...  12.2 us
    ppermute x4, starting transfers between devices, across(): lax.ppermute(value, 'lat', [(i, i + step) for i in range(lats) if 0 <= i...  11.4 us
    ppermute x4, starting transfers between devices, along(): lax.ppermute(value, 'lon', [(i, (i + step) % lons) for i in range(lons)])  9.54 us
    pallas_call x2, Pallas kernels, finish(): pl.pallas_call(functools.partial(finish_kernel, own), out_shape=(grad, gr...  5.97 us
  transfers between devices with their start and end apart: 15, of which 9 were waited for; matrix products, arithmetic and copies ran while one was open for 1% of the time, Pallas kernels for 12%

profile of v6, /device:TPU:1, one launch (start us, length us, event | category | flops | bytes accessed | tf_op | source)
XLA Modules:
  0.0 171.7 jit_solution(1188916510571833027)
XLA Ops:
  0.6 3.8 %shard_map.84 = (bf16[256,1024]{1,0:T(8,128)(2,1)}, bf16[256,1024]{1,0:T(8,128)(2,1)}, bf16[32,256]{1,0:T(8,128)(2,1)}, bf16[32,256]{1,0:T(8,128)(2,1)}, bf16[54...) custom-call(s32[7,8]{1,0:T(8,128)} %flips.7, bf16[256,8,128]{2,1,0:T(8,128)(2,1)} %bitcast.8, bf16[256,8,128]{2,1,0:T(8,128)(2,1)} %bitcast.9), custom_call_target="tpu_custom_call" | custom-call | tf_op jit(solution)/shard_map/pallas_call | solution.py:349
  4.4 2.5 %collective-permute-start = (bf16[32,256]{1,0:T(8,128)(2,1)}, bf16[32,256]{1,0:T(8,128)(2,1)S(1)}, u32[]{:S(2)}, u32[]{:S(2)}) collective-permute-start(bf16[32,256]{1,0:T(8,128)(2,1)} %get-tuple-element.32), channel_id=1, source_target_pairs={{0,32},{32,64},{64,96},{96,128},{128,160},{160,192},{192,224},{224... | collective-permute-start | bytes 49160 | tf_op jit(solution)/shard_map/ppermute | solution.py:374
  6.9 4.0 %collective-permute-start.1 = (bf16[32,256]{1,0:T(8,128)(2,1)}, bf16[32,256]{1,0:T(8,128)(2,1)S(1)}, u32[]{:S(2)}, u32[]{:S(2)}) collective-permute-start(bf16[32,256]{1,0:T(8,128)(2,1)} %get-tuple-element.33), channel_id=1, source_target_pairs={{0,224},{32,0},{64,32},{96,64},{128,96},{160,128},{192,160},{224,1... | collective-permute-start | bytes 49160 | tf_op jit(solution)/shard_map/ppermute | solution.py:374
  10.9 1.3 collective-permute-done.from_w.refs_0_
  12.7 1.4 join.2
  14.1 4.8 %collective-permute-start.2 = (bf16[544,128]{1,0:T(8,128)(2,1)}, bf16[544,128]{1,0:T(8,128)(2,1)S(1)}, u32[]{:S(2)}, u32[]{:S(2)}) collective-permute-start(bf16[544,128]{1,0:T(8,128)(2,1)} %get-tuple-element.36), channel_id=1, source_target_pairs={{0,4},{4,8},{8,12},{12,16},{16,20},{20,24},{24,28},{1,5},{5,9},{9,... | collective-permute-start | bytes 417800 | tf_op jit(solution)/shard_map/ppermute | solution.py:377
  18.9 1.3 collective-permute-start.3
  21.3 5.2 %collective-permute-done.3.refs_3_ = bf16[544,128]{1,0:T(8,128)(2,1)S(1)} collective-permute-done((bf16[544,128]{1,0:T(8,128)(2,1)}, bf16[544,128]{1,0:T(8,128)(2,1)S(1)}, u32[]{:S(2)}, u32[]{:S(2)}) %collective-permute-start.3) | collective-permute-done | bytes 139296 | tf_op jit(solution)/shard_map/ppermute | solution.py:377
  27.1 7.8 %shard_map.85 = (bf16[256,1024]{1,0:T(8,128)(2,1)}, bf16[256,1024]{1,0:T(8,128)(2,1)}, bf16[768,1280]{1,0:T(8,128)(2,1)}, bf16[32,256]{1,0:T(8,128)(2,1)}, bf16[...) custom-call(s32[7,8]{1,0:T(8,128)} %flips.7, bf16[256,1024]{1,0:T(8,128)(2,1)} %get-tuple-element.30.field, ...), custom_call_target="tpu_custom_call" | custom-call | tf_op jit(solution)/shard_map/pallas_call | solution.py:349
  34.9 4.8 %shard_map.89 = (f32[2304,128]{1,0:T(8,128)}, bf16[2304,128]{1,0:T(8,128)(2,1)}) custom-call(bf16[256,1024]{1,0:T(8,128)(2,1)} %get-tuple-element.46.back.grad_tile, bf16[768,1280]{1,0:T(8,128)(2,1)} %get-tuple-element.47.pads), custom_call_target="tpu_custom_call" | custom-call | tf_op jit(solution)/shard_map/pallas_call | solution.py:349
  39.7 3.0 %collective-permute-start.8 = (bf16[2304,128]{1,0:T(8,128)(2,1)}, bf16[2304,128]{1,0:T(8,128)(2,1)S(1)}, u32[]{:S(2)}, u32[]{:S(2)}) collective-permute-start(bf16[2304,128]{1,0:T(8,128)(2,1)} %get-tuple-element.49), channel_id=1, source_target_pairs={{0,1},{1,0},{2,3},{3,2},{4,5},{5,4},{6,7},{7,6},{8,9},{9,8},{10,11... | collective-permute-start | bytes 1769480 | tf_op jit(solution)/shard_map/ppermute | solution.py:402
  42.6 3.1 %collective-permute-start.5 = (bf16[32,256]{1,0:T(8,128)(2,1)S(1)}, bf16[32,256]{1,0:T(8,128)(2,1)S(1)}, u32[]{:S(2)}, u32[]{:S(2)}) collective-permute-start(bf16[32,256]{1,0:T(8,128)(2,1)S(1)} %copy-done.14), channel_id=1, source_target_pairs={{0,224},{32,0},{64,32},{96,64},{128,96},{160,128},{192,160},{224,1... | collective-permute-start | bytes 49160 | tf_op jit(solution)/shard_map/ppermute | solution.py:374
  47.4 1.4 join.3
  48.7 3.8 %collective-permute-start.6 = (bf16[544,128]{1,0:T(8,128)(2,1)}, bf16[544,128]{1,0:T(8,128)(2,1)S(1)}, u32[]{:S(2)}, u32[]{:S(2)}) collective-permute-start(bf16[544,128]{1,0:T(8,128)(2,1)} %get-tuple-element.43), channel_id=1, source_target_pairs={{0,4},{4,8},{8,12},{12,16},{16,20},{20,24},{24,28},{1,5},{5,9},{9,... | collective-permute-start | bytes 417800 | tf_op jit(solution)/shard_map/ppermute | solution.py:377
  52.5 1.5 collective-permute-start.7
  54.9 5.2 %collective-permute-done.7.refs_3_ = bf16[544,128]{1,0:T(8,128)(2,1)S(1)} collective-permute-done((bf16[544,128]{1,0:T(8,128)(2,1)}, bf16[544,128]{1,0:T(8,128)(2,1)S(1)}, u32[]{:S(2)}, u32[]{:S(2)}) %collective-permute-start.7) | collective-permute-done | bytes 139296 | tf_op jit(solution)/shard_map/ppermute | solution.py:377
  60.7 4.8 %shard_map.86 = (bf16[768,1280]{1,0:T(8,128)(2,1)}, f32[2304,128]{1,0:T(8,128)}, bf16[2304,128]{1,0:T(8,128)(2,1)}) custom-call(s32[7,8]{1,0:T(8,128)} %flips.7, bf16[256,1024]{1,0:T(8,128)(2,1)} %get-tuple-element.38.act, bf16[256,1024]{1,0:T(8,128)(2,1)} %get-tuple-element.31.cotangent, bf16[32,256]{1,0:T(8,128)(2,1)} %copy-done.8, ...), custom_call_target="tpu_custom_call" | custom-call | tf_op jit(solution)/shard_map/pallas_call | solution.py:349
  65.5 2.4 %collective-permute-start.10 = (bf16[2304,128]{1,0:T(8,128)(2,1)}, bf16[2304,128]{1,0:T(8,128)(2,1)S(1)}, u32[]{:S(2)}, u32[]{:S(2)}) collective-permute-start(bf16[2304,128]{1,0:T(8,128)(2,1)} %get-tuple-element.51), channel_id=1, source_target_pairs={{0,1},{1,0},{2,3},{3,2},{4,5},{5,4},{6,7},{7,6},{8,9},{9,8},{10,11... | collective-permute-start | bytes 1769480 | tf_op jit(solution)/shard_map/ppermute | solution.py:402
  68.7 1.3 collective-permute-start.9
  71.2 6.3 %collective-permute-done.9 = bf16[1152,128]{1,0:T(8,128)(2,1)} collective-permute-done((bf16[1152,128]{1,0:T(8,128)(2,1)}, bf16[1152,128]{1,0:T(8,128)(2,1)}, u32[]{:S(2)}, u32[]{:S(2)}) %collective-permute-start.9) | collective-permute-done | bytes 294944 | tf_op jit(solution)/shard_map/ppermute | solution.py:398
  78.6 5.1 %collective-permute-done.11 = bf16[1152,128]{1,0:T(8,128)(2,1)S(1)} collective-permute-done((bf16[1152,128]{1,0:T(8,128)(2,1)S(1)}, bf16[1152,128]{1,0:T(8,128)(2,1)S(1)}, u32[]{:S(2)}, u32[]{:S(2)}) %collective-permute-start.11) | collective-permute-done | bytes 294944 | tf_op jit(solution)/shard_map/ppermute | solution.py:398
  83.9 16.9 %all_to_all.20 = bf16[8,288,128]{2,1,0:T(8,128)(2,1)S(1)} all-to-all(bf16[8,288,128]{2,1,0:T(8,128)(2,1)S(1)} %pad_maximum_fusion), channel_id=1, replica_groups=mesh['lon'=8,'lat'=8,'dp'=4] {'lat'}, dimensions={0} | all-to-all | bytes 1179648 | tf_op jit(solution)/shard_map/all_to_all | solution.py:406
  100.9 14.3 %all_to_all.21 = f32[8,36,128]{2,1,0:T(8,128)S(1)} all-to-all(f32[8,36,128]{2,1,0:T(8,128)S(1)} %reshape.39), channel_id=1, replica_groups=mesh['lon'=8,'lat'=8,'dp'=4] {'lon'}, dimensions={0} | all-to-all | bytes 294912 | tf_op jit(solution)/shard_map/all_to_all | solution.py:406
  115.2 9.8 %all_to_all.22 = bf16[8,36,128]{2,1,0:T(8,128)(2,1)S(1)} all-to-all(bf16[8,36,128]{2,1,0:T(8,128)(2,1)S(1)} %broadcast_in_dim.6), channel_id=1, replica_groups=mesh['lon'=8,'lat'=8,'dp'=4] {'lon'}, dimensions={0} | all-to-all | bytes 147456 | tf_op jit(solution)/shard_map/all_to_all | solution.py:406
  125.1 11.9 %all_to_all.23.near = bf16[8,288,128]{2,1,0:T(8,128)(2,1)S(1)} all-to-all(bf16[8,288,128]{2,1,0:T(8,128)(2,1)S(1)} %broadcast_in_dim.15), channel_id=1, replica_groups=mesh['lon'=8,'lat'=8,'dp'=4] {'lat'}, dimensions={0} | all-to-all | bytes 1179648 | tf_op jit(solution)/shard_map/all_to_all | solution.py:406
  137.7 6.3 %collective-permute-start.12 = (bf16[8,288,128]{2,1,0:T(8,128)(2,1)S(1)}, bf16[8,288,128]{2,1,0:T(8,128)(2,1)S(1)}, u32[]{:S(2)}, u32[]{:S(2)}) collective-permute-start(bf16[8,288,128]{2,1,0:T(8,128)(2,1)S(1)} %all_to_all.23.near), channel_id=1, source_target_pairs={{0,1},{1,0},{2,3},{3,2},{4,5},{5,4},{6,7},{7,6},{8,9},{9,8},{10,11... | collective-permute-start | bytes 1769480 | tf_op jit(solution)/shard_map/ppermute | solution.py:402
  144.0 2.2 %collective-permute-done.13.far = bf16[8,288,128]{2,1,0:T(8,128)(2,1)S(1)} collective-permute-done((bf16[8,288,128]{2,1,0:T(8,128)(2,1)S(1)}, bf16[8,288,128]{2,1,0:T(8,128)(2,1)S(1)}, u32[]{:S(2)}, u32[]{:S(2)}) %collective-permute-start.13) | collective-permute-done | bytes 589856 | tf_op jit(solution)/shard_map/ppermute | solution.py:398
  146.2 7.0 %collective-permute-start.14 = (bf16[8,288,128]{2,1,0:T(8,128)(2,1)S(1)}, bf16[8,288,128]{2,1,0:T(8,128)(2,1)S(1)}, u32[]{:S(2)}, u32[]{:S(2)}) collective-permute-start(bf16[8,288,128]{2,1,0:T(8,128)(2,1)S(1)} %collective-permute-done.13.far), channel_id=1, source_target_pairs={{0,1},{1,0},{2,3},{3,2},{4,5},{5,4},{6,7},{7,6},{8,9},{9,8},{10,11... | collective-permute-start | bytes 1769480 | tf_op jit(solution)/shard_map/ppermute | solution.py:402
  153.2 5.4 %shard_map.87 = bf16[256,8,128]{2,1,0:T(8,128)(2,1)} custom-call(bf16[256,1024]{1,0:T(8,128)(2,1)} %get-tuple-element.30.field, bf16[9,256,256]{2,1,0:T(8,128)(2,1)} %weight.2, bf16[768,1280]{1,0:T(8,128)(2,1)} %get-tuple-element.45.pads), custom_call_target="tpu_custom_call" | custom-call | tf_op jit(solution)/shard_map/pallas_call | solution.py:349
  158.6 5.9 %shard_map.88 = bf16[256,8,128]{2,1,0:T(8,128)(2,1)} custom-call(s32[7,8]{1,0:T(8,128)} %flips.7, bf16[256,1024]{1,0:T(8,128)(2,1)} %get-tuple-element.31.cotangent, bf16[256,1024]{1,0:T(8,128)(2,1)} %get-tuple-element.46.back.grad_tile, bf16[9,256,256]{2,1,0:T(8,128)(2,1)} %weight.3, bf16[32,256]{1,0:T(8,128)(2,1)} %copy-done.8, bf16[32,256]{1,0:T(8,128)(2,1)} %copy-done.9, ...), custom_call_target="tpu_custom_call" | custom-call | tf_op jit(solution)/shard_map/pallas_call | solution.py:349
  164.5 3.0 %shard_map.90 = (f32[9,256,256]{2,1,0:T(8,128)}, f32[9,256,256]{2,1,0:T(8,128)}) custom-call(bf16[8,288,128]{2,1,0:T(8,128)(2,1)} %copy-done, bf16[8,288,128]{2,1,0:T(8,128)(2,1)} %copy-done.5), custom_call_target="tpu_custom_call" | custom-call | tf_op jit(solution)/shard_map/pallas_call | solution.py:327
  168.6 3.0 %shard_map.91 = (f32[9,256,256]{2,1,0:T(8,128)}, f32[9,256,256]{2,1,0:T(8,128)}) custom-call(bf16[8,288,128]{2,1,0:T(8,128)(2,1)} %copy-done.3, bf16[8,288,128]{2,1,0:T(8,128)(2,1)} %copy-done.4, f32[9,256,256]{2,1,0:T(8,128)} %get-tuple-element.52.refs_0_, f32[9,256,256]{2,1,0:T(8,128)} %get-tuple-element.53.refs_1_), custom_call_target="tpu_custom_call", output_to_operand_aliasing={{0}: (2, {}), {1}: (3, {})} | custom-call | tf_op jit(solution)/shard_map/pallas_call | solution.py:327
  (55 shorter events, 10.5 us)
Async XLA Ops:
  4.4 7.7 %collective-permute-start = (bf16[32,256]{1,0:T(8,128)(2,1)}, bf16[32,256]{1,0:T(8,128)(2,1)S(1)}, u32[]{:S(2)}, u32[]{:S(2)}) collective-permute-start(bf16[32,256]{1,0:T(8,128)(2,1)} %get-tuple-element.32), channel_id=1, source_target_pairs={{0,32},{32,64},{64,96},{96,128},{128,160},{160,192},{192,224},{224... | collective-permute-start | bytes 49160 | tf_op jit(solution)/shard_map/ppermute | solution.py:374
  6.9 5.3 %collective-permute-start.1 = (bf16[32,256]{1,0:T(8,128)(2,1)}, bf16[32,256]{1,0:T(8,128)(2,1)S(1)}, u32[]{:S(2)}, u32[]{:S(2)}) collective-permute-start(bf16[32,256]{1,0:T(8,128)(2,1)} %get-tuple-element.33), channel_id=1, source_target_pairs={{0,224},{32,0},{64,32},{96,64},{128,96},{160,128},{192,160},{224,1... | collective-permute-start | bytes 49160 | tf_op jit(solution)/shard_map/ppermute | solution.py:374
  12.1 0.6 copy-start.12
  12.1 0.6 copy-start.13
  14.1 7.1 %collective-permute-start.2 = (bf16[544,128]{1,0:T(8,128)(2,1)}, bf16[544,128]{1,0:T(8,128)(2,1)S(1)}, u32[]{:S(2)}, u32[]{:S(2)}) collective-permute-start(bf16[544,128]{1,0:T(8,128)(2,1)} %get-tuple-element.36), channel_id=1, source_target_pairs={{0,4},{4,8},{8,12},{12,16},{16,20},{20,24},{24,28},{1,5},{5,9},{9,... | collective-permute-start | bytes 417800 | tf_op jit(solution)/shard_map/ppermute | solution.py:377
  18.9 7.5 %collective-permute-start.3 = (bf16[544,128]{1,0:T(8,128)(2,1)}, bf16[544,128]{1,0:T(8,128)(2,1)S(1)}, u32[]{:S(2)}, u32[]{:S(2)}) collective-permute-start(bf16[544,128]{1,0:T(8,128)(2,1)} %get-tuple-element.37), channel_id=1, source_target_pairs={{4,0},{8,4},{12,8},{16,12},{20,16},{24,20},{28,24},{5,1},{9,5},{13... | collective-permute-start | bytes 417800 | tf_op jit(solution)/shard_map/ppermute | solution.py:377
  21.3 5.2 %copy-start.10 = (bf16[544,128]{1,0:T(8,128)(2,1)}, bf16[544,128]{1,0:T(8,128)(2,1)S(1)}, u32[]{:S(2)}) copy-start(bf16[544,128]{1,0:T(8,128)(2,1)S(1)} %collective-permute-done.2.refs_2_) | copy-start | bytes 417796
  26.5 0.6 copy-start.11
  34.9 7.8 %copy-start.15 = (bf16[32,256]{1,0:T(8,128)(2,1)S(1)}, bf16[32,256]{1,0:T(8,128)(2,1)}, u32[]{:S(2)}) copy-start(bf16[32,256]{1,0:T(8,128)(2,1)} %get-tuple-element.39) | copy-start | bytes 49156
  34.9 7.8 %copy-start.14 = (bf16[32,256]{1,0:T(8,128)(2,1)S(1)}, bf16[32,256]{1,0:T(8,128)(2,1)}, u32[]{:S(2)}) copy-start(bf16[32,256]{1,0:T(8,128)(2,1)} %get-tuple-element.40) | copy-start | bytes 49156
  39.7 28.2 %copy-start.1 = (f32[2304,128]{1,0:T(8,128)S(1)}, f32[2304,128]{1,0:T(8,128)}, u32[]{:S(2)}) copy-start(f32[2304,128]{1,0:T(8,128)} %get-tuple-element.48) | copy-start | bytes 3538948
  39.7 28.2 %collective-permute-start.8 = (bf16[2304,128]{1,0:T(8,128)(2,1)}, bf16[2304,128]{1,0:T(8,128)(2,1)S(1)}, u32[]{:S(2)}, u32[]{:S(2)}) collective-permute-start(bf16[2304,128]{1,0:T(8,128)(2,1)} %get-tuple-element.49), channel_id=1, source_target_pairs={{0,1},{1,0},{2,3},{3,2},{4,5},{5,4},{6,7},{7,6},{8,9},{9,8},{10,11... | collective-permute-start | bytes 1769480 | tf_op jit(solution)/shard_map/ppermute | solution.py:402
  42.6 4.1 %collective-permute-start.4 = (bf16[32,256]{1,0:T(8,128)(2,1)S(1)}, bf16[32,256]{1,0:T(8,128)(2,1)S(1)}, u32[]{:S(2)}, u32[]{:S(2)}) collective-permute-start(bf16[32,256]{1,0:T(8,128)(2,1)S(1)} %copy-done.15), channel_id=1, source_target_pairs={{0,32},{32,64},{64,96},{96,128},{128,160},{160,192},{192,224},{224... | collective-permute-start | bytes 49160 | tf_op jit(solution)/shard_map/ppermute | solution.py:374
  42.6 4.1 %collective-permute-start.5 = (bf16[32,256]{1,0:T(8,128)(2,1)S(1)}, bf16[32,256]{1,0:T(8,128)(2,1)S(1)}, u32[]{:S(2)}, u32[]{:S(2)}) collective-permute-start(bf16[32,256]{1,0:T(8,128)(2,1)S(1)} %copy-done.14), channel_id=1, source_target_pairs={{0,224},{32,0},{64,32},{96,64},{128,96},{160,128},{192,160},{224,1... | collective-permute-start | bytes 49160 | tf_op jit(solution)/shard_map/ppermute | solution.py:374
  46.8 0.6 copy-start.8
  46.8 0.6 copy-start.9
  48.7 6.1 %collective-permute-start.6 = (bf16[544,128]{1,0:T(8,128)(2,1)}, bf16[544,128]{1,0:T(8,128)(2,1)S(1)}, u32[]{:S(2)}, u32[]{:S(2)}) collective-permute-start(bf16[544,128]{1,0:T(8,128)(2,1)} %get-tuple-element.43), channel_id=1, source_target_pairs={{0,4},{4,8},{8,12},{12,16},{16,20},{20,24},{24,28},{1,5},{5,9},{9,... | collective-permute-start | bytes 417800 | tf_op jit(solution)/shard_map/ppermute | solution.py:377
  52.5 7.5 %collective-permute-start.7 = (bf16[544,128]{1,0:T(8,128)(2,1)}, bf16[544,128]{1,0:T(8,128)(2,1)S(1)}, u32[]{:S(2)}, u32[]{:S(2)}) collective-permute-start(bf16[544,128]{1,0:T(8,128)(2,1)} %get-tuple-element.44), channel_id=1, source_target_pairs={{4,0},{8,4},{12,8},{16,12},{20,16},{24,20},{28,24},{5,1},{9,5},{13... | collective-permute-start | bytes 417800 | tf_op jit(solution)/shard_map/ppermute | solution.py:377
  54.8 5.2 %copy-start.6 = (bf16[544,128]{1,0:T(8,128)(2,1)}, bf16[544,128]{1,0:T(8,128)(2,1)S(1)}, u32[]{:S(2)}) copy-start(bf16[544,128]{1,0:T(8,128)(2,1)S(1)} %collective-permute-done.6.refs_2_) | copy-start | bytes 417796
  60.0 0.7 copy-start.7
  65.5 4.5 %copy-start.2 = (f32[2304,128]{1,0:T(8,128)S(1)}, f32[2304,128]{1,0:T(8,128)}, u32[]{:S(2)}) copy-start(f32[2304,128]{1,0:T(8,128)} %get-tuple-element.50) | copy-start | bytes 3538948
  65.5 4.5 %collective-permute-start.10 = (bf16[2304,128]{1,0:T(8,128)(2,1)}, bf16[2304,128]{1,0:T(8,128)(2,1)S(1)}, u32[]{:S(2)}, u32[]{:S(2)}) collective-permute-start(bf16[2304,128]{1,0:T(8,128)(2,1)} %get-tuple-element.51), channel_id=1, source_target_pairs={{0,1},{1,0},{2,3},{3,2},{4,5},{5,4},{6,7},{7,6},{8,9},{9,8},{10,11... | collective-permute-start | bytes 1769480 | tf_op jit(solution)/shard_map/ppermute | solution.py:402
  68.7 8.9 %collective-permute-start.9 = (bf16[1152,128]{1,0:T(8,128)(2,1)}, bf16[1152,128]{1,0:T(8,128)(2,1)}, u32[]{:S(2)}, u32[]{:S(2)}) collective-permute-start(bf16[1152,128]{1,0:T(8,128)(2,1)} %add_convert_fusion.3), channel_id=1, source_target_pairs={{0,2},{1,3},{2,0},{3,1},{4,6},{5,7},{6,4},{7,5},{8,10},{9,11},{10,... | collective-permute-start | bytes 884744 | tf_op jit(solution)/shard_map/ppermute | solution.py:398
  70.0 13.7 %collective-permute-start.11 = (bf16[1152,128]{1,0:T(8,128)(2,1)S(1)}, bf16[1152,128]{1,0:T(8,128)(2,1)S(1)}, u32[]{:S(2)}, u32[]{:S(2)}) collective-permute-start(bf16[1152,128]{1,0:T(8,128)(2,1)S(1)} %add_convert_fusion.1), channel_id=1, source_target_pairs={{0,2},{1,3},{2,0},{3,1},{4,6},{5,7},{6,4},{7,5},{8,10},{9,11},{10,... | collective-permute-start | bytes 884744 | tf_op jit(solution)/shard_map/ppermute | solution.py:398
  137.0 21.6 %copy-start = (bf16[8,288,128]{2,1,0:T(8,128)(2,1)}, bf16[8,288,128]{2,1,0:T(8,128)(2,1)S(1)}, u32[]{:S(2)}) copy-start(bf16[8,288,128]{2,1,0:T(8,128)(2,1)S(1)} %all_to_all.23.near) | copy-start | bytes 1769476
  137.0 9.2 %collective-permute-start.13 = (bf16[8,288,128]{2,1,0:T(8,128)(2,1)S(1)}, bf16[8,288,128]{2,1,0:T(8,128)(2,1)S(1)}, u32[]{:S(2)}, u32[]{:S(2)}) collective-permute-start(bf16[8,288,128]{2,1,0:T(8,128)(2,1)S(1)} %all_to_all.23.near), channel_id=1, source_target_pairs={{0,2},{1,3},{2,0},{3,1},{4,6},{5,7},{6,4},{7,5},{8,10},{9,11},{10,... | collective-permute-start | bytes 1769480 | tf_op jit(solution)/shard_map/ppermute | solution.py:398
  137.7 29.8 %collective-permute-start.12 = (bf16[8,288,128]{2,1,0:T(8,128)(2,1)S(1)}, bf16[8,288,128]{2,1,0:T(8,128)(2,1)S(1)}, u32[]{:S(2)}, u32[]{:S(2)}) collective-permute-start(bf16[8,288,128]{2,1,0:T(8,128)(2,1)S(1)} %all_to_all.23.near), channel_id=1, source_target_pairs={{0,1},{1,0},{2,3},{3,2},{4,5},{5,4},{6,7},{7,6},{8,9},{9,8},{10,11... | collective-permute-start | bytes 1769480 | tf_op jit(solution)/shard_map/ppermute | solution.py:402
  146.2 12.4 %copy-start.5 = (bf16[8,288,128]{2,1,0:T(8,128)(2,1)}, bf16[8,288,128]{2,1,0:T(8,128)(2,1)S(1)}, u32[]{:S(2)}) copy-start(bf16[8,288,128]{2,1,0:T(8,128)(2,1)S(1)} %collective-permute-done.13.far) | copy-start | bytes 1769476
  146.2 21.3 %collective-permute-start.14 = (bf16[8,288,128]{2,1,0:T(8,128)(2,1)S(1)}, bf16[8,288,128]{2,1,0:T(8,128)(2,1)S(1)}, u32[]{:S(2)}, u32[]{:S(2)}) collective-permute-start(bf16[8,288,128]{2,1,0:T(8,128)(2,1)S(1)} %collective-permute-done.13.far), channel_id=1, source_target_pairs={{0,1},{1,0},{2,3},{3,2},{4,5},{5,4},{6,7},{7,6},{8,9},{9,8},{10,11... | collective-permute-start | bytes 1769480 | tf_op jit(solution)/shard_map/ppermute | solution.py:402
  167.5 0.8 copy-start.3
  167.6 1.0 copy-start.4

commit v7 on v6

--- a/solution.py
+++ b/solution.py
@@ -108,10 +108,10 @@
     return dot(line, turn)
 
 
-def shifted(out, centre, top, bottom, west, east, swaps=(None, None)):
+def shifted(out, centre, top, bottom, west, east, swaps=(None, None), edges=False):
     swap_top, swap_bottom = swaps
+    chans = west.shape[1]
     order = (0, 1, 2) if swap_top is None else (2, 1, 0)
-    chans = centre.shape[0]
     k, lane = (iota((16, PADDED), 0), iota((16, PADDED), 1))
     placed_west = lax.dot_general(
         west, one_hot(lane == k * LANES), TN, preferred_element_type=F32
@@ -120,8 +120,12 @@
         east, one_hot(lane == k * LANES + LANES - 1), TN, preferred_element_type=F32
     )
     lane_in = iota((chans, LANES), 1)
-    for block in range(ROWS + 2):
+    for block in (0, ROWS + 1) if edges else range(ROWS + 2):
         span = slice(block * LANES, (block + 1) * LANES)
+        to = slice(LANES, 2 * LANES) if edges and block else span
+        if top is None and block in (0, ROWS + 1):
+            out[:, span] = jnp.zeros((3 * chans, LANES), BF16)
+            continue
         if block == 0:
             line = top
         elif block == ROWS + 1:
@@ -134,36 +138,49 @@
         if swap is not None:
             left, right = (jnp.where(swap, right, left), jnp.where(swap, left, right))
         for slot, cells in zip(order, (left, line, right)):
-            out[slot * chans : (slot + 1) * chans, span] = cells.astype(BF16)
+            out[slot * chans : (slot + 1) * chans, to] = cells.astype(BF16)
 
 
 def lines(top, mid, bottom):
     return jnp.concatenate([top, mid, bottom, jnp.zeros((6, mid.shape[1]), F32)], 0).astype(BF16)
 
 
-def pad_forward(out, centre, flags, halo):
+def pad_forward(out, centre, flags, halo, part=None):
     from_w, from_e, from_n, from_s = halo
-    chans = centre.shape[0]
+    chans = out.shape[0] // 3
+    sides = [jnp.zeros((ROWS, chans), F32)] * 2
+    if part != "edges":
+        sides = [ref[...].astype(F32)[:ROWS] for ref in (from_w, from_e)]
+    if part == "inner":
+        none = jnp.zeros((1, chans), F32)
+        west, east = (lines(none, side, none) for side in sides)
+        shifted(out, centre, None, None, west, east)
+        return
     upper, lower = (flags[0] == 1, flags[1] == 1)
     above, below = (corners_of(ref, chans).astype(F32) for ref in (from_n, from_s))
     nw, ne, sw, se = (above[:1], above[2:3], below[:1], below[2:3])
-    west = lines(jnp.where(upper, ne, nw), from_w[...].astype(F32)[:ROWS], jnp.where(lower, se, sw))
-    east = lines(jnp.where(upper, nw, ne), from_e[...].astype(F32)[:ROWS], jnp.where(lower, sw, se))
+    west = lines(jnp.where(upper, ne, nw), sides[0], jnp.where(lower, se, sw))
+    east = lines(jnp.where(upper, nw, ne), sides[1], jnp.where(lower, sw, se))
     top = turned(from_n[:chans], flags[0])
     bottom = turned(from_s[:chans], flags[1])
-    shifted(out, centre, top, bottom, west, east)
-
-
-def pad_backward(out, centre, flags, halo):
+    shifted(out, centre, top, bottom, west, east, edges=part == "edges")
+
+
+def pad_backward(out, centre, flags, halo, part=None):
     from_w, from_e, from_n, from_s = halo
-    chans = centre.shape[0]
+    chans = out.shape[0] // 3
+    none = jnp.zeros((1, chans), F32)
+    sides = [jnp.zeros((ROWS, chans), F32)] * 2
+    if part != "edges":
+        sides = [ref[...].astype(F32)[ROWS : 2 * ROWS] for ref in (from_w, from_e)]
+    west, east = (lines(none, side, none) for side in sides)
+    if part == "inner":
+        shifted(out, centre, None, None, west, east, (False, False))
+        return
     upper, lower = (flags[0] == 1, flags[1] == 1)
-    none = jnp.zeros((1, chans), F32)
-    west = lines(none, from_w[...].astype(F32)[ROWS : 2 * ROWS], none)
-    east = lines(none, from_e[...].astype(F32)[ROWS : 2 * ROWS], none)
     top = turned(from_n[chans : 2 * chans], flags[0])
     bottom = turned(from_s[chans : 2 * chans], flags[1])
-    shifted(out, centre, top, bottom, west, east, (upper, lower))
+    shifted(out, centre, top, bottom, west, east, (upper, lower), part == "edges")
 
 
 def conv(weight, pads):
@@ -175,16 +192,12 @@
     return total
 
 
-def conv_adjoint(weight, pads, flags, halo):
-    total = None
-    for r in range(3):
-        start = (2 - r) * LANES
-        taps = jnp.concatenate([weight[3 * r + s] for s in range(3)], 0)
-        term = lax.dot_general(
-            taps, pads[:, start : start + CELLS], TN, preferred_element_type=F32
-        )
-        total = term if total is None else total + term
-    chans = total.shape[0]
+def adjoint_rows(weight, r, cells):
+    taps = jnp.concatenate([weight[3 * r + s] for s in range(3)], 0)
+    return lax.dot_general(taps, cells, TN, preferred_element_type=F32)
+
+
+def adjoint_corners(weight, flags, halo, chans):
     above, below = (corners_of(ref, chans) for ref in halo[2:])
     k, lane = (iota((16, LANES), 0), iota((16, LANES), 1))
 
@@ -197,10 +210,28 @@
     east = LANES - 1
     top = corner(above, 1, 0, 8 - 2 * flags[2]) + corner(above, 3, east, 6 + 2 * flags[3])
     bottom = corner(below, 1, 0, 2 - 2 * flags[4]) + corner(below, 3, east, 2 * flags[5])
+    return (top, bottom)
+
+
+def with_ends(total, top, bottom):
     return jnp.concatenate(
         [total[:, :LANES] + top, total[:, LANES : CELLS - LANES], total[:, CELLS - LANES :] + bottom],
         1,
     )
+
+
+def adjoint_inner(weight, pads):
+    total = None
+    for r in range(3):
+        start = (2 - r) * LANES
+        term = adjoint_rows(weight, r, pads[:, start : start + CELLS])
+        total = term if total is None else total + term
+    return total
+
+
+def conv_adjoint(weight, pads, flags, halo):
+    total = adjoint_inner(weight, pads)
+    return with_ends(total, *adjoint_corners(weight, flags, halo, total.shape[0]))
 
 
 def prepare_kernel(flips, field, cotangent, *outs):
@@ -212,18 +243,48 @@
     rims(flat_field[...], flat_cot[...], edge_flags(flips), outs[2:])
 
 
-def hidden_kernel(flips, field, cotangent, one, two, *refs):
-    halo, outs, back_pads = (refs[:4], refs[4:-1], refs[-1])
-    act_out, back_out, pads = outs[:3]
+def inner_kernel(field, cotangent, one, two, from_w, from_e, pads, hidden, back_act, back_pads):
+    halo = (from_w, from_e, None, None)
+    pad_forward(pads, field[...], None, halo, "inner")
+    hidden[...] = conv(one, pads)
+    pad_backward(back_pads, cotangent[...], None, halo, "inner")
+    back_act[...] = adjoint_inner(two, back_pads)
+
+
+def hidden_kernel(flips, pads_in, hidden_in, back_in, one, two, from_n, from_s, *refs):
+    act_out, back_out, pads_out = refs[:3]
+    ends, back_ends, sems = refs[-3:]
     flags = edge_flags(flips)
-    pad_forward(pads, field[...], flags, halo)
-    pad_backward(back_pads, cotangent[...], flags, halo)
-    hidden = conv(one, pads)
-    back_act = conv_adjoint(two, back_pads, flags, halo)
+    halo = (None, None, from_n, from_s)
+    chans = hidden_in.shape[0]
+    pad_forward(ends, None, flags, halo, "edges")
+    copies = [
+        pltpu.make_async_copy(
+            ends.at[:, pl.ds(k * LANES, LANES)],
+            pads_out.at[:, pl.ds(k * (PADDED - LANES), LANES)],
+            sems.at[k],
+        )
+        for k in range(2)
+    ]
+    for copy in copies:
+        copy.start()
+    pad_backward(back_ends, None, flags, halo, "edges")
+    first, last = (jnp.concatenate([one[k + s] for s in range(3)], 1) for k in (0, 6))
+    hidden = with_ends(
+        hidden_in[...], dot(first, ends[:, :LANES]), dot(last, ends[:, LANES:])
+    )
+    top, bottom = adjoint_corners(two, flags, halo, chans)
+    back_act = with_ends(
+        back_in[...],
+        top + adjoint_rows(two, 2, back_ends[:, :LANES]),
+        bottom + adjoint_rows(two, 0, back_ends[:, LANES:]),
+    )
     sigma = 1.0 / (1.0 + jnp.exp(-hidden))
     act_out[...] = (hidden * sigma).astype(BF16)
     back_out[...] = (back_act * sigma * (1.0 + hidden * (1.0 - sigma))).astype(BF16)
-    rims(act_out[...], back_out[...], flags, outs[3:])
+    rims(act_out[...], back_out[...], flags, refs[3:-3])
+    for copy in copies:
+        copy.wait()
 
 
 def grad_kernel(grad_tile, pads, keep, away, both):
@@ -450,12 +511,26 @@
         (edge_flips, fields.reshape(tile.shape), cotangent.reshape(tile.shape)),
     )
     halo = exchange(rim)
-    act, back, pads_in, *rim = call(
+    sums = struct(*flat.shape, dtype=F32)
+    pads_in, hidden, back_act = call(
+        inner_kernel,
+        (pads, sums, sums),
+        (field, cot, weight_one, weight_two) + halo[:2],
+        scratch,
+        flags=False,
+    )
+    ends = pltpu.VMEM((3 * chans, 2 * LANES), BF16)
+    shapes = (flat, flat, pads) + rim_shapes(chans)
+    act, back, pads_in, *rim = pl.pallas_call(
         hidden_kernel,
-        (flat, flat, pads) + rim_shapes(chans),
-        (edge_flips, field, cot, weight_one, weight_two) + halo,
-        scratch,
-    )
+        name="hidden",
+        out_shape=shapes,
+        in_specs=[SMEM, ANY] + [VMEM] * 6,
+        out_specs=[VMEM, VMEM, ANY] + [VMEM] * (len(shapes) - 3),
+        input_output_aliases={1: 2},
+        scratch_shapes=[ends, ends, pltpu.SemaphoreType.DMA((2,))],
+        compiler_params=pltpu.CompilerParams(vmem_limit_bytes=56 * 1024 * 1024),
+    )(edge_flips, pads_in, hidden, back_act, weight_one, weight_two, *halo[2:])
     halo = exchange(rim)
     local = (struct(9 * chans, LANES, dtype=F32), struct(9 * chans, LANES))
     halves = [pltpu.VMEM((2, 9 * chans, LANES), F32)]

time: 173 us -> 172 us (level)
  Pallas kernels: 41.1 us -> 45.1 us
  waiting for transfers between devices: 28.3 us -> 24.9 us
  starting transfers between devices: 42.7 us -> 40.4 us
    ppermute x4, waiting for transfers between devices: 12.2 us -> 6.04 us  [across(): lax.ppermute(value, 'lat', [(i, i + step) for i in range(lats) if 0 <= i...]
    pallas_call x0 -> x1, Pallas kernels: none -> 5.25 us  [per_device(): pl.pallas_call(hidden_kernel, name='hidden', out_shape=shapes, in_specs=[...]
    ppermute x3, starting transfers between devices: 3.09 us -> 0.9 us  [beside(): return lax.ppermute(value, 'dp', [(i, (i + 2) % 4) for i in range(4)])]
    ppermute x3, waiting for transfers between devices: 13.7 us -> 15.8 us  [beside(): return lax.ppermute(value, 'dp', [(i, (i + 2) % 4) for i in range(4)])]
  transfers between devices with their start and end apart: 15 -> 15, of which waited for: 9 -> 8; matrix products, arithmetic and copies ran while one was open for 1% -> 1% of each run, Pallas kernels for 12% -> 16%
where the time goes in v7:
time: 172 us
  blocking collectives  54.4 us (32%)
  Pallas kernels  45.1 us (26%)
  starting transfers between devices  40.4 us (23%)
  waiting for transfers between devices  24.9 us (14%)
  local copies, waits for them, and re-layouts  3.72 us (2%)
  other arithmetic  2.13 us (1%)
    all_to_all x4, blocking collectives, over(): return lax.all_to_all(value, axis, 0, 0)  54.4 us
    pallas_call x6, Pallas kernels, call(): pl.pallas_call(kernel, out_shape=out_shape, in_specs=([SMEM] if flags els...  31.1 us
    ppermute x4, starting transfers between devices, paired(): return lax.ppermute(value, 'dp', [(0, 1), (1, 0), (2, 3), (3, 2)])  17.4 us
    ppermute x3, waiting for transfers between devices, beside(): return lax.ppermute(value, 'dp', [(i, (i + 2) % 4) for i in range(4)])  15.8 us
    ppermute x4, starting transfers between devices, across(): lax.ppermute(value, 'lat', [(i, i + step) for i in range(lats) if 0 <= i...  12.6 us
    ppermute x4, starting transfers between devices, along(): lax.ppermute(value, 'lon', [(i, (i + step) % lons) for i in range(lons)])  9.57 us
    ppermute x4, waiting for transfers between devices, across(): lax.ppermute(value, 'lat', [(i, i + step) for i in range(lats) if 0 <= i...  6.04 us
    pallas_call x2, Pallas kernels, finish(): pl.pallas_call(functools.partial(finish_kernel, own), out_shape=(grad, gr...  5.97 us
  transfers between devices with their start and end apart: 15, of which 8 were waited for; matrix products, arithmetic and copies ran while one was open for 1% of the time, Pallas kernels for 16%

profile of v7, /device:TPU:1, one launch (start us, length us, event | category | flops | bytes accessed | tf_op | source)
XLA Modules:
  0.0 171.6 jit_solution(11676806671654556307)
XLA Ops:
  0.6 3.8 %shard_map.84 = (bf16[256,1024]{1,0:T(8,128)(2,1)}, bf16[256,1024]{1,0:T(8,128)(2,1)}, bf16[32,256]{1,0:T(8,128)(2,1)}, bf16[32,256]{1,0:T(8,128)(2,1)}, bf16[54...) custom-call(s32[7,8]{1,0:T(8,128)} %flips.7, bf16[256,8,128]{2,1,0:T(8,128)(2,1)} %bitcast.8, bf16[256,8,128]{2,1,0:T(8,128)(2,1)} %bitcast.9), custom_call_target="tpu_custom_call" | custom-call | tf_op jit(solution)/shard_map/pallas_call | solution.py:410
  4.4 2.5 %collective-permute-start = (bf16[32,256]{1,0:T(8,128)(2,1)}, bf16[32,256]{1,0:T(8,128)(2,1)S(1)}, u32[]{:S(2)}, u32[]{:S(2)}) collective-permute-start(bf16[32,256]{1,0:T(8,128)(2,1)} %get-tuple-element.35), channel_id=1, source_target_pairs={{0,32},{32,64},{64,96},{96,128},{128,160},{160,192},{192,224},{224... | collective-permute-start | bytes 49160 | tf_op jit(solution)/shard_map/ppermute | solution.py:435
  6.9 4.0 %collective-permute-start.1 = (bf16[32,256]{1,0:T(8,128)(2,1)}, bf16[32,256]{1,0:T(8,128)(2,1)S(1)}, u32[]{:S(2)}, u32[]{:S(2)}) collective-permute-start(bf16[32,256]{1,0:T(8,128)(2,1)} %get-tuple-element.36), channel_id=1, source_target_pairs={{0,224},{32,0},{64,32},{96,64},{128,96},{160,128},{192,160},{224,1... | collective-permute-start | bytes 49160 | tf_op jit(solution)/shard_map/ppermute | solution.py:435
  10.9 1.3 collective-permute-done.from_w
  12.7 1.4 join.2
  14.1 4.8 %collective-permute-start.2 = (bf16[544,128]{1,0:T(8,128)(2,1)}, bf16[544,128]{1,0:T(8,128)(2,1)S(1)}, u32[]{:S(2)}, u32[]{:S(2)}) collective-permute-start(bf16[544,128]{1,0:T(8,128)(2,1)} %get-tuple-element.42), channel_id=1, source_target_pairs={{0,4},{4,8},{8,12},{12,16},{16,20},{20,24},{24,28},{1,5},{5,9},{9,... | collective-permute-start | bytes 417800 | tf_op jit(solution)/shard_map/ppermute | solution.py:438
  18.9 1.3 collective-permute-start.3
  20.2 6.5 %shard_map.85 = (bf16[768,1280]{1,0:T(8,128)(2,1)}, f32[256,1024]{1,0:T(8,128)}, f32[256,1024]{1,0:T(8,128)}) custom-call(bf16[256,1024]{1,0:T(8,128)(2,1)} %get-tuple-element.33.field, bf16[256,1024]{1,0:T(8,128)(2,1)} %get-tuple-element.34.cotangent, bf16[9,256,256]{2,1,0:T(8,128)(2,1)} %weight.3, bf16[9,256,256]{2,1,0:T(8,128)(2,1)} %weight.2, ...), custom_call_target="tpu_custom_call" | custom-call | tf_op jit(solution)/shard_map/pallas_call | solution.py:410
  27.4 5.3 %hidden.1 = (bf16[256,1024]{1,0:T(8,128)(2,1)}, bf16[256,1024]{1,0:T(8,128)(2,1)}, bf16[768,1280]{1,0:T(8,128)(2,1)}, bf16[32,256]{1,0:T(8,128)(2,1)}, bf16[32,2...) custom-call(s32[7,8]{1,0:T(8,128)} %flips.7, ...), custom_call_target="tpu_custom_call", output_to_operand_aliasing={{2}: (1, {})} | custom-call | tf_op jit(solution)/shard_map/hidden/pallas_call | solution.py:524
  32.7 4.8 %shard_map.89 = (f32[2304,128]{1,0:T(8,128)}, bf16[2304,128]{1,0:T(8,128)(2,1)}) custom-call(bf16[256,1024]{1,0:T(8,128)(2,1)} %get-tuple-element.52.back.grad_tile, bf16[768,1280]{1,0:T(8,128)(2,1)} %get-tuple-element.53.pads), custom_call_target="tpu_custom_call" | custom-call | tf_op jit(solution)/shard_map/pallas_call | solution.py:410
  37.5 2.6 %collective-permute-start.8 = (bf16[2304,128]{1,0:T(8,128)(2,1)}, bf16[2304,128]{1,0:T(8,128)(2,1)S(1)}, u32[]{:S(2)}, u32[]{:S(2)}) collective-permute-start(bf16[2304,128]{1,0:T(8,128)(2,1)} %get-tuple-element.55), channel_id=1, source_target_pairs={{0,1},{1,0},{2,3},{3,2},{4,5},{5,4},{6,7},{7,6},{8,9},{9,8},{10,11... | collective-permute-start | bytes 1769480 | tf_op jit(solution)/shard_map/ppermute | solution.py:463
  40.2 3.1 %collective-permute-start.5 = (bf16[32,256]{1,0:T(8,128)(2,1)S(1)}, bf16[32,256]{1,0:T(8,128)(2,1)S(1)}, u32[]{:S(2)}, u32[]{:S(2)}) collective-permute-start(bf16[32,256]{1,0:T(8,128)(2,1)S(1)} %copy-done.14), channel_id=1, source_target_pairs={{0,224},{32,0},{64,32},{96,64},{128,96},{160,128},{192,160},{224,1... | collective-permute-start | bytes 49160 | tf_op jit(solution)/shard_map/ppermute | solution.py:435
  44.9 1.4 join.3
  46.3 5.0 %collective-permute-start.6 = (bf16[544,128]{1,0:T(8,128)(2,1)}, bf16[544,128]{1,0:T(8,128)(2,1)S(1)}, u32[]{:S(2)}, u32[]{:S(2)}) collective-permute-start(bf16[544,128]{1,0:T(8,128)(2,1)} %get-tuple-element.49), channel_id=1, source_target_pairs={{0,4},{4,8},{8,12},{12,16},{16,20},{20,24},{24,28},{1,5},{5,9},{9,... | collective-permute-start | bytes 417800 | tf_op jit(solution)/shard_map/ppermute | solution.py:438
  51.3 1.5 collective-permute-start.7
  53.6 5.2 %collective-permute-done.7.refs_3_ = bf16[544,128]{1,0:T(8,128)(2,1)S(1)} collective-permute-done((bf16[544,128]{1,0:T(8,128)(2,1)}, bf16[544,128]{1,0:T(8,128)(2,1)S(1)}, u32[]{:S(2)}, u32[]{:S(2)}) %collective-permute-start.7) | collective-permute-done | bytes 139296 | tf_op jit(solution)/shard_map/ppermute | solution.py:438
  59.4 4.8 %shard_map.86 = (bf16[768,1280]{1,0:T(8,128)(2,1)}, f32[2304,128]{1,0:T(8,128)}, bf16[2304,128]{1,0:T(8,128)(2,1)}) custom-call(s32[7,8]{1,0:T(8,128)} %flips.7, bf16[256,1024]{1,0:T(8,128)(2,1)} %get-tuple-element.44.act, bf16[256,1024]{1,0:T(8,128)(2,1)} %get-tuple-element.34.cotangent, bf16[32,256]{1,0:T(8,128)(2,1)} %copy-done.8, ...), custom_call_target="tpu_custom_call" | custom-call | tf_op jit(solution)/shard_map/pallas_call | solution.py:410
  64.2 2.4 %collective-permute-start.10 = (bf16[2304,128]{1,0:T(8,128)(2,1)}, bf16[2304,128]{1,0:T(8,128)(2,1)S(1)}, u32[]{:S(2)}, u32[]{:S(2)}) collective-permute-start(bf16[2304,128]{1,0:T(8,128)(2,1)} %get-tuple-element.57), channel_id=1, source_target_pairs={{0,1},{1,0},{2,3},{3,2},{4,5},{5,4},{6,7},{7,6},{8,9},{9,8},{10,11... | collective-permute-start | bytes 1769480 | tf_op jit(solution)/shard_map/ppermute | solution.py:463
  69.0 7.2 %collective-permute-done.9 = bf16[1152,128]{1,0:T(8,128)(2,1)} collective-permute-done((bf16[1152,128]{1,0:T(8,128)(2,1)}, bf16[1152,128]{1,0:T(8,128)(2,1)}, u32[]{:S(2)}, u32[]{:S(2)}) %collective-permute-start.9) | collective-permute-done | bytes 294944 | tf_op jit(solution)/shard_map/ppermute | solution.py:459
  76.2 1.1 add_convert_fusion.2
  77.3 5.1 %collective-permute-done.11 = bf16[1152,128]{1,0:T(8,128)(2,1)S(1)} collective-permute-done((bf16[1152,128]{1,0:T(8,128)(2,1)S(1)}, bf16[1152,128]{1,0:T(8,128)(2,1)S(1)}, u32[]{:S(2)}, u32[]{:S(2)}) %collective-permute-start.11) | collective-permute-done | bytes 294944 | tf_op jit(solution)/shard_map/ppermute | solution.py:459
  82.6 18.0 %all_to_all.20 = bf16[8,288,128]{2,1,0:T(8,128)(2,1)S(1)} all-to-all(bf16[8,288,128]{2,1,0:T(8,128)(2,1)S(1)} %pad_maximum_fusion), channel_id=1, replica_groups=mesh['lon'=8,'lat'=8,'dp'=4] {'lat'}, dimensions={0} | all-to-all | bytes 1179648 | tf_op jit(solution)/shard_map/all_to_all | solution.py:467
  100.7 14.3 %all_to_all.21 = f32[8,36,128]{2,1,0:T(8,128)S(1)} all-to-all(f32[8,36,128]{2,1,0:T(8,128)S(1)} %reshape.39), channel_id=1, replica_groups=mesh['lon'=8,'lat'=8,'dp'=4] {'lon'}, dimensions={0} | all-to-all | bytes 294912 | tf_op jit(solution)/shard_map/all_to_all | solution.py:467
  115.0 9.8 %all_to_all.22 = bf16[8,36,128]{2,1,0:T(8,128)(2,1)S(1)} all-to-all(bf16[8,36,128]{2,1,0:T(8,128)(2,1)S(1)} %broadcast_in_dim.6), channel_id=1, replica_groups=mesh['lon'=8,'lat'=8,'dp'=4] {'lon'}, dimensions={0} | all-to-all | bytes 147456 | tf_op jit(solution)/shard_map/all_to_all | solution.py:467
  124.9 12.3 %all_to_all.23.near = bf16[8,288,128]{2,1,0:T(8,128)(2,1)S(1)} all-to-all(bf16[8,288,128]{2,1,0:T(8,128)(2,1)S(1)} %broadcast_in_dim.15), channel_id=1, replica_groups=mesh['lon'=8,'lat'=8,'dp'=4] {'lat'}, dimensions={0} | all-to-all | bytes 1179648 | tf_op jit(solution)/shard_map/all_to_all | solution.py:467
  137.2 6.2 %collective-permute-start.12 = (bf16[8,288,128]{2,1,0:T(8,128)(2,1)S(1)}, bf16[8,288,128]{2,1,0:T(8,128)(2,1)S(1)}, u32[]{:S(2)}, u32[]{:S(2)}) collective-permute-start(bf16[8,288,128]{2,1,0:T(8,128)(2,1)S(1)} %all_to_all.23.near), channel_id=1, source_target_pairs={{0,1},{1,0},{2,3},{3,2},{4,5},{5,4},{6,7},{7,6},{8,9},{9,8},{10,11... | collective-permute-start | bytes 1769480 | tf_op jit(solution)/shard_map/ppermute | solution.py:463
  143.4 3.5 %collective-permute-done.13.far = bf16[8,288,128]{2,1,0:T(8,128)(2,1)S(1)} collective-permute-done((bf16[8,288,128]{2,1,0:T(8,128)(2,1)S(1)}, bf16[8,288,128]{2,1,0:T(8,128)(2,1)S(1)}, u32[]{:S(2)}, u32[]{:S(2)}) %collective-permute-start.13) | collective-permute-done | bytes 589856 | tf_op jit(solution)/shard_map/ppermute | solution.py:459
  146.9 6.1 %collective-permute-start.14 = (bf16[8,288,128]{2,1,0:T(8,128)(2,1)S(1)}, bf16[8,288,128]{2,1,0:T(8,128)(2,1)S(1)}, u32[]{:S(2)}, u32[]{:S(2)}) collective-permute-start(bf16[8,288,128]{2,1,0:T(8,128)(2,1)S(1)} %collective-permute-done.13.far), channel_id=1, source_target_pairs={{0,1},{1,0},{2,3},{3,2},{4,5},{5,4},{6,7},{7,6},{8,9},{9,8},{10,11... | collective-permute-start | bytes 1769480 | tf_op jit(solution)/shard_map/ppermute | solution.py:463
  153.1 5.4 %shard_map.87 = bf16[256,8,128]{2,1,0:T(8,128)(2,1)} custom-call(bf16[256,1024]{1,0:T(8,128)(2,1)} %get-tuple-element.33.field, bf16[9,256,256]{2,1,0:T(8,128)(2,1)} %weight.2, bf16[768,1280]{1,0:T(8,128)(2,1)} %get-tuple-element.51.pads), custom_call_target="tpu_custom_call" | custom-call | tf_op jit(solution)/shard_map/pallas_call | solution.py:410
  158.4 5.9 %shard_map.88 = bf16[256,8,128]{2,1,0:T(8,128)(2,1)} custom-call(s32[7,8]{1,0:T(8,128)} %flips.7, bf16[256,1024]{1,0:T(8,128)(2,1)} %get-tuple-element.34.cotangent, bf16[256,1024]{1,0:T(8,128)(2,1)} %get-tuple-element.52.back.grad_tile, bf16[9,256,256]{2,1,0:T(8,128)(2,1)} %weight.3, bf16[32,256]{1,0:T(8,128)(2,1)} %copy-done.8, bf16[32,256]{1,0:T(8,128)(2,1)} %copy-done.9, ...), custom_call_target="tpu_custom_call" | custom-call | tf_op jit(solution)/shard_map/pallas_call | solution.py:410
  164.4 3.0 %shard_map.90 = (f32[9,256,256]{2,1,0:T(8,128)}, f32[9,256,256]{2,1,0:T(8,128)}) custom-call(bf16[8,288,128]{2,1,0:T(8,128)(2,1)} %copy-done, bf16[8,288,128]{2,1,0:T(8,128)(2,1)} %copy-done.5), custom_call_target="tpu_custom_call" | custom-call | tf_op jit(solution)/shard_map/pallas_call | solution.py:388
  168.4 3.0 %shard_map.91 = (f32[9,256,256]{2,1,0:T(8,128)}, f32[9,256,256]{2,1,0:T(8,128)}) custom-call(bf16[8,288,128]{2,1,0:T(8,128)(2,1)} %copy-done.3, bf16[8,288,128]{2,1,0:T(8,128)(2,1)} %copy-done.4, f32[9,256,256]{2,1,0:T(8,128)} %get-tuple-element.58.refs_0_, f32[9,256,256]{2,1,0:T(8,128)} %get-tuple-element.59.refs_1_), custom_call_target="tpu_custom_call", output_to_operand_aliasing={{0}: (2, {}), {1}: (3, {})} | custom-call | tf_op jit(solution)/shard_map/pallas_call | solution.py:388
  (56 shorter events, 8.2 us)
Async XLA Ops:
  4.4 7.7 %collective-permute-start = (bf16[32,256]{1,0:T(8,128)(2,1)}, bf16[32,256]{1,0:T(8,128)(2,1)S(1)}, u32[]{:S(2)}, u32[]{:S(2)}) collective-permute-start(bf16[32,256]{1,0:T(8,128)(2,1)} %get-tuple-element.35), channel_id=1, source_target_pairs={{0,32},{32,64},{64,96},{96,128},{128,160},{160,192},{192,224},{224... | collective-permute-start | bytes 49160 | tf_op jit(solution)/shard_map/ppermute | solution.py:435
  6.9 5.3 %collective-permute-start.1 = (bf16[32,256]{1,0:T(8,128)(2,1)}, bf16[32,256]{1,0:T(8,128)(2,1)S(1)}, u32[]{:S(2)}, u32[]{:S(2)}) collective-permute-start(bf16[32,256]{1,0:T(8,128)(2,1)} %get-tuple-element.36), channel_id=1, source_target_pairs={{0,224},{32,0},{64,32},{96,64},{128,96},{160,128},{192,160},{224,1... | collective-permute-start | bytes 49160 | tf_op jit(solution)/shard_map/ppermute | solution.py:435
  12.1 0.6 copy-start.12
  12.1 0.6 copy-start.13
  14.1 12.6 %collective-permute-start.2 = (bf16[544,128]{1,0:T(8,128)(2,1)}, bf16[544,128]{1,0:T(8,128)(2,1)S(1)}, u32[]{:S(2)}, u32[]{:S(2)}) collective-permute-start(bf16[544,128]{1,0:T(8,128)(2,1)} %get-tuple-element.42), channel_id=1, source_target_pairs={{0,4},{4,8},{8,12},{12,16},{16,20},{20,24},{24,28},{1,5},{5,9},{9,... | collective-permute-start | bytes 417800 | tf_op jit(solution)/shard_map/ppermute | solution.py:438
  18.9 7.8 %collective-permute-start.3 = (bf16[544,128]{1,0:T(8,128)(2,1)}, bf16[544,128]{1,0:T(8,128)(2,1)S(1)}, u32[]{:S(2)}, u32[]{:S(2)}) collective-permute-start(bf16[544,128]{1,0:T(8,128)(2,1)} %get-tuple-element.43), channel_id=1, source_target_pairs={{4,0},{8,4},{12,8},{16,12},{20,16},{24,20},{28,24},{5,1},{9,5},{13... | collective-permute-start | bytes 417800 | tf_op jit(solution)/shard_map/ppermute | solution.py:438
  26.7 0.6 copy-start.10
  26.7 0.7 copy-start.11
  32.7 7.4 %copy-start.15 = (bf16[32,256]{1,0:T(8,128)(2,1)S(1)}, bf16[32,256]{1,0:T(8,128)(2,1)}, u32[]{:S(2)}) copy-start(bf16[32,256]{1,0:T(8,128)(2,1)} %get-tuple-element.45) | copy-start | bytes 49156
  32.7 7.4 %copy-start.14 = (bf16[32,256]{1,0:T(8,128)(2,1)S(1)}, bf16[32,256]{1,0:T(8,128)(2,1)}, u32[]{:S(2)}) copy-start(bf16[32,256]{1,0:T(8,128)(2,1)} %get-tuple-element.46) | copy-start | bytes 49156
  37.5 29.1 %copy-start.1 = (f32[2304,128]{1,0:T(8,128)S(1)}, f32[2304,128]{1,0:T(8,128)}, u32[]{:S(2)}) copy-start(f32[2304,128]{1,0:T(8,128)} %get-tuple-element.54) | copy-start | bytes 3538948
  37.5 29.1 %collective-permute-start.8 = (bf16[2304,128]{1,0:T(8,128)(2,1)}, bf16[2304,128]{1,0:T(8,128)(2,1)S(1)}, u32[]{:S(2)}, u32[]{:S(2)}) collective-permute-start(bf16[2304,128]{1,0:T(8,128)(2,1)} %get-tuple-element.55), channel_id=1, source_target_pairs={{0,1},{1,0},{2,3},{3,2},{4,5},{5,4},{6,7},{7,6},{8,9},{9,8},{10,11... | collective-permute-start | bytes 1769480 | tf_op jit(solution)/shard_map/ppermute | solution.py:463
  40.1 4.2 %collective-permute-start.4 = (bf16[32,256]{1,0:T(8,128)(2,1)S(1)}, bf16[32,256]{1,0:T(8,128)(2,1)S(1)}, u32[]{:S(2)}, u32[]{:S(2)}) collective-permute-start(bf16[32,256]{1,0:T(8,128)(2,1)S(1)} %copy-done.15), channel_id=1, source_target_pairs={{0,32},{32,64},{64,96},{96,128},{128,160},{160,192},{192,224},{224... | collective-permute-start | bytes 49160 | tf_op jit(solution)/shard_map/ppermute | solution.py:435
  40.2 4.2 %collective-permute-start.5 = (bf16[32,256]{1,0:T(8,128)(2,1)S(1)}, bf16[32,256]{1,0:T(8,128)(2,1)S(1)}, u32[]{:S(2)}, u32[]{:S(2)}) collective-permute-start(bf16[32,256]{1,0:T(8,128)(2,1)S(1)} %copy-done.14), channel_id=1, source_target_pairs={{0,224},{32,0},{64,32},{96,64},{128,96},{160,128},{192,160},{224,1... | collective-permute-start | bytes 49160 | tf_op jit(solution)/shard_map/ppermute | solution.py:435
  44.3 0.6 copy-start.8
  44.3 0.6 copy-start.9
  46.3 7.3 %collective-permute-start.6 = (bf16[544,128]{1,0:T(8,128)(2,1)}, bf16[544,128]{1,0:T(8,128)(2,1)S(1)}, u32[]{:S(2)}, u32[]{:S(2)}) collective-permute-start(bf16[544,128]{1,0:T(8,128)(2,1)} %get-tuple-element.49), channel_id=1, source_target_pairs={{0,4},{4,8},{8,12},{12,16},{16,20},{20,24},{24,28},{1,5},{5,9},{9,... | collective-permute-start | bytes 417800 | tf_op jit(solution)/shard_map/ppermute | solution.py:438
  51.3 7.5 %collective-permute-start.7 = (bf16[544,128]{1,0:T(8,128)(2,1)}, bf16[544,128]{1,0:T(8,128)(2,1)S(1)}, u32[]{:S(2)}, u32[]{:S(2)}) collective-permute-start(bf16[544,128]{1,0:T(8,128)(2,1)} %get-tuple-element.50), channel_id=1, source_target_pairs={{4,0},{8,4},{12,8},{16,12},{20,16},{24,20},{28,24},{5,1},{9,5},{13... | collective-permute-start | bytes 417800 | tf_op jit(solution)/shard_map/ppermute | solution.py:438
  53.6 5.2 %copy-start.6 = (bf16[544,128]{1,0:T(8,128)(2,1)}, bf16[544,128]{1,0:T(8,128)(2,1)S(1)}, u32[]{:S(2)}) copy-start(bf16[544,128]{1,0:T(8,128)(2,1)S(1)} %collective-permute-done.6.refs_2_) | copy-start | bytes 417796
  58.8 0.7 copy-start.7
  64.2 4.2 %copy-start.2 = (f32[2304,128]{1,0:T(8,128)S(1)}, f32[2304,128]{1,0:T(8,128)}, u32[]{:S(2)}) copy-start(f32[2304,128]{1,0:T(8,128)} %get-tuple-element.56) | copy-start | bytes 3538948
  64.2 4.2 %collective-permute-start.10 = (bf16[2304,128]{1,0:T(8,128)(2,1)}, bf16[2304,128]{1,0:T(8,128)(2,1)S(1)}, u32[]{:S(2)}, u32[]{:S(2)}) collective-permute-start(bf16[2304,128]{1,0:T(8,128)(2,1)} %get-tuple-element.57), channel_id=1, source_target_pairs={{0,1},{1,0},{2,3},{3,2},{4,5},{5,4},{6,7},{7,6},{8,9},{9,8},{10,11... | collective-permute-start | bytes 1769480 | tf_op jit(solution)/shard_map/ppermute | solution.py:463
  67.4 8.9 %collective-permute-start.9 = (bf16[1152,128]{1,0:T(8,128)(2,1)}, bf16[1152,128]{1,0:T(8,128)(2,1)}, u32[]{:S(2)}, u32[]{:S(2)}) collective-permute-start(bf16[1152,128]{1,0:T(8,128)(2,1)} %add_convert_fusion.3), channel_id=1, source_target_pairs={{0,2},{1,3},{2,0},{3,1},{4,6},{5,7},{6,4},{7,5},{8,10},{9,11},{10,... | collective-permute-start | bytes 884744 | tf_op jit(solution)/shard_map/ppermute | solution.py:459
  68.5 13.9 %collective-permute-start.11 = (bf16[1152,128]{1,0:T(8,128)(2,1)S(1)}, bf16[1152,128]{1,0:T(8,128)(2,1)S(1)}, u32[]{:S(2)}, u32[]{:S(2)}) collective-permute-start(bf16[1152,128]{1,0:T(8,128)(2,1)S(1)} %add_convert_fusion.1), channel_id=1, source_target_pairs={{0,2},{1,3},{2,0},{3,1},{4,6},{5,7},{6,4},{7,5},{8,10},{9,11},{10,... | collective-permute-start | bytes 884744 | tf_op jit(solution)/shard_map/ppermute | solution.py:459
  137.2 21.2 %copy-start = (bf16[8,288,128]{2,1,0:T(8,128)(2,1)}, bf16[8,288,128]{2,1,0:T(8,128)(2,1)S(1)}, u32[]{:S(2)}) copy-start(bf16[8,288,128]{2,1,0:T(8,128)(2,1)S(1)} %all_to_all.23.near) | copy-start | bytes 1769476
  137.2 9.7 %collective-permute-start.13 = (bf16[8,288,128]{2,1,0:T(8,128)(2,1)S(1)}, bf16[8,288,128]{2,1,0:T(8,128)(2,1)S(1)}, u32[]{:S(2)}, u32[]{:S(2)}) collective-permute-start(bf16[8,288,128]{2,1,0:T(8,128)(2,1)S(1)} %all_to_all.23.near), channel_id=1, source_target_pairs={{0,2},{1,3},{2,0},{3,1},{4,6},{5,7},{6,4},{7,5},{8,10},{9,11},{10,... | collective-permute-start | bytes 1769480 | tf_op jit(solution)/shard_map/ppermute | solution.py:459
  137.2 30.1 %collective-permute-start.12 = (bf16[8,288,128]{2,1,0:T(8,128)(2,1)S(1)}, bf16[8,288,128]{2,1,0:T(8,128)(2,1)S(1)}, u32[]{:S(2)}, u32[]{:S(2)}) collective-permute-start(bf16[8,288,128]{2,1,0:T(8,128)(2,1)S(1)} %all_to_all.23.near), channel_id=1, source_target_pairs={{0,1},{1,0},{2,3},{3,2},{4,5},{5,4},{6,7},{7,6},{8,9},{9,8},{10,11... | collective-permute-start | bytes 1769480 | tf_op jit(solution)/shard_map/ppermute | solution.py:463
  146.9 11.5 %copy-start.5 = (bf16[8,288,128]{2,1,0:T(8,128)(2,1)}, bf16[8,288,128]{2,1,0:T(8,128)(2,1)S(1)}, u32[]{:S(2)}) copy-start(bf16[8,288,128]{2,1,0:T(8,128)(2,1)S(1)} %collective-permute-done.13.far) | copy-start | bytes 1769476
  146.9 20.5 %collective-permute-start.14 = (bf16[8,288,128]{2,1,0:T(8,128)(2,1)S(1)}, bf16[8,288,128]{2,1,0:T(8,128)(2,1)S(1)}, u32[]{:S(2)}, u32[]{:S(2)}) collective-permute-start(bf16[8,288,128]{2,1,0:T(8,128)(2,1)S(1)} %collective-permute-done.13.far), channel_id=1, source_target_pairs={{0,1},{1,0},{2,3},{3,2},{4,5},{5,4},{6,7},{7,6},{8,9},{9,8},{10,11... | collective-permute-start | bytes 1769480 | tf_op jit(solution)/shard_map/ppermute | solution.py:463
  167.4 0.8 copy-start.3
  167.4 1.0 copy-start.4

commit v8 on v7

--- a/solution.py
+++ b/solution.py
@@ -324,81 +324,77 @@
         grad_fields[:, row, :] = total[:, row * LANES : (row + 1) * LANES]
 
 
-def finish_kernel(own, near, far, *refs):
-    outs, (flat, stage, sems, got) = (refs[-6:-4], refs[-4:])
+def quarter_kernel(own_core, own_side, quarter, *refs):
+    outs, (flat, stage, got, sems) = (refs[-6:-4], refs[-4:])
     place = lax.axis_index("dp")
     side, core = (lax.shift_right_logical(place, 1), lax.rem(place, 2))
-    half = core if own else 1 - core
+    half = core if own_core else 1 - core
+    part = side if own_side else 1 - side
     chans = stage.shape[2]
-    tiles, depth = near.shape[:2]
+    tiles, depth = quarter.shape[:2]
     depth = depth // 2
     size = tiles * depth
-    loads = []
-    for which in range(2):
-        for tile in range(tiles):
-            for index, (ref, to) in enumerate(((near, side), (far, 1 - side))):
-                start = pl.multiple_of(to * size + tile * depth, 16)
-                loads.append(
-                    pltpu.make_async_copy(
-                        ref.at[tile, pl.ds(which * depth, depth), :],
-                        flat.at[which, pl.ds(start, depth), :],
-                        got.at[which, tile, index],
-                    )
-                )
-                loads[-1].start()
+    loads = [
+        pltpu.make_async_copy(
+            quarter.at[tile, pl.ds(which * depth, depth), :],
+            flat.at[which, pl.ds(tile * depth, depth), :],
+            got.at[which, tile],
+        )
+        for which in range(2)
+        for tile in range(tiles)
+    ]
+    for load in loads:
+        load.start()
     for load in loads:
         load.wait()
 
-    def place_half(odd):
+    def place_quarter(half_at, part_at):
         copies = []
+        base = part_at * size
         for which, out in enumerate(outs):
-            for slot in range(5):
-                lanes = slice(0, 2 * LANES)
-                for part in range(2):
-                    group = 2 * slot + part - odd
-                    if 0 <= group < 9:
-                        span = slice(part * LANES, (part + 1) * LANES)
-                        rows = slice(group * chans, (group + 1) * chans)
-                        stage[which, slot, :, span] = flat[which, rows].astype(F32)
-                    else:
-                        lanes = slice((1 - part) * LANES, (2 - part) * LANES)
+            slot = 0
+            for group in range(9):
+                low, high = (max(group * chans, base), min((group + 1) * chans, base + size))
+                if high <= low:
+                    continue
+                tap, lanes = divmod(group + 9 * half_at, 2)
+                count = high - low
+                stage[which, slot, :count] = flat[which, low - base : high - base].astype(F32)
                 copies.append(
                     pltpu.make_async_copy(
-                        stage.at[which, slot, :, lanes],
-                        out.at[slot + 4 * odd, :, lanes],
+                        stage.at[which, slot, pl.ds(0, count), :],
+                        out.at[tap, pl.ds(low - group * chans, count), pl.ds(lanes * LANES, LANES)],
                         sems.at[which, slot],
                     )
                 )
                 copies[-1].start()
+                slot += 1
         for copy in copies:
             copy.wait()
 
-    @pl.when(half == 0)
-    def _():
-        place_half(0)
-
-    @pl.when(half == 1)
-    def _():
-        place_half(1)
-
-
-def finish(own, near, far, *partial):
-    chans = partial[0].shape[1] if partial else 2 * LANES
+    for half_at in range(2):
+        for part_at in range(2):
+            pl.when((half == half_at) & (part == part_at))(
+                functools.partial(place_quarter, half_at, part_at)
+            )
+
+
+def finish(own_core, own_side, quarter, *partial):
+    chans = 2 * LANES
     grad = struct(9, chans, chans, dtype=F32)
     return pl.pallas_call(
-        functools.partial(finish_kernel, own),
+        functools.partial(quarter_kernel, own_core, own_side),
         out_shape=(grad, grad),
-        in_specs=[ANY, ANY] + [ANY] * len(partial),
+        in_specs=[ANY] * (1 + len(partial)),
         out_specs=(ANY, ANY),
-        input_output_aliases={2 + k: k for k in range(len(partial))},
+        input_output_aliases={1 + k: k for k in range(len(partial))},
         scratch_shapes=[
-            pltpu.VMEM((2, 9 * chans, LANES), BF16),
-            pltpu.VMEM((2, 5, chans, chans), F32),
+            pltpu.VMEM((2, 9 * chans // 2, LANES), BF16),
+            pltpu.VMEM((2, 5, chans, LANES), F32),
+            pltpu.SemaphoreType.DMA((2, quarter.shape[0])),
             pltpu.SemaphoreType.DMA((2, 5)),
-            pltpu.SemaphoreType.DMA((2, near.shape[0], 2)),
         ],
-        compiler_params=pltpu.CompilerParams(vmem_limit_bytes=56 * 1024 * 1024),
-    )(near, far, *partial)
+    )(quarter, *partial)
 
 
 SMEM = pl.BlockSpec(memory_space=pltpu.SMEM)
@@ -546,8 +542,10 @@
     )
     pair = paired(quarter)
     across = paired(other)
-    grads = finish(True, quarter, other)
-    grad_one, grad_two = finish(False, pair, across, *grads)
+    grads = finish(True, True, quarter)
+    grads = finish(False, True, pair, *grads)
+    grads = finish(True, False, other, *grads)
+    grad_one, grad_two = finish(False, False, across, *grads)
     return (output.reshape(fields.shape), grad_fields.reshape(fields.shape), grad_one, grad_two)
 
 

time: 172 us -> 176 us (1.023)
  Pallas kernels: 45.1 us -> 48.1 us
    pallas_call x2 -> x4, Pallas kernels: 5.97 us -> 9.06 us  [finish(): pl.pallas_call(functools.partial(quarter_kernel, own_core, own_side), out...]
  transfers between devices with their start and end apart: 15 -> 15, of which waited for: 8 -> 8; matrix products, arithmetic and copies ran while one was open for 1% -> 1% of each run, Pallas kernels for 16% -> 18%
where the time goes in v8:
time: 176 us; the launch traced here: 175 us
  blocking collectives  54.4 us (31%)
  Pallas kernels  48.1 us (27%)
  starting transfers between devices  40.4 us (23%)
  waiting for transfers between devices  24.9 us (14%)
  local copies, waits for them, and re-layouts  4.36 us (2%)
  other arithmetic  2.13 us (1%)
    all_to_all x4, blocking collectives, over(): return lax.all_to_all(value, axis, 0, 0)  54.4 us
    pallas_call x6, Pallas kernels, call(): pl.pallas_call(kernel, out_shape=out_shape, in_specs=([SMEM] if flags els...  31.1 us
    ppermute x4, starting transfers between devices, paired(): return lax.ppermute(value, 'dp', [(0, 1), (1, 0), (2, 3), (3, 2)])  17.4 us
    ppermute x3, waiting for transfers between devices, beside(): return lax.ppermute(value, 'dp', [(i, (i + 2) % 4) for i in range(4)])  15.8 us
    ppermute x4, starting transfers between devices, across(): lax.ppermute(value, 'lat', [(i, i + step) for i in range(lats) if 0 <= i...  12.6 us
    ppermute x4, starting transfers between devices, along(): lax.ppermute(value, 'lon', [(i, (i + step) % lons) for i in range(lons)])  9.54 us
    pallas_call x4, Pallas kernels, finish(): pl.pallas_call(functools.partial(quarter_kernel, own_core, own_side), out...  9.06 us
    ppermute x4, waiting for transfers between devices, across(): lax.ppermute(value, 'lat', [(i, i + step) for i in range(lats) if 0 <= i...  6.04 us
  transfers between devices with their start and end apart: 15, of which 8 were waited for; matrix products, arithmetic and copies ran while one was open for 1% of the time, Pallas kernels for 18%

profile of v8, /device:TPU:1, one launch (start us, length us, event | category | flops | bytes accessed | tf_op | source)
XLA Modules:
  0.0 175.3 jit_solution(7236767192586765429)
XLA Ops:
  0.6 3.8 %shard_map.84 = (bf16[256,1024]{1,0:T(8,128)(2,1)}, bf16[256,1024]{1,0:T(8,128)(2,1)}, bf16[32,256]{1,0:T(8,128)(2,1)}, bf16[32,256]{1,0:T(8,128)(2,1)}, bf16[54...) custom-call(s32[7,8]{1,0:T(8,128)} %flips.7, bf16[256,8,128]{2,1,0:T(8,128)(2,1)} %bitcast.8, bf16[256,8,128]{2,1,0:T(8,128)(2,1)} %bitcast.9), custom_call_target="tpu_custom_call" | custom-call | tf_op jit(solution)/shard_map/pallas_call | solution.py:406
  4.4 2.5 %collective-permute-start = (bf16[32,256]{1,0:T(8,128)(2,1)}, bf16[32,256]{1,0:T(8,128)(2,1)S(1)}, u32[]{:S(2)}, u32[]{:S(2)}) collective-permute-start(bf16[32,256]{1,0:T(8,128)(2,1)} %get-tuple-element.39), channel_id=1, source_target_pairs={{0,32},{32,64},{64,96},{96,128},{128,160},{160,192},{192,224},{224... | collective-permute-start | bytes 49160 | tf_op jit(solution)/shard_map/ppermute | solution.py:431
  6.9 4.0 %collective-permute-start.1 = (bf16[32,256]{1,0:T(8,128)(2,1)}, bf16[32,256]{1,0:T(8,128)(2,1)S(1)}, u32[]{:S(2)}, u32[]{:S(2)}) collective-permute-start(bf16[32,256]{1,0:T(8,128)(2,1)} %get-tuple-element.40), channel_id=1, source_target_pairs={{0,224},{32,0},{64,32},{96,64},{128,96},{160,128},{192,160},{224,1... | collective-permute-start | bytes 49160 | tf_op jit(solution)/shard_map/ppermute | solution.py:431
  12.7 1.4 join.2
  14.1 4.8 %collective-permute-start.2 = (bf16[544,128]{1,0:T(8,128)(2,1)}, bf16[544,128]{1,0:T(8,128)(2,1)S(1)}, u32[]{:S(2)}, u32[]{:S(2)}) collective-permute-start(bf16[544,128]{1,0:T(8,128)(2,1)} %get-tuple-element.46), channel_id=1, source_target_pairs={{0,4},{4,8},{8,12},{12,16},{16,20},{20,24},{24,28},{1,5},{5,9},{9,... | collective-permute-start | bytes 417800 | tf_op jit(solution)/shard_map/ppermute | solution.py:434
  18.9 1.3 collective-permute-start.3
  20.2 6.5 %shard_map.85 = (bf16[768,1280]{1,0:T(8,128)(2,1)}, f32[256,1024]{1,0:T(8,128)}, f32[256,1024]{1,0:T(8,128)}) custom-call(bf16[256,1024]{1,0:T(8,128)(2,1)} %get-tuple-element.37.field, bf16[256,1024]{1,0:T(8,128)(2,1)} %get-tuple-element.38.cotangent, bf16[9,256,256]{2,1,0:T(8,128)(2,1)} %weight.3, bf16[9,256,256]{2,1,0:T(8,128)(2,1)} %weight.2, ...), custom_call_target="tpu_custom_call" | custom-call | tf_op jit(solution)/shard_map/pallas_call | solution.py:406
  27.4 5.3 %hidden.1 = (bf16[256,1024]{1,0:T(8,128)(2,1)}, bf16[256,1024]{1,0:T(8,128)(2,1)}, bf16[768,1280]{1,0:T(8,128)(2,1)}, bf16[32,256]{1,0:T(8,128)(2,1)}, bf16[32,2...) custom-call(s32[7,8]{1,0:T(8,128)} %flips.7, ...), custom_call_target="tpu_custom_call", output_to_operand_aliasing={{2}: (1, {})} | custom-call | tf_op jit(solution)/shard_map/hidden/pallas_call | solution.py:520
  32.7 4.8 %shard_map.89 = (f32[2304,128]{1,0:T(8,128)}, bf16[2304,128]{1,0:T(8,128)(2,1)}) custom-call(bf16[256,1024]{1,0:T(8,128)(2,1)} %get-tuple-element.56.back.grad_tile, bf16[768,1280]{1,0:T(8,128)(2,1)} %get-tuple-element.57.pads), custom_call_target="tpu_custom_call" | custom-call | tf_op jit(solution)/shard_map/pallas_call | solution.py:406
  37.5 2.6 %collective-permute-start.8 = (bf16[2304,128]{1,0:T(8,128)(2,1)}, bf16[2304,128]{1,0:T(8,128)(2,1)S(1)}, u32[]{:S(2)}, u32[]{:S(2)}) collective-permute-start(bf16[2304,128]{1,0:T(8,128)(2,1)} %get-tuple-element.59), channel_id=1, source_target_pairs={{0,1},{1,0},{2,3},{3,2},{4,5},{5,4},{6,7},{7,6},{8,9},{9,8},{10,11... | collective-permute-start | bytes 1769480 | tf_op jit(solution)/shard_map/ppermute | solution.py:459
  40.2 3.1 %collective-permute-start.5 = (bf16[32,256]{1,0:T(8,128)(2,1)S(1)}, bf16[32,256]{1,0:T(8,128)(2,1)S(1)}, u32[]{:S(2)}, u32[]{:S(2)}) collective-permute-start(bf16[32,256]{1,0:T(8,128)(2,1)S(1)} %copy-done.14), channel_id=1, source_target_pairs={{0,224},{32,0},{64,32},{96,64},{128,96},{160,128},{192,160},{224,1... | collective-permute-start | bytes 49160 | tf_op jit(solution)/shard_map/ppermute | solution.py:431
  44.9 1.4 join.3
  46.2 5.0 %collective-permute-start.6 = (bf16[544,128]{1,0:T(8,128)(2,1)}, bf16[544,128]{1,0:T(8,128)(2,1)S(1)}, u32[]{:S(2)}, u32[]{:S(2)}) collective-permute-start(bf16[544,128]{1,0:T(8,128)(2,1)} %get-tuple-element.53), channel_id=1, source_target_pairs={{0,4},{4,8},{8,12},{12,16},{16,20},{20,24},{24,28},{1,5},{5,9},{9,... | collective-permute-start | bytes 417800 | tf_op jit(solution)/shard_map/ppermute | solution.py:434
  51.2 1.5 collective-permute-start.7
  53.5 5.2 %collective-permute-done.7.refs_3_ = bf16[544,128]{1,0:T(8,128)(2,1)S(1)} collective-permute-done((bf16[544,128]{1,0:T(8,128)(2,1)}, bf16[544,128]{1,0:T(8,128)(2,1)S(1)}, u32[]{:S(2)}, u32[]{:S(2)}) %collective-permute-start.7) | collective-permute-done | bytes 139296 | tf_op jit(solution)/shard_map/ppermute | solution.py:434
  59.4 4.8 %shard_map.86 = (bf16[768,1280]{1,0:T(8,128)(2,1)}, f32[2304,128]{1,0:T(8,128)}, bf16[2304,128]{1,0:T(8,128)(2,1)}) custom-call(s32[7,8]{1,0:T(8,128)} %flips.7, bf16[256,1024]{1,0:T(8,128)(2,1)} %get-tuple-element.48.act, bf16[256,1024]{1,0:T(8,128)(2,1)} %get-tuple-element.38.cotangent, bf16[32,256]{1,0:T(8,128)(2,1)} %copy-done.8, ...), custom_call_target="tpu_custom_call" | custom-call | tf_op jit(solution)/shard_map/pallas_call | solution.py:406
  64.2 2.4 %collective-permute-start.10 = (bf16[2304,128]{1,0:T(8,128)(2,1)}, bf16[2304,128]{1,0:T(8,128)(2,1)S(1)}, u32[]{:S(2)}, u32[]{:S(2)}) collective-permute-start(bf16[2304,128]{1,0:T(8,128)(2,1)} %get-tuple-element.61), channel_id=1, source_target_pairs={{0,1},{1,0},{2,3},{3,2},{4,5},{5,4},{6,7},{7,6},{8,9},{9,8},{10,11... | collective-permute-start | bytes 1769480 | tf_op jit(solution)/shard_map/ppermute | solution.py:459
  68.9 7.2 %collective-permute-done.9 = bf16[1152,128]{1,0:T(8,128)(2,1)} collective-permute-done((bf16[1152,128]{1,0:T(8,128)(2,1)}, bf16[1152,128]{1,0:T(8,128)(2,1)}, u32[]{:S(2)}, u32[]{:S(2)}) %collective-permute-start.9) | collective-permute-done | bytes 294944 | tf_op jit(solution)/shard_map/ppermute | solution.py:455
  77.2 5.1 %collective-permute-done.11 = bf16[1152,128]{1,0:T(8,128)(2,1)S(1)} collective-permute-done((bf16[1152,128]{1,0:T(8,128)(2,1)S(1)}, bf16[1152,128]{1,0:T(8,128)(2,1)S(1)}, u32[]{:S(2)}, u32[]{:S(2)}) %collective-permute-start.11) | collective-permute-done | bytes 294944 | tf_op jit(solution)/shard_map/ppermute | solution.py:455
  82.5 18.0 %all_to_all.20 = bf16[8,288,128]{2,1,0:T(8,128)(2,1)S(1)} all-to-all(bf16[8,288,128]{2,1,0:T(8,128)(2,1)S(1)} %pad_maximum_fusion), channel_id=1, replica_groups=mesh['lon'=8,'lat'=8,'dp'=4] {'lat'}, dimensions={0} | all-to-all | bytes 1179648 | tf_op jit(solution)/shard_map/all_to_all | solution.py:463
  100.6 14.3 %all_to_all.21 = f32[8,36,128]{2,1,0:T(8,128)S(1)} all-to-all(f32[8,36,128]{2,1,0:T(8,128)S(1)} %reshape.39), channel_id=1, replica_groups=mesh['lon'=8,'lat'=8,'dp'=4] {'lon'}, dimensions={0} | all-to-all | bytes 294912 | tf_op jit(solution)/shard_map/all_to_all | solution.py:463
  115.0 9.8 %all_to_all.22 = bf16[8,36,128]{2,1,0:T(8,128)(2,1)S(1)} all-to-all(bf16[8,36,128]{2,1,0:T(8,128)(2,1)S(1)} %broadcast_in_dim.6), channel_id=1, replica_groups=mesh['lon'=8,'lat'=8,'dp'=4] {'lon'}, dimensions={0} | all-to-all | bytes 147456 | tf_op jit(solution)/shard_map/all_to_all | solution.py:463
  124.9 12.3 %all_to_all.23.quarter = bf16[8,288,128]{2,1,0:T(8,128)(2,1)S(1)} all-to-all(bf16[8,288,128]{2,1,0:T(8,128)(2,1)S(1)} %broadcast_in_dim.15), channel_id=1, replica_groups=mesh['lon'=8,'lat'=8,'dp'=4] {'lat'}, dimensions={0} | all-to-all | bytes 1179648 | tf_op jit(solution)/shard_map/all_to_all | solution.py:463
  137.2 6.2 %collective-permute-start.14 = (bf16[8,288,128]{2,1,0:T(8,128)(2,1)S(1)}, bf16[8,288,128]{2,1,0:T(8,128)(2,1)S(1)}, u32[]{:S(2)}, u32[]{:S(2)}) collective-permute-start(bf16[8,288,128]{2,1,0:T(8,128)(2,1)S(1)} %all_to_all.23.quarter), channel_id=1, source_target_pairs={{0,1},{1,0},{2,3},{3,2},{4,5},{5,4},{6,7},{7,6},{8,9},{9,8},{10,11... | collective-permute-start | bytes 1769480 | tf_op jit(solution)/shard_map/ppermute | solution.py:459
  143.4 3.5 %collective-permute-done.12.quarter = bf16[8,288,128]{2,1,0:T(8,128)(2,1)S(1)} collective-permute-done((bf16[8,288,128]{2,1,0:T(8,128)(2,1)S(1)}, bf16[8,288,128]{2,1,0:T(8,128)(2,1)S(1)}, u32[]{:S(2)}, u32[]{:S(2)}) %collective-permute-start.12) | collective-permute-done | bytes 589856 | tf_op jit(solution)/shard_map/ppermute | solution.py:455
  146.9 6.1 %collective-permute-start.13 = (bf16[8,288,128]{2,1,0:T(8,128)(2,1)S(1)}, bf16[8,288,128]{2,1,0:T(8,128)(2,1)S(1)}, u32[]{:S(2)}, u32[]{:S(2)}) collective-permute-start(bf16[8,288,128]{2,1,0:T(8,128)(2,1)S(1)} %collective-permute-done.12.quarter), channel_id=1, source_target_pairs={{0,1},{1,0},{2,3},{3,2},{4,5},{5,4},{6,7},{7,6},{8,9},{9,8},{10,11... | collective-permute-start | bytes 1769480 | tf_op jit(solution)/shard_map/ppermute | solution.py:459
  153.0 5.4 %shard_map.87 = bf16[256,8,128]{2,1,0:T(8,128)(2,1)} custom-call(bf16[256,1024]{1,0:T(8,128)(2,1)} %get-tuple-element.37.field, bf16[9,256,256]{2,1,0:T(8,128)(2,1)} %weight.2, bf16[768,1280]{1,0:T(8,128)(2,1)} %get-tuple-element.55.pads), custom_call_target="tpu_custom_call" | custom-call | tf_op jit(solution)/shard_map/pallas_call | solution.py:406
  158.4 5.9 %shard_map.88 = bf16[256,8,128]{2,1,0:T(8,128)(2,1)} custom-call(s32[7,8]{1,0:T(8,128)} %flips.7, bf16[256,1024]{1,0:T(8,128)(2,1)} %get-tuple-element.38.cotangent, bf16[256,1024]{1,0:T(8,128)(2,1)} %get-tuple-element.56.back.grad_tile, bf16[9,256,256]{2,1,0:T(8,128)(2,1)} %weight.3, bf16[32,256]{1,0:T(8,128)(2,1)} %copy-done.8, bf16[32,256]{1,0:T(8,128)(2,1)} %copy-done.9, ...), custom_call_target="tpu_custom_call" | custom-call | tf_op jit(solution)/shard_map/pallas_call | solution.py:406
  164.4 2.3 %shard_map.90 = (f32[9,256,256]{2,1,0:T(8,128)}, f32[9,256,256]{2,1,0:T(8,128)}) custom-call(bf16[8,288,128]{2,1,0:T(8,128)(2,1)} %copy-done), custom_call_target="tpu_custom_call" | custom-call | tf_op jit(solution)/shard_map/pallas_call | solution.py:385
  167.5 2.3 %shard_map.91 = (f32[9,256,256]{2,1,0:T(8,128)}, f32[9,256,256]{2,1,0:T(8,128)}) custom-call(bf16[8,288,128]{2,1,0:T(8,128)(2,1)} %copy-done.5, f32[9,256,256]{2,1,0:T(8,128)} %get-tuple-element.62.refs_0_, f32[9,256,256]{2,1,0:T(8,128)} %get-tuple-element.63.refs_1_), custom_call_target="tpu_custom_call", output_to_operand_aliasing={{0}: (1, {}), {1}: (2, {})} | custom-call | tf_op jit(solution)/shard_map/pallas_call | solution.py:385
  169.8 2.3 %shard_map.92 = (f32[9,256,256]{2,1,0:T(8,128)}, f32[9,256,256]{2,1,0:T(8,128)}) custom-call(bf16[8,288,128]{2,1,0:T(8,128)(2,1)} %copy-done.3, f32[9,256,256]{2,1,0:T(8,128)} %get-tuple-element.64.refs_0_, f32[9,256,256]{2,1,0:T(8,128)} %get-tuple-element.65.refs_1_), custom_call_target="tpu_custom_call", output_to_operand_aliasing={{0}: (1, {}), {1}: (2, {})} | custom-call | tf_op jit(solution)/shard_map/pallas_call | solution.py:385
  172.9 2.3 %shard_map.93 = (f32[9,256,256]{2,1,0:T(8,128)}, f32[9,256,256]{2,1,0:T(8,128)}) custom-call(bf16[8,288,128]{2,1,0:T(8,128)(2,1)} %copy-done.4, f32[9,256,256]{2,1,0:T(8,128)} %get-tuple-element.66.refs_0_, f32[9,256,256]{2,1,0:T(8,128)} %get-tuple-element.67.refs_1_), custom_call_target="tpu_custom_call", output_to_operand_aliasing={{0}: (1, {}), {1}: (2, {})} | custom-call | tf_op jit(solution)/shard_map/pallas_call | solution.py:385
  (58 shorter events, 11.2 us)
Async XLA Ops:
  4.4 7.7 %collective-permute-start = (bf16[32,256]{1,0:T(8,128)(2,1)}, bf16[32,256]{1,0:T(8,128)(2,1)S(1)}, u32[]{:S(2)}, u32[]{:S(2)}) collective-permute-start(bf16[32,256]{1,0:T(8,128)(2,1)} %get-tuple-element.39), channel_id=1, source_target_pairs={{0,32},{32,64},{64,96},{96,128},{128,160},{160,192},{192,224},{224... | collective-permute-start | bytes 49160 | tf_op jit(solution)/shard_map/ppermute | solution.py:431
  6.9 5.3 %collective-permute-start.1 = (bf16[32,256]{1,0:T(8,128)(2,1)}, bf16[32,256]{1,0:T(8,128)(2,1)S(1)}, u32[]{:S(2)}, u32[]{:S(2)}) collective-permute-start(bf16[32,256]{1,0:T(8,128)(2,1)} %get-tuple-element.40), channel_id=1, source_target_pairs={{0,224},{32,0},{64,32},{96,64},{128,96},{160,128},{192,160},{224,1... | collective-permute-start | bytes 49160 | tf_op jit(solution)/shard_map/ppermute | solution.py:431
  12.1 0.6 copy-start.12
  12.1 0.6 copy-start.13
  14.1 12.6 %collective-permute-start.2 = (bf16[544,128]{1,0:T(8,128)(2,1)}, bf16[544,128]{1,0:T(8,128)(2,1)S(1)}, u32[]{:S(2)}, u32[]{:S(2)}) collective-permute-start(bf16[544,128]{1,0:T(8,128)(2,1)} %get-tuple-element.46), channel_id=1, source_target_pairs={{0,4},{4,8},{8,12},{12,16},{16,20},{20,24},{24,28},{1,5},{5,9},{9,... | collective-permute-start | bytes 417800 | tf_op jit(solution)/shard_map/ppermute | solution.py:434
  18.9 7.8 %collective-permute-start.3 = (bf16[544,128]{1,0:T(8,128)(2,1)}, bf16[544,128]{1,0:T(8,128)(2,1)S(1)}, u32[]{:S(2)}, u32[]{:S(2)}) collective-permute-start(bf16[544,128]{1,0:T(8,128)(2,1)} %get-tuple-element.47), channel_id=1, source_target_pairs={{4,0},{8,4},{12,8},{16,12},{20,16},{24,20},{28,24},{5,1},{9,5},{13... | collective-permute-start | bytes 417800 | tf_op jit(solution)/shard_map/ppermute | solution.py:434
  26.7 0.7 copy-start.10
  26.7 0.7 copy-start.11
  32.7 7.4 %copy-start.15 = (bf16[32,256]{1,0:T(8,128)(2,1)S(1)}, bf16[32,256]{1,0:T(8,128)(2,1)}, u32[]{:S(2)}) copy-start(bf16[32,256]{1,0:T(8,128)(2,1)} %get-tuple-element.49) | copy-start | bytes 49156
  32.7 7.4 %copy-start.14 = (bf16[32,256]{1,0:T(8,128)(2,1)S(1)}, bf16[32,256]{1,0:T(8,128)(2,1)}, u32[]{:S(2)}) copy-start(bf16[32,256]{1,0:T(8,128)(2,1)} %get-tuple-element.50) | copy-start | bytes 49156
  37.5 29.0 %copy-start.1 = (f32[2304,128]{1,0:T(8,128)S(1)}, f32[2304,128]{1,0:T(8,128)}, u32[]{:S(2)}) copy-start(f32[2304,128]{1,0:T(8,128)} %get-tuple-element.58) | copy-start | bytes 3538948
  37.5 29.0 %collective-permute-start.8 = (bf16[2304,128]{1,0:T(8,128)(2,1)}, bf16[2304,128]{1,0:T(8,128)(2,1)S(1)}, u32[]{:S(2)}, u32[]{:S(2)}) collective-permute-start(bf16[2304,128]{1,0:T(8,128)(2,1)} %get-tuple-element.59), channel_id=1, source_target_pairs={{0,1},{1,0},{2,3},{3,2},{4,5},{5,4},{6,7},{7,6},{8,9},{9,8},{10,11... | collective-permute-start | bytes 1769480 | tf_op jit(solution)/shard_map/ppermute | solution.py:459
  40.1 4.1 %collective-permute-start.4 = (bf16[32,256]{1,0:T(8,128)(2,1)S(1)}, bf16[32,256]{1,0:T(8,128)(2,1)S(1)}, u32[]{:S(2)}, u32[]{:S(2)}) collective-permute-start(bf16[32,256]{1,0:T(8,128)(2,1)S(1)} %copy-done.15), channel_id=1, source_target_pairs={{0,32},{32,64},{64,96},{96,128},{128,160},{160,192},{192,224},{224... | collective-permute-start | bytes 49160 | tf_op jit(solution)/shard_map/ppermute | solution.py:431
  40.2 4.1 %collective-permute-start.5 = (bf16[32,256]{1,0:T(8,128)(2,1)S(1)}, bf16[32,256]{1,0:T(8,128)(2,1)S(1)}, u32[]{:S(2)}, u32[]{:S(2)}) collective-permute-start(bf16[32,256]{1,0:T(8,128)(2,1)S(1)} %copy-done.14), channel_id=1, source_target_pairs={{0,224},{32,0},{64,32},{96,64},{128,96},{160,128},{192,160},{224,1... | collective-permute-start | bytes 49160 | tf_op jit(solution)/shard_map/ppermute | solution.py:431
  44.3 0.6 copy-start.8
  44.3 0.6 copy-start.9
  46.2 7.3 %collective-permute-start.6 = (bf16[544,128]{1,0:T(8,128)(2,1)}, bf16[544,128]{1,0:T(8,128)(2,1)S(1)}, u32[]{:S(2)}, u32[]{:S(2)}) collective-permute-start(bf16[544,128]{1,0:T(8,128)(2,1)} %get-tuple-element.53), channel_id=1, source_target_pairs={{0,4},{4,8},{8,12},{12,16},{16,20},{20,24},{24,28},{1,5},{5,9},{9,... | collective-permute-start | bytes 417800 | tf_op jit(solution)/shard_map/ppermute | solution.py:434
  51.2 7.5 %collective-permute-start.7 = (bf16[544,128]{1,0:T(8,128)(2,1)}, bf16[544,128]{1,0:T(8,128)(2,1)S(1)}, u32[]{:S(2)}, u32[]{:S(2)}) collective-permute-start(bf16[544,128]{1,0:T(8,128)(2,1)} %get-tuple-element.54), channel_id=1, source_target_pairs={{4,0},{8,4},{12,8},{16,12},{20,16},{24,20},{28,24},{5,1},{9,5},{13... | collective-permute-start | bytes 417800 | tf_op jit(solution)/shard_map/ppermute | solution.py:434
  53.5 5.2 %copy-start.6 = (bf16[544,128]{1,0:T(8,128)(2,1)}, bf16[544,128]{1,0:T(8,128)(2,1)S(1)}, u32[]{:S(2)}) copy-start(bf16[544,128]{1,0:T(8,128)(2,1)S(1)} %collective-permute-done.6.refs_2_) | copy-start | bytes 417796
  58.7 0.7 copy-start.7
  64.2 4.2 %copy-start.2 = (f32[2304,128]{1,0:T(8,128)S(1)}, f32[2304,128]{1,0:T(8,128)}, u32[]{:S(2)}) copy-start(f32[2304,128]{1,0:T(8,128)} %get-tuple-element.60) | copy-start | bytes 3538948
  64.2 4.2 %collective-permute-start.10 = (bf16[2304,128]{1,0:T(8,128)(2,1)}, bf16[2304,128]{1,0:T(8,128)(2,1)S(1)}, u32[]{:S(2)}, u32[]{:S(2)}) collective-permute-start(bf16[2304,128]{1,0:T(8,128)(2,1)} %get-tuple-element.61), channel_id=1, source_target_pairs={{0,1},{1,0},{2,3},{3,2},{4,5},{5,4},{6,7},{7,6},{8,9},{9,8},{10,11... | collective-permute-start | bytes 1769480 | tf_op jit(solution)/shard_map/ppermute | solution.py:459
  67.3 8.9 %collective-permute-start.9 = (bf16[1152,128]{1,0:T(8,128)(2,1)}, bf16[1152,128]{1,0:T(8,128)(2,1)}, u32[]{:S(2)}, u32[]{:S(2)}) collective-permute-start(bf16[1152,128]{1,0:T(8,128)(2,1)} %add_convert_fusion.3), channel_id=1, source_target_pairs={{0,2},{1,3},{2,0},{3,1},{4,6},{5,7},{6,4},{7,5},{8,10},{9,11},{10,... | collective-permute-start | bytes 884744 | tf_op jit(solution)/shard_map/ppermute | solution.py:455
  68.4 13.9 %collective-permute-start.11 = (bf16[1152,128]{1,0:T(8,128)(2,1)S(1)}, bf16[1152,128]{1,0:T(8,128)(2,1)S(1)}, u32[]{:S(2)}, u32[]{:S(2)}) collective-permute-start(bf16[1152,128]{1,0:T(8,128)(2,1)S(1)} %add_convert_fusion.1), channel_id=1, source_target_pairs={{0,2},{1,3},{2,0},{3,1},{4,6},{5,7},{6,4},{7,5},{8,10},{9,11},{10,... | collective-permute-start | bytes 884744 | tf_op jit(solution)/shard_map/ppermute | solution.py:455
  137.2 21.2 %copy-start = (bf16[8,288,128]{2,1,0:T(8,128)(2,1)}, bf16[8,288,128]{2,1,0:T(8,128)(2,1)S(1)}, u32[]{:S(2)}) copy-start(bf16[8,288,128]{2,1,0:T(8,128)(2,1)S(1)} %all_to_all.23.quarter) | copy-start | bytes 1769476
  137.2 9.7 %collective-permute-start.12 = (bf16[8,288,128]{2,1,0:T(8,128)(2,1)S(1)}, bf16[8,288,128]{2,1,0:T(8,128)(2,1)S(1)}, u32[]{:S(2)}, u32[]{:S(2)}) collective-permute-start(bf16[8,288,128]{2,1,0:T(8,128)(2,1)S(1)} %all_to_all.23.quarter), channel_id=1, source_target_pairs={{0,2},{1,3},{2,0},{3,1},{4,6},{5,7},{6,4},{7,5},{8,10},{9,11},{10,... | collective-permute-start | bytes 1769480 | tf_op jit(solution)/shard_map/ppermute | solution.py:455
  137.2 29.4 %collective-permute-start.14 = (bf16[8,288,128]{2,1,0:T(8,128)(2,1)S(1)}, bf16[8,288,128]{2,1,0:T(8,128)(2,1)S(1)}, u32[]{:S(2)}, u32[]{:S(2)}) collective-permute-start(bf16[8,288,128]{2,1,0:T(8,128)(2,1)S(1)} %all_to_all.23.quarter), channel_id=1, source_target_pairs={{0,1},{1,0},{2,3},{3,2},{4,5},{5,4},{6,7},{7,6},{8,9},{9,8},{10,11... | collective-permute-start | bytes 1769480 | tf_op jit(solution)/shard_map/ppermute | solution.py:459
  146.9 11.5 %copy-start.3 = (bf16[8,288,128]{2,1,0:T(8,128)(2,1)}, bf16[8,288,128]{2,1,0:T(8,128)(2,1)S(1)}, u32[]{:S(2)}) copy-start(bf16[8,288,128]{2,1,0:T(8,128)(2,1)S(1)} %collective-permute-done.12.quarter) | copy-start | bytes 1769476
  146.9 25.1 %collective-permute-start.13 = (bf16[8,288,128]{2,1,0:T(8,128)(2,1)S(1)}, bf16[8,288,128]{2,1,0:T(8,128)(2,1)S(1)}, u32[]{:S(2)}, u32[]{:S(2)}) collective-permute-start(bf16[8,288,128]{2,1,0:T(8,128)(2,1)S(1)} %collective-permute-done.12.quarter), channel_id=1, source_target_pairs={{0,1},{1,0},{2,3},{3,2},{4,5},{5,4},{6,7},{7,6},{8,9},{9,8},{10,11... | collective-permute-start | bytes 1769480 | tf_op jit(solution)/shard_map/ppermute | solution.py:459
  166.6 0.8 copy-start.5
  172.0 0.8 copy-start.4

commit v9 on v7

--- a/solution.py
+++ b/solution.py
@@ -202,10 +202,14 @@
     k, lane = (iota((16, LANES), 0), iota((16, LANES), 1))
 
     def corner(block, which, at, tap):
-        spread = lax.dot_general(
-            block, one_hot((k == which) & (lane == at)), TN, preferred_element_type=F32
-        ).astype(BF16)
-        return lax.dot_general(weight[tap], spread, TN, preferred_element_type=F32)
+        spread = jnp.where((k == which) & (lane == at), 1.0, 0.0)
+        return lax.dot_general(
+            dot(block, weight[tap]),
+            spread,
+            TN,
+            precision=lax.Precision.HIGHEST,
+            preferred_element_type=F32,
+        )
 
     east = LANES - 1
     top = corner(above, 1, 0, 8 - 2 * flags[2]) + corner(above, 3, east, 6 + 2 * flags[3])

time: 172 us -> 173 us (level)
  no operation moved by 1% of the time
where the time goes in v9:
time: 173 us; the launch traced here: 172 us
  blocking collectives  54.4 us (31%)
  Pallas kernels  45.6 us (26%)
  starting transfers between devices  40.4 us (23%)
  waiting for transfers between devices  24.9 us (14%)
  local copies, waits for them, and re-layouts  3.72 us (2%)
  other arithmetic  2.13 us (1%)
    all_to_all x4, blocking collectives, over(): return lax.all_to_all(value, axis, 0, 0)  54.4 us
    pallas_call x6, Pallas kernels, call(): pl.pallas_call(kernel, out_shape=out_shape, in_specs=([SMEM] if flags els...  31.5 us
    ppermute x4, starting transfers between devices, paired(): return lax.ppermute(value, 'dp', [(0, 1), (1, 0), (2, 3), (3, 2)])  17.4 us
    ppermute x3, waiting for transfers between devices, beside(): return lax.ppermute(value, 'dp', [(i, (i + 2) % 4) for i in range(4)])  15.8 us
    ppermute x4, starting transfers between devices, across(): lax.ppermute(value, 'lat', [(i, i + step) for i in range(lats) if 0 <= i...  12.6 us
    ppermute x4, starting transfers between devices, along(): lax.ppermute(value, 'lon', [(i, (i + step) % lons) for i in range(lons)])  9.54 us
    ppermute x4, waiting for transfers between devices, across(): lax.ppermute(value, 'lat', [(i, i + step) for i in range(lats) if 0 <= i...  6.04 us
    pallas_call x2, Pallas kernels, finish(): pl.pallas_call(functools.partial(finish_kernel, own), out_shape=(grad, gr...  5.97 us
  transfers between devices with their start and end apart: 15, of which 8 were waited for; matrix products, arithmetic and copies ran while one was open for 1% of the time, Pallas kernels for 16%

profile of v9, /device:TPU:1, one launch (start us, length us, event | category | flops | bytes accessed | tf_op | source)
XLA Modules:
  0.0 172.1 jit_solution(12955595639489788702)
XLA Ops:
  0.6 3.8 %shard_map.84 = (bf16[256,1024]{1,0:T(8,128)(2,1)}, bf16[256,1024]{1,0:T(8,128)(2,1)}, bf16[32,256]{1,0:T(8,128)(2,1)}, bf16[32,256]{1,0:T(8,128)(2,1)}, bf16[54...) custom-call(s32[7,8]{1,0:T(8,128)} %flips.7, bf16[256,8,128]{2,1,0:T(8,128)(2,1)} %bitcast.8, bf16[256,8,128]{2,1,0:T(8,128)(2,1)} %bitcast.9), custom_call_target="tpu_custom_call" | custom-call | tf_op jit(solution)/shard_map/pallas_call | solution.py:414
  4.4 2.5 %collective-permute-start = (bf16[32,256]{1,0:T(8,128)(2,1)}, bf16[32,256]{1,0:T(8,128)(2,1)S(1)}, u32[]{:S(2)}, u32[]{:S(2)}) collective-permute-start(bf16[32,256]{1,0:T(8,128)(2,1)} %get-tuple-element.35), channel_id=1, source_target_pairs={{0,32},{32,64},{64,96},{96,128},{128,160},{160,192},{192,224},{224... | collective-permute-start | bytes 49160 | tf_op jit(solution)/shard_map/ppermute | solution.py:439
  6.9 4.0 %collective-permute-start.1 = (bf16[32,256]{1,0:T(8,128)(2,1)}, bf16[32,256]{1,0:T(8,128)(2,1)S(1)}, u32[]{:S(2)}, u32[]{:S(2)}) collective-permute-start(bf16[32,256]{1,0:T(8,128)(2,1)} %get-tuple-element.36), channel_id=1, source_target_pairs={{0,224},{32,0},{64,32},{96,64},{128,96},{160,128},{192,160},{224,1... | collective-permute-start | bytes 49160 | tf_op jit(solution)/shard_map/ppermute | solution.py:439
  10.9 1.3 collective-permute-done.from_w
  12.7 1.4 join.2
  14.1 4.8 %collective-permute-start.2 = (bf16[544,128]{1,0:T(8,128)(2,1)}, bf16[544,128]{1,0:T(8,128)(2,1)S(1)}, u32[]{:S(2)}, u32[]{:S(2)}) collective-permute-start(bf16[544,128]{1,0:T(8,128)(2,1)} %get-tuple-element.42), channel_id=1, source_target_pairs={{0,4},{4,8},{8,12},{12,16},{16,20},{20,24},{24,28},{1,5},{5,9},{9,... | collective-permute-start | bytes 417800 | tf_op jit(solution)/shard_map/ppermute | solution.py:442
  18.9 1.3 collective-permute-start.3
  20.2 6.5 %shard_map.85 = (bf16[768,1280]{1,0:T(8,128)(2,1)}, f32[256,1024]{1,0:T(8,128)}, f32[256,1024]{1,0:T(8,128)}) custom-call(bf16[256,1024]{1,0:T(8,128)(2,1)} %get-tuple-element.33.field, bf16[256,1024]{1,0:T(8,128)(2,1)} %get-tuple-element.34.cotangent, bf16[9,256,256]{2,1,0:T(8,128)(2,1)} %weight.3, bf16[9,256,256]{2,1,0:T(8,128)(2,1)} %weight.2, ...), custom_call_target="tpu_custom_call" | custom-call | tf_op jit(solution)/shard_map/pallas_call | solution.py:414
  27.4 5.4 %hidden.1 = (bf16[256,1024]{1,0:T(8,128)(2,1)}, bf16[256,1024]{1,0:T(8,128)(2,1)}, bf16[768,1280]{1,0:T(8,128)(2,1)}, bf16[32,256]{1,0:T(8,128)(2,1)}, bf16[32,2...) custom-call(s32[7,8]{1,0:T(8,128)} %flips.7, ...), custom_call_target="tpu_custom_call", output_to_operand_aliasing={{2}: (1, {})} | custom-call | tf_op jit(solution)/shard_map/hidden/pallas_call | solution.py:528
  32.8 4.8 %shard_map.89 = (f32[2304,128]{1,0:T(8,128)}, bf16[2304,128]{1,0:T(8,128)(2,1)}) custom-call(bf16[256,1024]{1,0:T(8,128)(2,1)} %get-tuple-element.52.back.grad_tile, bf16[768,1280]{1,0:T(8,128)(2,1)} %get-tuple-element.53.pads), custom_call_target="tpu_custom_call" | custom-call | tf_op jit(solution)/shard_map/pallas_call | solution.py:414
  37.6 2.6 %collective-permute-start.8 = (bf16[2304,128]{1,0:T(8,128)(2,1)}, bf16[2304,128]{1,0:T(8,128)(2,1)S(1)}, u32[]{:S(2)}, u32[]{:S(2)}) collective-permute-start(bf16[2304,128]{1,0:T(8,128)(2,1)} %get-tuple-element.55), channel_id=1, source_target_pairs={{0,1},{1,0},{2,3},{3,2},{4,5},{5,4},{6,7},{7,6},{8,9},{9,8},{10,11... | collective-permute-start | bytes 1769480 | tf_op jit(solution)/shard_map/ppermute | solution.py:467
  40.3 3.1 %collective-permute-start.5 = (bf16[32,256]{1,0:T(8,128)(2,1)S(1)}, bf16[32,256]{1,0:T(8,128)(2,1)S(1)}, u32[]{:S(2)}, u32[]{:S(2)}) collective-permute-start(bf16[32,256]{1,0:T(8,128)(2,1)S(1)} %copy-done.14), channel_id=1, source_target_pairs={{0,224},{32,0},{64,32},{96,64},{128,96},{160,128},{192,160},{224,1... | collective-permute-start | bytes 49160 | tf_op jit(solution)/shard_map/ppermute | solution.py:439
  45.0 1.4 join.3
  46.4 5.0 %collective-permute-start.6 = (bf16[544,128]{1,0:T(8,128)(2,1)}, bf16[544,128]{1,0:T(8,128)(2,1)S(1)}, u32[]{:S(2)}, u32[]{:S(2)}) collective-permute-start(bf16[544,128]{1,0:T(8,128)(2,1)} %get-tuple-element.49), channel_id=1, source_target_pairs={{0,4},{4,8},{8,12},{12,16},{16,20},{20,24},{24,28},{1,5},{5,9},{9,... | collective-permute-start | bytes 417800 | tf_op jit(solution)/shard_map/ppermute | solution.py:442
  51.4 1.5 collective-permute-start.7
  53.7 5.2 %collective-permute-done.7.refs_3_ = bf16[544,128]{1,0:T(8,128)(2,1)S(1)} collective-permute-done((bf16[544,128]{1,0:T(8,128)(2,1)}, bf16[544,128]{1,0:T(8,128)(2,1)S(1)}, u32[]{:S(2)}, u32[]{:S(2)}) %collective-permute-start.7) | collective-permute-done | bytes 139296 | tf_op jit(solution)/shard_map/ppermute | solution.py:442
  59.5 4.8 %shard_map.86 = (bf16[768,1280]{1,0:T(8,128)(2,1)}, f32[2304,128]{1,0:T(8,128)}, bf16[2304,128]{1,0:T(8,128)(2,1)}) custom-call(s32[7,8]{1,0:T(8,128)} %flips.7, bf16[256,1024]{1,0:T(8,128)(2,1)} %get-tuple-element.44.act, bf16[256,1024]{1,0:T(8,128)(2,1)} %get-tuple-element.34.cotangent, bf16[32,256]{1,0:T(8,128)(2,1)} %copy-done.8, ...), custom_call_target="tpu_custom_call" | custom-call | tf_op jit(solution)/shard_map/pallas_call | solution.py:414
  64.3 2.4 %collective-permute-start.10 = (bf16[2304,128]{1,0:T(8,128)(2,1)}, bf16[2304,128]{1,0:T(8,128)(2,1)S(1)}, u32[]{:S(2)}, u32[]{:S(2)}) collective-permute-start(bf16[2304,128]{1,0:T(8,128)(2,1)} %get-tuple-element.57), channel_id=1, source_target_pairs={{0,1},{1,0},{2,3},{3,2},{4,5},{5,4},{6,7},{7,6},{8,9},{9,8},{10,11... | collective-permute-start | bytes 1769480 | tf_op jit(solution)/shard_map/ppermute | solution.py:467
  69.1 7.2 %collective-permute-done.9 = bf16[1152,128]{1,0:T(8,128)(2,1)} collective-permute-done((bf16[1152,128]{1,0:T(8,128)(2,1)}, bf16[1152,128]{1,0:T(8,128)(2,1)}, u32[]{:S(2)}, u32[]{:S(2)}) %collective-permute-start.9) | collective-permute-done | bytes 294944 | tf_op jit(solution)/shard_map/ppermute | solution.py:463
  76.3 1.1 add_convert_fusion.2
  77.4 5.1 %collective-permute-done.11 = bf16[1152,128]{1,0:T(8,128)(2,1)S(1)} collective-permute-done((bf16[1152,128]{1,0:T(8,128)(2,1)S(1)}, bf16[1152,128]{1,0:T(8,128)(2,1)S(1)}, u32[]{:S(2)}, u32[]{:S(2)}) %collective-permute-start.11) | collective-permute-done | bytes 294944 | tf_op jit(solution)/shard_map/ppermute | solution.py:463
  82.7 18.0 %all_to_all.20 = bf16[8,288,128]{2,1,0:T(8,128)(2,1)S(1)} all-to-all(bf16[8,288,128]{2,1,0:T(8,128)(2,1)S(1)} %pad_maximum_fusion), channel_id=1, replica_groups=mesh['lon'=8,'lat'=8,'dp'=4] {'lat'}, dimensions={0} | all-to-all | bytes 1179648 | tf_op jit(solution)/shard_map/all_to_all | solution.py:471
  100.8 14.3 %all_to_all.21 = f32[8,36,128]{2,1,0:T(8,128)S(1)} all-to-all(f32[8,36,128]{2,1,0:T(8,128)S(1)} %reshape.39), channel_id=1, replica_groups=mesh['lon'=8,'lat'=8,'dp'=4] {'lon'}, dimensions={0} | all-to-all | bytes 294912 | tf_op jit(solution)/shard_map/all_to_all | solution.py:471
  115.2 9.8 %all_to_all.22 = bf16[8,36,128]{2,1,0:T(8,128)(2,1)S(1)} all-to-all(bf16[8,36,128]{2,1,0:T(8,128)(2,1)S(1)} %broadcast_in_dim.6), channel_id=1, replica_groups=mesh['lon'=8,'lat'=8,'dp'=4] {'lon'}, dimensions={0} | all-to-all | bytes 147456 | tf_op jit(solution)/shard_map/all_to_all | solution.py:471
  125.0 12.3 %all_to_all.23.near = bf16[8,288,128]{2,1,0:T(8,128)(2,1)S(1)} all-to-all(bf16[8,288,128]{2,1,0:T(8,128)(2,1)S(1)} %broadcast_in_dim.15), channel_id=1, replica_groups=mesh['lon'=8,'lat'=8,'dp'=4] {'lat'}, dimensions={0} | all-to-all | bytes 1179648 | tf_op jit(solution)/shard_map/all_to_all | solution.py:471
  137.3 6.2 %collective-permute-start.12 = (bf16[8,288,128]{2,1,0:T(8,128)(2,1)S(1)}, bf16[8,288,128]{2,1,0:T(8,128)(2,1)S(1)}, u32[]{:S(2)}, u32[]{:S(2)}) collective-permute-start(bf16[8,288,128]{2,1,0:T(8,128)(2,1)S(1)} %all_to_all.23.near), channel_id=1, source_target_pairs={{0,1},{1,0},{2,3},{3,2},{4,5},{5,4},{6,7},{7,6},{8,9},{9,8},{10,11... | collective-permute-start | bytes 1769480 | tf_op jit(solution)/shard_map/ppermute | solution.py:467
  143.6 3.5 %collective-permute-done.13.far = bf16[8,288,128]{2,1,0:T(8,128)(2,1)S(1)} collective-permute-done((bf16[8,288,128]{2,1,0:T(8,128)(2,1)S(1)}, bf16[8,288,128]{2,1,0:T(8,128)(2,1)S(1)}, u32[]{:S(2)}, u32[]{:S(2)}) %collective-permute-start.13) | collective-permute-done | bytes 589856 | tf_op jit(solution)/shard_map/ppermute | solution.py:463
  147.0 6.1 %collective-permute-start.14 = (bf16[8,288,128]{2,1,0:T(8,128)(2,1)S(1)}, bf16[8,288,128]{2,1,0:T(8,128)(2,1)S(1)}, u32[]{:S(2)}, u32[]{:S(2)}) collective-permute-start(bf16[8,288,128]{2,1,0:T(8,128)(2,1)S(1)} %collective-permute-done.13.far), channel_id=1, source_target_pairs={{0,1},{1,0},{2,3},{3,2},{4,5},{5,4},{6,7},{7,6},{8,9},{9,8},{10,11... | collective-permute-start | bytes 1769480 | tf_op jit(solution)/shard_map/ppermute | solution.py:467
  153.2 5.4 %shard_map.87 = bf16[256,8,128]{2,1,0:T(8,128)(2,1)} custom-call(bf16[256,1024]{1,0:T(8,128)(2,1)} %get-tuple-element.33.field, bf16[9,256,256]{2,1,0:T(8,128)(2,1)} %weight.2, bf16[768,1280]{1,0:T(8,128)(2,1)} %get-tuple-element.51.pads), custom_call_target="tpu_custom_call" | custom-call | tf_op jit(solution)/shard_map/pallas_call | solution.py:414
  158.6 6.3 %shard_map.88 = bf16[256,8,128]{2,1,0:T(8,128)(2,1)} custom-call(s32[7,8]{1,0:T(8,128)} %flips.7, bf16[256,1024]{1,0:T(8,128)(2,1)} %get-tuple-element.34.cotangent, bf16[256,1024]{1,0:T(8,128)(2,1)} %get-tuple-element.52.back.grad_tile, bf16[9,256,256]{2,1,0:T(8,128)(2,1)} %weight.3, bf16[32,256]{1,0:T(8,128)(2,1)} %copy-done.8, bf16[32,256]{1,0:T(8,128)(2,1)} %copy-done.9, ...), custom_call_target="tpu_custom_call" | custom-call | tf_op jit(solution)/shard_map/pallas_call | solution.py:414
  164.9 3.0 %shard_map.90 = (f32[9,256,256]{2,1,0:T(8,128)}, f32[9,256,256]{2,1,0:T(8,128)}) custom-call(bf16[8,288,128]{2,1,0:T(8,128)(2,1)} %copy-done, bf16[8,288,128]{2,1,0:T(8,128)(2,1)} %copy-done.5), custom_call_target="tpu_custom_call" | custom-call | tf_op jit(solution)/shard_map/pallas_call | solution.py:392
  168.9 3.0 %shard_map.91 = (f32[9,256,256]{2,1,0:T(8,128)}, f32[9,256,256]{2,1,0:T(8,128)}) custom-call(bf16[8,288,128]{2,1,0:T(8,128)(2,1)} %copy-done.3, bf16[8,288,128]{2,1,0:T(8,128)(2,1)} %copy-done.4, f32[9,256,256]{2,1,0:T(8,128)} %get-tuple-element.58.refs_0_, f32[9,256,256]{2,1,0:T(8,128)} %get-tuple-element.59.refs_1_), custom_call_target="tpu_custom_call", output_to_operand_aliasing={{0}: (2, {}), {1}: (3, {})} | custom-call | tf_op jit(solution)/shard_map/pallas_call | solution.py:392
  (56 shorter events, 8.2 us)
Async XLA Ops:
  4.4 7.7 %collective-permute-start = (bf16[32,256]{1,0:T(8,128)(2,1)}, bf16[32,256]{1,0:T(8,128)(2,1)S(1)}, u32[]{:S(2)}, u32[]{:S(2)}) collective-permute-start(bf16[32,256]{1,0:T(8,128)(2,1)} %get-tuple-element.35), channel_id=1, source_target_pairs={{0,32},{32,64},{64,96},{96,128},{128,160},{160,192},{192,224},{224... | collective-permute-start | bytes 49160 | tf_op jit(solution)/shard_map/ppermute | solution.py:439
  6.9 5.3 %collective-permute-start.1 = (bf16[32,256]{1,0:T(8,128)(2,1)}, bf16[32,256]{1,0:T(8,128)(2,1)S(1)}, u32[]{:S(2)}, u32[]{:S(2)}) collective-permute-start(bf16[32,256]{1,0:T(8,128)(2,1)} %get-tuple-element.36), channel_id=1, source_target_pairs={{0,224},{32,0},{64,32},{96,64},{128,96},{160,128},{192,160},{224,1... | collective-permute-start | bytes 49160 | tf_op jit(solution)/shard_map/ppermute | solution.py:439
  12.1 0.6 copy-start.12
  12.1 0.6 copy-start.13
  14.1 12.6 %collective-permute-start.2 = (bf16[544,128]{1,0:T(8,128)(2,1)}, bf16[544,128]{1,0:T(8,128)(2,1)S(1)}, u32[]{:S(2)}, u32[]{:S(2)}) collective-permute-start(bf16[544,128]{1,0:T(8,128)(2,1)} %get-tuple-element.42), channel_id=1, source_target_pairs={{0,4},{4,8},{8,12},{12,16},{16,20},{20,24},{24,28},{1,5},{5,9},{9,... | collective-permute-start | bytes 417800 | tf_op jit(solution)/shard_map/ppermute | solution.py:442
  18.9 7.8 %collective-permute-start.3 = (bf16[544,128]{1,0:T(8,128)(2,1)}, bf16[544,128]{1,0:T(8,128)(2,1)S(1)}, u32[]{:S(2)}, u32[]{:S(2)}) collective-permute-start(bf16[544,128]{1,0:T(8,128)(2,1)} %get-tuple-element.43), channel_id=1, source_target_pairs={{4,0},{8,4},{12,8},{16,12},{20,16},{24,20},{28,24},{5,1},{9,5},{13... | collective-permute-start | bytes 417800 | tf_op jit(solution)/shard_map/ppermute | solution.py:442
  26.7 0.6 copy-start.10
  26.7 0.7 copy-start.11
  32.8 7.4 %copy-start.15 = (bf16[32,256]{1,0:T(8,128)(2,1)S(1)}, bf16[32,256]{1,0:T(8,128)(2,1)}, u32[]{:S(2)}) copy-start(bf16[32,256]{1,0:T(8,128)(2,1)} %get-tuple-element.45) | copy-start | bytes 49156
  32.8 7.4 %copy-start.14 = (bf16[32,256]{1,0:T(8,128)(2,1)S(1)}, bf16[32,256]{1,0:T(8,128)(2,1)}, u32[]{:S(2)}) copy-start(bf16[32,256]{1,0:T(8,128)(2,1)} %get-tuple-element.46) | copy-start | bytes 49156
  37.6 29.1 %copy-start.1 = (f32[2304,128]{1,0:T(8,128)S(1)}, f32[2304,128]{1,0:T(8,128)}, u32[]{:S(2)}) copy-start(f32[2304,128]{1,0:T(8,128)} %get-tuple-element.54) | copy-start | bytes 3538948
  37.6 29.1 %collective-permute-start.8 = (bf16[2304,128]{1,0:T(8,128)(2,1)}, bf16[2304,128]{1,0:T(8,128)(2,1)S(1)}, u32[]{:S(2)}, u32[]{:S(2)}) collective-permute-start(bf16[2304,128]{1,0:T(8,128)(2,1)} %get-tuple-element.55), channel_id=1, source_target_pairs={{0,1},{1,0},{2,3},{3,2},{4,5},{5,4},{6,7},{7,6},{8,9},{9,8},{10,11... | collective-permute-start | bytes 1769480 | tf_op jit(solution)/shard_map/ppermute | solution.py:467
  40.3 4.1 %collective-permute-start.4 = (bf16[32,256]{1,0:T(8,128)(2,1)S(1)}, bf16[32,256]{1,0:T(8,128)(2,1)S(1)}, u32[]{:S(2)}, u32[]{:S(2)}) collective-permute-start(bf16[32,256]{1,0:T(8,128)(2,1)S(1)} %copy-done.15), channel_id=1, source_target_pairs={{0,32},{32,64},{64,96},{96,128},{128,160},{160,192},{192,224},{224... | collective-permute-start | bytes 49160 | tf_op jit(solution)/shard_map/ppermute | solution.py:439
  40.3 4.1 %collective-permute-start.5 = (bf16[32,256]{1,0:T(8,128)(2,1)S(1)}, bf16[32,256]{1,0:T(8,128)(2,1)S(1)}, u32[]{:S(2)}, u32[]{:S(2)}) collective-permute-start(bf16[32,256]{1,0:T(8,128)(2,1)S(1)} %copy-done.14), channel_id=1, source_target_pairs={{0,224},{32,0},{64,32},{96,64},{128,96},{160,128},{192,160},{224,1... | collective-permute-start | bytes 49160 | tf_op jit(solution)/shard_map/ppermute | solution.py:439
  44.4 0.6 copy-start.8
  44.4 0.6 copy-start.9
  46.4 7.3 %collective-permute-start.6 = (bf16[544,128]{1,0:T(8,128)(2,1)}, bf16[544,128]{1,0:T(8,128)(2,1)S(1)}, u32[]{:S(2)}, u32[]{:S(2)}) collective-permute-start(bf16[544,128]{1,0:T(8,128)(2,1)} %get-tuple-element.49), channel_id=1, source_target_pairs={{0,4},{4,8},{8,12},{12,16},{16,20},{20,24},{24,28},{1,5},{5,9},{9,... | collective-permute-start | bytes 417800 | tf_op jit(solution)/shard_map/ppermute | solution.py:442
  51.4 7.5 %collective-permute-start.7 = (bf16[544,128]{1,0:T(8,128)(2,1)}, bf16[544,128]{1,0:T(8,128)(2,1)S(1)}, u32[]{:S(2)}, u32[]{:S(2)}) collective-permute-start(bf16[544,128]{1,0:T(8,128)(2,1)} %get-tuple-element.50), channel_id=1, source_target_pairs={{4,0},{8,4},{12,8},{16,12},{20,16},{24,20},{28,24},{5,1},{9,5},{13... | collective-permute-start | bytes 417800 | tf_op jit(solution)/shard_map/ppermute | solution.py:442
  53.7 5.2 %copy-start.6 = (bf16[544,128]{1,0:T(8,128)(2,1)}, bf16[544,128]{1,0:T(8,128)(2,1)S(1)}, u32[]{:S(2)}) copy-start(bf16[544,128]{1,0:T(8,128)(2,1)S(1)} %collective-permute-done.6.refs_2_) | copy-start | bytes 417796
  58.9 0.7 copy-start.7
  64.3 4.2 %copy-start.2 = (f32[2304,128]{1,0:T(8,128)S(1)}, f32[2304,128]{1,0:T(8,128)}, u32[]{:S(2)}) copy-start(f32[2304,128]{1,0:T(8,128)} %get-tuple-element.56) | copy-start | bytes 3538948
  64.3 4.2 %collective-permute-start.10 = (bf16[2304,128]{1,0:T(8,128)(2,1)}, bf16[2304,128]{1,0:T(8,128)(2,1)S(1)}, u32[]{:S(2)}, u32[]{:S(2)}) collective-permute-start(bf16[2304,128]{1,0:T(8,128)(2,1)} %get-tuple-element.57), channel_id=1, source_target_pairs={{0,1},{1,0},{2,3},{3,2},{4,5},{5,4},{6,7},{7,6},{8,9},{9,8},{10,11... | collective-permute-start | bytes 1769480 | tf_op jit(solution)/shard_map/ppermute | solution.py:467
  67.5 8.9 %collective-permute-start.9 = (bf16[1152,128]{1,0:T(8,128)(2,1)}, bf16[1152,128]{1,0:T(8,128)(2,1)}, u32[]{:S(2)}, u32[]{:S(2)}) collective-permute-start(bf16[1152,128]{1,0:T(8,128)(2,1)} %add_convert_fusion.3), channel_id=1, source_target_pairs={{0,2},{1,3},{2,0},{3,1},{4,6},{5,7},{6,4},{7,5},{8,10},{9,11},{10,... | collective-permute-start | bytes 884744 | tf_op jit(solution)/shard_map/ppermute | solution.py:463
  68.6 13.9 %collective-permute-start.11 = (bf16[1152,128]{1,0:T(8,128)(2,1)S(1)}, bf16[1152,128]{1,0:T(8,128)(2,1)S(1)}, u32[]{:S(2)}, u32[]{:S(2)}) collective-permute-start(bf16[1152,128]{1,0:T(8,128)(2,1)S(1)} %add_convert_fusion.1), channel_id=1, source_target_pairs={{0,2},{1,3},{2,0},{3,1},{4,6},{5,7},{6,4},{7,5},{8,10},{9,11},{10,... | collective-permute-start | bytes 884744 | tf_op jit(solution)/shard_map/ppermute | solution.py:463
  137.3 21.2 %copy-start = (bf16[8,288,128]{2,1,0:T(8,128)(2,1)}, bf16[8,288,128]{2,1,0:T(8,128)(2,1)S(1)}, u32[]{:S(2)}) copy-start(bf16[8,288,128]{2,1,0:T(8,128)(2,1)S(1)} %all_to_all.23.near) | copy-start | bytes 1769476
  137.3 9.7 %collective-permute-start.13 = (bf16[8,288,128]{2,1,0:T(8,128)(2,1)S(1)}, bf16[8,288,128]{2,1,0:T(8,128)(2,1)S(1)}, u32[]{:S(2)}, u32[]{:S(2)}) collective-permute-start(bf16[8,288,128]{2,1,0:T(8,128)(2,1)S(1)} %all_to_all.23.near), channel_id=1, source_target_pairs={{0,2},{1,3},{2,0},{3,1},{4,6},{5,7},{6,4},{7,5},{8,10},{9,11},{10,... | collective-permute-start | bytes 1769480 | tf_op jit(solution)/shard_map/ppermute | solution.py:463
  137.3 30.5 %collective-permute-start.12 = (bf16[8,288,128]{2,1,0:T(8,128)(2,1)S(1)}, bf16[8,288,128]{2,1,0:T(8,128)(2,1)S(1)}, u32[]{:S(2)}, u32[]{:S(2)}) collective-permute-start(bf16[8,288,128]{2,1,0:T(8,128)(2,1)S(1)} %all_to_all.23.near), channel_id=1, source_target_pairs={{0,1},{1,0},{2,3},{3,2},{4,5},{5,4},{6,7},{7,6},{8,9},{9,8},{10,11... | collective-permute-start | bytes 1769480 | tf_op jit(solution)/shard_map/ppermute | solution.py:467
  147.0 11.5 %copy-start.5 = (bf16[8,288,128]{2,1,0:T(8,128)(2,1)}, bf16[8,288,128]{2,1,0:T(8,128)(2,1)S(1)}, u32[]{:S(2)}) copy-start(bf16[8,288,128]{2,1,0:T(8,128)(2,1)S(1)} %collective-permute-done.13.far) | copy-start | bytes 1769476
  147.0 20.9 %collective-permute-start.14 = (bf16[8,288,128]{2,1,0:T(8,128)(2,1)S(1)}, bf16[8,288,128]{2,1,0:T(8,128)(2,1)S(1)}, u32[]{:S(2)}, u32[]{:S(2)}) collective-permute-start(bf16[8,288,128]{2,1,0:T(8,128)(2,1)S(1)} %collective-permute-done.13.far), channel_id=1, source_target_pairs={{0,1},{1,0},{2,3},{3,2},{4,5},{5,4},{6,7},{7,6},{8,9},{9,8},{10,11... | collective-permute-start | bytes 1769480 | tf_op jit(solution)/shard_map/ppermute | solution.py:467
  167.9 0.8 copy-start.3
  167.9 1.0 copy-start.4
